TPU v7x, 32 devices: a whole 2x2x4 slice. The times are simulated.
32 devices in a mesh: seq: 8 (over z, y), ff: 4 (over x, core).
Axes of the slice: x: 2, y: 2, z: 4, core: 2. Of those that a mesh axis runs over, the one named last changes fastest.
Arguments:
- tokens: bfloat16 [15360, 1024], P(('seq', 'ff')), may hold values from -6 to 6
- cotangent: bfloat16 [15360, 1024], P(('seq', 'ff')), may hold values from -6 to 6
- live_items: int32 [8], P('seq'), may hold values from 16 to 128, as said below
- qkv_weight: bfloat16 [1024, 3072], replicated, may hold values from -0.25 to 0.25
- out_weight: bfloat16 [1024, 1024], replicated, may hold values from -0.375 to 0.375
- up_weight: bfloat16 [1024, 2048], P(None, 'ff'), may hold values from -0.1875 to 0.1875
- down_weight: bfloat16 [2048, 1024], P('ff'), may hold values from -0.125 to 0.125
- gain_one: float32 [1024], replicated, may hold values from 0.5 to 1.5
- shift_one: float32 [1024], replicated, may hold values from -1 to 1
- gain_two: float32 [1024], replicated, may hold values from 0.5 to 1.5
- shift_two: float32 [1024], replicated, may hold values from -1 to 1
Outputs:
- layer_out: bfloat16 [15360, 1024], P(('seq', 'ff'))
- grad_tokens: bfloat16 [15360, 1024], P(('seq', 'ff'))
- grad_qkv_weight: float32 [1024, 3072], P('seq')
- grad_out_weight: float32 [1024, 1024], P('seq')
- grad_up_weight: float32 [1024, 2048], P('seq', 'ff')
- grad_down_weight: float32 [2048, 1024], P('ff', 'seq')
- grad_gain_one: float32 [1024], P('seq')
- grad_shift_one: float32 [1024], P('seq')
- grad_gain_two: float32 [1024], P('seq')
- grad_shift_two: float32 [1024], P('seq')
Inputs may be any that keep to these rules, and one draw needn't show every extreme that they name: live_items of a group counts its live items, which stand at the front of the group's 4 * 32 items; in every draw some group is full.
All inputs are finite; a program needn't handle non-finite values.
Results may differ from a plain program's by a relative error of at most 0.015.
Values may be sent and summed in bfloat16 or wider, within the bound.
A program may use at most 192 MiB of HBM per device.

v0:
```python
import jax
import jax.numpy as jnp
from jax import lax
from jax.sharding import PartitionSpec as P

HEADS = 8
HEAD_DIM = 128
ITEM_LEN = 15


tile_items = 16
tiles_block = 4


def in_blocks(x, dim, length):
    before, after = (x.shape[:dim], x.shape[dim + 1 :])
    return jnp.moveaxis(x.reshape(*before, length, -1, *after), dim, 0)


def summed_on_arrival(x, axis, dim):
    pieces = in_blocks(x, dim, lax.axis_size(axis))
    arrived = lax.all_to_all(pieces, axis, split_axis=0, concat_axis=0, tiled=True)
    return arrived.astype(jnp.float32).sum(axis=0)


def layer_norm(content_matrix, gain, shift):
    centre = content_matrix - jnp.mean(content_matrix, axis=-1, keepdims=True)
    spread = jnp.mean(centre * centre, axis=-1, keepdims=True)
    return centre * lax.rsqrt(spread + 1e-05) * gain + shift


def tile_allowed(tile_rows):
    position = jnp.arange(tile_rows, dtype=jnp.int32)
    same_item = position[:, None] // ITEM_LEN == position[None, :] // ITEM_LEN
    return same_item & (position[None, :] <= position[:, None])


def to_tiles(packed):
    return packed.reshape(-1, tiles_block, tile_items * ITEM_LEN, packed.shape[-1])


def to_heads(row_array, parts, classes):
    per_class = row_array.shape[0] // (classes * ITEM_LEN)
    shaped = row_array.reshape(classes, per_class, ITEM_LEN, parts, HEADS, HEAD_DIM)
    shaped = jnp.transpose(shaped, (4, 0, 1, 2, 3, 5))
    return shaped.reshape(HEADS * classes, per_class, ITEM_LEN, parts * HEAD_DIM)


def from_heads(head_array, parts, classes):
    per_class = head_array.shape[1]
    shaped = head_array.reshape(HEADS, classes, per_class, ITEM_LEN, parts, HEAD_DIM)
    shaped = jnp.transpose(shaped, (1, 2, 3, 4, 0, 5))
    return shaped.reshape(classes * per_class * ITEM_LEN, parts * HEADS * HEAD_DIM)


def attend_forward(packed):
    tiles = to_tiles(packed)
    allowed = tile_allowed(tiles.shape[2])

    def attend_block(tile):
        probe_matrix = tile[..., :HEAD_DIM]
        lookup_matrix = tile[..., HEAD_DIM : 2 * HEAD_DIM]
        content_matrix = tile[..., 2 * HEAD_DIM :]
        scores = jnp.einsum(
            "tsu,tyu->tsy", probe_matrix, lookup_matrix, preferred_element_type=jnp.float32
        ) * HEAD_DIM ** (-0.5)
        scores = jnp.where(allowed, scores, -1e30)
        row_max = jnp.max(scores, axis=-1, keepdims=True)
        weights = jnp.exp(scores - row_max)
        total = jnp.sum(weights, axis=-1, keepdims=True)
        attention_weights = (weights / total).astype(jnp.bfloat16)
        mixed_values = jnp.einsum(
            "rus,rsf->ruf", attention_weights, content_matrix, preferred_element_type=jnp.float32
        )
        return (mixed_values.astype(jnp.bfloat16), row_max[..., 0] + jnp.log(total[..., 0]))

    mixed_values, log_total = lax.map(attend_block, tiles)
    return (mixed_values.reshape(packed.shape[:-1] + (HEAD_DIM,)), log_total)


def attend_backward(packed, log_total, grad_mixed):
    tiles = to_tiles(packed)
    grad_tiles = to_tiles(grad_mixed)
    allowed = tile_allowed(tiles.shape[2])
    score_scale = HEAD_DIM ** (-0.5)

    def block_grad(pieces):
        tile, totals, block_derivative = pieces
        probe_matrix = tile[..., :HEAD_DIM]
        lookup_matrix = tile[..., HEAD_DIM : 2 * HEAD_DIM]
        content_matrix = tile[..., 2 * HEAD_DIM :]
        scores = (
            jnp.einsum(
                "tsu,tyu->tsy", probe_matrix, lookup_matrix, preferred_element_type=jnp.float32
            )
            * score_scale
        )
        scores = jnp.where(allowed, scores, -1e30)
        attention_weights = jnp.exp(scores - totals[..., None])
        grad_probs = jnp.einsum(
            "tsu,tyu->tsy", block_derivative, content_matrix, preferred_element_type=jnp.float32
        )
        grad_values = jnp.einsum(
            "msy,msi->myi",
            attention_weights.astype(jnp.bfloat16),
            block_derivative,
            preferred_element_type=jnp.float32,
        )
        inner = jnp.sum(attention_weights * grad_probs, axis=-1, keepdims=True)
        score_gradient = (attention_weights * (grad_probs - inner)).astype(jnp.bfloat16)
        grad_queries = (
            jnp.einsum(
                "rus,rsf->ruf", score_gradient, lookup_matrix, preferred_element_type=jnp.float32
            )
            * score_scale
        )
        grad_keys = (
            jnp.einsum(
                "msy,msi->myi", score_gradient, probe_matrix, preferred_element_type=jnp.float32
            )
            * score_scale
        )
        return jnp.concatenate((grad_queries, grad_keys, grad_values), axis=-1).astype(jnp.bfloat16)

    grads = lax.map(block_grad, (tiles, log_total, grad_tiles))
    return grads.reshape(packed.shape)


def local(
    tokens,
    cotangent,
    live_items,
    qkv_weight,
    out_weight,
    up_weight,
    down_weight,
    gain_one,
    shift_one,
    gain_two,
    shift_two,
):
    local_rows = tokens.shape[0]
    items = local_rows // ITEM_LEN
    item_place = lax.axis_index("ff") * items + jnp.arange(local_rows, dtype=jnp.int32) // ITEM_LEN
    keep_mask = (item_place < live_items[0]).astype(jnp.float32)[:, None]
    inputs = tokens.astype(jnp.float32)
    normed, norm_one_pull = jax.vjp(layer_norm, inputs, gain_one, shift_one)
    normed = normed.astype(jnp.bfloat16)
    packed = jnp.dot(normed, qkv_weight, preferred_element_type=jnp.float32).astype(jnp.bfloat16)
    classes = lax.axis_size("seq") // HEADS
    head_packed = lax.all_to_all(
        to_heads(packed, 3, classes), "seq", split_axis=0, concat_axis=0, tiled=True
    )
    head_mixed, log_total = attend_forward(head_packed)
    mixed_values = from_heads(
        lax.all_to_all(head_mixed, "seq", split_axis=0, concat_axis=0, tiled=True), 1, classes
    )
    context_output = jnp.dot(mixed_values, out_weight, preferred_element_type=jnp.float32)
    middle = inputs + keep_mask * context_output
    normed_two, norm_two_pull = jax.vjp(layer_norm, middle, gain_two, shift_two)
    normed_two = normed_two.astype(jnp.bfloat16)
    grad_out = cotangent.astype(jnp.float32)
    grad_branch = (keep_mask * grad_out).astype(jnp.bfloat16)
    gathered = lax.all_gather(normed_two, "ff", axis=0, tiled=True)
    activation_input = jnp.dot(gathered, up_weight, preferred_element_type=jnp.float32)
    hidden = jax.nn.gelu(activation_input).astype(jnp.bfloat16)
    branch = lax.psum_scatter(
        jnp.dot(hidden, down_weight, preferred_element_type=jnp.float32).astype(jnp.bfloat16),
        "ff",
        scatter_dimension=0,
        tiled=True,
    ).astype(jnp.float32)
    layer_out = (middle + keep_mask * branch).astype(jnp.bfloat16)
    grad_gathered = lax.all_gather(grad_branch, "ff", axis=0, tiled=True)
    grad_hidden = jnp.dot(grad_gathered, down_weight.T, preferred_element_type=jnp.float32)
    grad_down = jnp.dot(hidden.T, grad_gathered, preferred_element_type=jnp.float32)
    grad_pre = jax.vjp(jax.nn.gelu, activation_input)[1](grad_hidden)[0].astype(jnp.bfloat16)
    grad_up = jnp.dot(gathered.T, grad_pre, preferred_element_type=jnp.float32)
    grad_normed_two = lax.psum_scatter(
        jnp.dot(grad_pre, up_weight.T, preferred_element_type=jnp.float32),
        "ff",
        scatter_dimension=0,
        tiled=True,
    )
    grad_middle_norm, grad_gain_two, grad_shift_two = norm_two_pull(grad_normed_two)
    grad_middle = grad_out + grad_middle_norm
    grad_attended = (keep_mask * grad_middle).astype(jnp.bfloat16)
    grad_out_weight = jnp.dot(mixed_values.T, grad_attended, preferred_element_type=jnp.float32)
    grad_mixed = jnp.dot(grad_attended, out_weight.T, preferred_element_type=jnp.float32).astype(
        jnp.bfloat16
    )
    head_grad = lax.all_to_all(
        to_heads(grad_mixed, 1, classes), "seq", split_axis=0, concat_axis=0, tiled=True
    )
    head_packed_grad = attend_backward(head_packed, log_total, head_grad)
    grad_packed = from_heads(
        lax.all_to_all(head_packed_grad, "seq", split_axis=0, concat_axis=0, tiled=True), 3, classes
    )
    grad_qkv = jnp.dot(normed.T, grad_packed, preferred_element_type=jnp.float32)
    grad_normed = jnp.dot(grad_packed, qkv_weight.T, preferred_element_type=jnp.float32)
    grad_inputs, grad_gain_one, grad_shift_one = norm_one_pull(grad_normed)
    grad_tokens = (grad_middle + grad_inputs).astype(jnp.bfloat16)
    summed = (
        lax.psum_scatter(grad_qkv, "seq", scatter_dimension=0, tiled=True),
        lax.psum_scatter(grad_out_weight, "seq", scatter_dimension=0, tiled=True),
        lax.psum_scatter(grad_gain_one, "seq", scatter_dimension=0, tiled=True),
        lax.psum_scatter(grad_shift_one, "seq", scatter_dimension=0, tiled=True),
        lax.psum_scatter(grad_gain_two, "seq", scatter_dimension=0, tiled=True),
        lax.psum_scatter(grad_shift_two, "seq", scatter_dimension=0, tiled=True),
    )
    summed = (
        lax.psum(summed[0].astype(jnp.bfloat16), "ff").astype(jnp.float32),
        lax.psum(summed[1].astype(jnp.bfloat16), "ff").astype(jnp.float32),
        lax.psum(summed[2].astype(jnp.bfloat16), "ff").astype(jnp.float32),
        lax.psum(summed[3].astype(jnp.bfloat16), "ff").astype(jnp.float32),
        lax.psum(summed[4].astype(jnp.bfloat16), "ff").astype(jnp.float32),
        lax.psum(summed[5].astype(jnp.bfloat16), "ff").astype(jnp.float32),
    )
    grad_up, grad_down = (
        summed_on_arrival(grad_up.astype(jnp.bfloat16), "seq", 0),
        summed_on_arrival(grad_down.astype(jnp.bfloat16), "seq", 1),
    )
    return (
        layer_out,
        grad_tokens,
        summed[0],
        summed[1],
        grad_up,
        grad_down,
        summed[2],
        summed[3],
        summed[4],
        summed[5],
    )


def solution(mesh):
    in_specs = (
        P(("seq", "ff"), None),
        P(("seq", "ff"), None),
        P("seq"),
        P(),
        P(),
        P(None, "ff"),
        P("ff", None),
        P(),
        P(),
        P(),
        P(),
    )
    out_specs = (
        P(("seq", "ff"), None),
        P(("seq", "ff"), None),
        P("seq", None),
        P("seq", None),
        P("seq", "ff"),
        P("ff", "seq"),
        P("seq"),
        P("seq"),
        P("seq"),
        P("seq"),
    )
    return jax.shard_map(local, mesh=mesh, in_specs=in_specs, out_specs=out_specs, check_vma=False)
```

profile of v0, /device:TPU:0, one launch (start us, length us, event | category | flops | bytes accessed | tf_op | source)
XLA Modules:
  0.0 843.7 jit_solution(3582981950440449871)
XLA Ops:
  10.4 6.5 fusion.55
  21.9 8.6 %reshape.256 = bf16[8,32,15,384]{3,1,2,0:T(8,128)(2,1)} reshape(bf16[8,1,32,15,3,128]{5,4,2,3,0,1:T(4,128)(2,1)} %bitcast.122) | data formatting | bytes 5898240 | tf_op jit(solution)/shard_map/reshape | solution.py:46
  30.5 7.3 all-to-all-start
  40.9 63.4 %all-to-all-done = bf16[8,32,15,384]{3,1,2,0:T(8,128)(2,1)} async-done(((bf16[8,32,15,384]{3,1,2,0:T(8,128)(2,1)}), bf16[8,32,15,384]{3,1,2,0:T(8,128)(2,1)}, u32[]{:S(2)}, u32[]{:S(2)}) %all-to-all-start) | async-done | bytes 2949152 | tf_op jit(solution)/shard_map/all_to_all | solution.py:151
  104.3 4.7 copy.35
  109.0 5.5 reshape.257
  114.5 11.7 %while.24 = (s32[]{:T(128)}, bf16[4,4,240,128]{3,2,1,0:T(8,128)(2,1)}, f32[4,4,240]{2,1,0:T(4,128)S(1)}, bf16[4,4,240,384]{3,2,1,0:T(8,128)(2,1)}, s32[240]{0:T(256)S(1)}, /*index=5*/s32[]{:T(128)}) while((s32[]{:T(128)}, bf16[4,4,240,128]{3,2,1,0:T(8,128)(2,1)}, f32[4,4,240]{2,1,0:T(4,128)S(1)}, ...), condition=%wide.region_5.6_spmd.clone, body=%wide.region_2.5_spmd.clone.sunk | while | flops 120102720 | bytes 5435929 | solution.py:77
  129.9 28.0 %all_to_all.30 = bf16[8,32,15,128]{3,1,2,0:T(8,128)(2,1)S(1)} all-to-all(bf16[8,32,15,128]{3,1,2,0:T(8,128)(2,1)S(1)} %copy.36), channel_id=1, replica_groups=mesh['seq'=8,'ff'=4] {'seq'}, dimensions={0} | all-to-all | bytes 1966080 | tf_op jit(solution)/shard_map/all_to_all | solution.py:156
  162.6 6.6 fusion.79
  169.2 25.2 %all-gather.3.cloned.1.call-done = bf16[1920,1024]{1,0:T(8,128)(2,1)} async-done(((bf16[480,1024]{1,0:T(8,128)(2,1)}), bf16[1920,1024]{1,0:T(8,128)(2,1)}) %all-gather.3.cloned.1.call-update) | async-done | bytes 3932176 | tf_op jit(solution)/shard_map/all_gather | solution.py:164
  194.4 10.1 %fusion.42 = (bf16[1920,512]{1,0:T(8,128)(2,1)S(1)}, f32[1920,512]{1,0:T(8,128)}) fusion(f32[1920,512]{1,0:T(8,128)} %fusion.79, bf16[1920,1024]{1,0:T(8,128)(2,1)} %all-gather.3.cloned.1.call-done, bf16[1024,512]{1,0:T(8,128)(2,1)} %param.20), kind=kOutput, calls=%fused_computation.60 | convolution fusion | flops 2032926720 | bytes 14811136 | tf_op jit(solution)/shard_map/dot_general | solution.py:165
  205.8 5.3 fusion.80
  211.6 7.0 convolution_convert_fusion.3
  218.7 61.7 %reduce-scatter.7.cloned.1.call-done = f32[480,1024]{1,0:T(8,128)} async-done(((f32[1920,1024]{1,0:T(8,128)}), f32[480,1024]{1,0:T(8,128)}) %reduce-scatter.7.cloned.1.call-update) | async-done | bytes 1966096 | tf_op jit(solution)/shard_map/reduce_scatter | solution.py:179
  283.2 42.6 %reduce-scatter.5.cloned.1.call-done = bf16[480,1024]{1,0:T(8,128)(2,1)} async-done(((bf16[1920,1024]{1,0:T(8,128)(2,1)}), bf16[480,1024]{1,0:T(8,128)(2,1)}) %reduce-scatter.5.cloned.1.call-update) | async-done | bytes 983056 | tf_op jit(solution)/shard_map/reduce_scatter | solution.py:167
  333.9 5.5 all-to-all-start.2
  342.8 34.8 %all-to-all-done.2 = bf16[8,32,15,128]{3,1,2,0:T(8,128)(2,1)} async-done(((bf16[8,32,15,128]{3,1,2,0:T(8,128)(2,1)}), bf16[8,32,15,128]{3,1,2,0:T(8,128)(2,1)}, u32[]{:S(2)}, u32[]{:S(2)}) %all-to-all-start.2) | async-done | bytes 983072 | tf_op jit(solution)/shard_map/all_to_all | solution.py:192
  380.5 24.5 %while.25 = (s32[]{:T(128)}, bf16[4,4,240,384]{3,2,1,0:T(8,128)(2,1)}, bf16[4,4,240,384]{3,2,1,0:T(8,128)(2,1)}, f32[4,4,240]{2,1,0:T(4,128)S(1)}, bf16[4,4,240,...) while((s32[]{:T(128)}, bf16[4,4,240,384]{3,2,1,0:T(8,128)(2,1)}, ...), condition=%wide.region_14.15_spmd.clone, body=%wide.region_12.14_spmd.clone.sunk | while | flops 299983680 | bytes 12581161 | solution.py:125
  405.0 5.5 reshape.264
  413.1 86.0 %all_to_all.31 = bf16[8,32,15,384]{3,1,2,0:T(8,128)(2,1)} all-to-all(bf16[8,32,15,384]{3,1,2,0:T(8,128)(2,1)S(1)} %copy.40), channel_id=1, replica_groups=mesh['seq'=8,'ff'=4] {'seq'}, dimensions={0} | all-to-all | bytes 5898240 | tf_op jit(solution)/shard_map/all_to_all | solution.py:197
  499.1 8.5 %reshape.265 = bf16[8,1,32,15,3,128]{5,4,2,3,0,1:T(4,128)(2,1)} reshape(bf16[8,32,15,384]{3,1,2,0:T(8,128)(2,1)} %all_to_all.31) | data formatting | bytes 5898240 | tf_op jit(solution)/shard_map/reshape | solution.py:51
  507.7 7.2 copy.41
  514.8 5.6 reshape.266
  520.4 8.4 fusion.71
  528.9 5.8 fusion.56
  539.4 6.1 convolution_convert_fusion.5
  545.5 48.7 %all-to-all-done.5 = bf16[8,512,128]{2,1,0:T(8,128)(2,1)S(1)} async-done(((bf16[8,512,128]{2,1,0:T(8,128)(2,1)}), bf16[8,512,128]{2,1,0:T(8,128)(2,1)S(1)}, u32[]{:S(2)}, u32[]{:S(2)}) %all-to-all-start.5) | async-done | bytes 1048608 | tf_op jit(solution)/shard_map/all_to_all | solution.py:22
  600.1 47.9 %all-to-all-done.4 = bf16[8,128,512]{2,1,0:T(8,128)(2,1)S(1)} async-done(((bf16[8,128,512]{2,1,0:T(8,128)(2,1)}), bf16[8,128,512]{2,1,0:T(8,128)(2,1)S(1)}, u32[]{:S(2)}, u32[]{:S(2)}) %all-to-all-start.4) | async-done | bytes 1048608 | tf_op jit(solution)/shard_map/all_to_all | solution.py:22
  648.9 6.5 fusion.75
  658.1 124.3 %reduce-scatter.9.cloned.1.call-done = f32[128,3072]{1,0:T(8,128)} async-done(((f32[1024,3072]{1,0:T(8,128)}), f32[128,3072]{1,0:T(8,128)}) %reduce-scatter.9.cloned.1.call-update) | async-done | bytes 1572880 | tf_op jit(solution)/shard_map/reduce_scatter | solution.py:204
  784.9 35.2 %all-reduce.4 = (bf16[1024]{0:T(1024)(128)(2,1)S(1)}, bf16[1024]{0:T(1024)(128)(2,1)S(1)}, bf16[1024]{0:T(1024)(128)(2,1)S(1)}, bf16[1024]{0:T(1024)(128)(2,1)S(1)}) all-reduce(f32[1024]{0:T(1024)S(1)} %get-tuple-element.103, f32[1024]{0:T(1024)S(1)} %get-tuple-element.106, ...), channel_id=6, replica_groups=mesh['seq'=8,'ff'=4] {'seq'}, use_global_device_ids=true, to_apply=%region_24.25.clone | all-reduce | flops 4096 | bytes 24576
  820.3 5.6 all-reduce.5
  (171 shorter events, 103.3 us)
Async XLA Ops:
  7.2 151.2 %copy-start = (bf16[1024,1024]{1,0:T(8,128)(2,1)S(1)}, bf16[1024,1024]{1,0:T(8,128)(2,1)}, u32[]{:S(2)}) copy-start(bf16[1024,1024]{1,0:T(8,128)(2,1)} %param.19) | copy-start | bytes 6291460
  7.2 3.2 copy-start.4
  7.2 3.2 copy-start.12
  7.2 3.2 copy-start.15
  30.5 73.9 %all-to-all-start = ((bf16[8,32,15,384]{3,1,2,0:T(8,128)(2,1)}), bf16[8,32,15,384]{3,1,2,0:T(8,128)(2,1)}, u32[]{:S(2)}, u32[]{:S(2)}) async-start(bf16[8,32,15,384]{3,1,2,0:T(8,128)(2,1)} %reshape.256), calls=%async_computation | async-start | bytes 5898240 | tf_op jit(solution)/shard_map/all_to_all | solution.py:151
  37.8 124.8 %all-gather.5.cloned.1.call-start = ((), (), s32[]{:S(2)}) async-start(), calls=%async_computation.12 | async-start | bytes 4915200 | tf_op jit(solution)/shard_map/all_gather | solution.py:174
  40.9 153.5 %all-gather.3.cloned.1.call-start = ((), (), s32[]{:S(2)}) async-start(), calls=%async_computation.10 | async-start | bytes 4915200 | tf_op jit(solution)/shard_map/all_gather | solution.py:164
  158.3 1.3 copy-start.7
  159.7 1.3 copy-start.2
  159.7 1.3 copy-start.11
  159.7 1.3 copy-start.13
  162.3 118.0 %reduce-scatter.7.cloned.1.call-start = ((), (), s32[]{:S(2)}) async-start(), calls=%async_computation.13 | async-start | bytes 9830400 | tf_op jit(solution)/shard_map/reduce_scatter | solution.py:179
  194.4 11.4 %copy-start.14 = (bf16[1024,512]{1,0:T(8,128)(2,1)S(1)}, bf16[1024,512]{1,0:T(8,128)(2,1)}, u32[]{:S(2)}) copy-start(bf16[1024,512]{1,0:T(8,128)(2,1)} %param.20) | copy-start | bytes 3145732
  204.5 1.3 copy-start.17
  211.2 114.6 %reduce-scatter.5.cloned.1.call-start = ((), (), s32[]{:S(2)}) async-start(), calls=%async_computation.11 | async-start | bytes 4915200 | tf_op jit(solution)/shard_map/reduce_scatter | solution.py:167
  325.8 4.2 copy-start.5
  330.0 1.3 copy-start.3
  331.3 1.2 copy-start.9
  332.8 6.7 copy-start.8
  332.8 6.7 copy-start.10
  333.9 43.8 %all-to-all-start.2 = ((bf16[8,32,15,128]{3,1,2,0:T(8,128)(2,1)}), bf16[8,32,15,128]{3,1,2,0:T(8,128)(2,1)}, u32[]{:S(2)}, u32[]{:S(2)}) async-start(bf16[8,32,15,128]{3,1,2,0:T(8,128)(2,1)} %bitcast.127), calls=%async_computation.4 | async-start | bytes 1966080 | tf_op jit(solution)/shard_map/all_to_all | solution.py:192
  339.4 316.9 %reduce-scatter.11.cloned.1.call-start = ((), (), s32[]{:S(2)}) async-start(), calls=%async_computation.15 | async-start | bytes 4718592 | tf_op jit(solution)/shard_map/reduce_scatter | solution.py:205
  342.8 439.6 %reduce-scatter.9.cloned.1.call-start = ((), (), s32[]{:S(2)}) async-start(), calls=%async_computation.14 | async-start | bytes 14155776 | tf_op jit(solution)/shard_map/reduce_scatter | solution.py:204
  535.8 58.4 %all-to-all-start.5 = ((bf16[8,512,128]{2,1,0:T(8,128)(2,1)}), bf16[8,512,128]{2,1,0:T(8,128)(2,1)S(1)}, u32[]{:S(2)}, u32[]{:S(2)}) async-start(bf16[8,512,128]{2,1,0:T(8,128)(2,1)} %bitcast.95), calls=%async_computation.9 | async-start | bytes 2097152 | tf_op jit(solution)/shard_map/all_to_all | solution.py:22
  545.5 52.6 %copy-start.16 = (u32[32]{0:T(128)S(1)}, u32[32]{0:T(128)}, u32[]{:S(2)}) copy-start(u32[32]{0:T(128)} %constant.105) | copy-start | bytes 388
  594.2 53.8 %all-to-all-start.4 = ((bf16[8,128,512]{2,1,0:T(8,128)(2,1)}), bf16[8,128,512]{2,1,0:T(8,128)(2,1)S(1)}, u32[]{:S(2)}, u32[]{:S(2)}) async-start(bf16[8,128,512]{2,1,0:T(8,128)(2,1)} %bitcast.130), calls=%async_computation.8 | async-start | bytes 2097152 | tf_op jit(solution)/shard_map/all_to_all | solution.py:22
  597.8 234.7 %all-reduce.9.cloned.1.call-start = ((), (), s32[]{:S(2)}) async-start(), calls=%async_computation.16 | async-start | bytes 2097152 | tf_op jit(solution)/shard_map/psum | solution.py:212
  655.4 129.5 %copy-start.6 = (f32[480,1024]{1,0:T(8,128)}, f32[480,1024]{1,0:T(8,128)S(1)}, u32[]{:S(2)}) copy-start(f32[480,1024]{1,0:T(8,128)S(1)} %get-tuple-element.151) | copy-start | bytes 5898244
  828.0 8.6 %copy-start.1 = (bf16[1024,1024]{1,0:T(8,128)(2,1)S(1)}, bf16[1024,1024]{1,0:T(8,128)(2,1)}, u32[]{:S(2)}) copy-start(bf16[1024,1024]{1,0:T(8,128)(2,1)} %param.19) | copy-start | bytes 6291460
Sparse Core Ops, SparseCore 0:
  41.0 34.3 all-gather.4
  162.4 31.9 all-gather.2
  211.3 68.9 reduce-scatter.6
  282.9 42.8 reduce-scatter.4
  343.6 123.4 reduce-scatter.10
  529.0 253.4 reduce-scatter.8
  785.5 35.3 all-reduce.8
where the time goes:
time: 854 us; the launch traced here: 844 us
  waiting for transfers between devices  449 us (53%)
  blocking collectives  155 us (18%)
  matrix products  88.4 us (10%)
  local copies, waits for them, and re-layouts  76.1 us (9%)
  other arithmetic  38.2 us (4%)
  starting transfers between devices  21.1 us (2%)
  between operations  16 us (2%)
    reduce_scatter x1, waiting for transfers between devices, local(): lax.psum_scatter(grad_qkv, 'seq', scatter_dimension=0, tiled=True)  124 us
    all_to_all x2, waiting for transfers between devices, summed_on_arrival(): lax.all_to_all(pieces, axis, split_axis=0, concat_axis=0, tiled=True)  96.6 us
    all_to_all x1, blocking collectives, local(): lax.all_to_all(head_packed_grad, 'seq', split_axis=0, concat_axis=0, tile...  86 us
    all_to_all x1, waiting for transfers between devices, local(): lax.all_to_all(to_heads(packed, 3, classes), 'seq', split_axis=0, concat_...  63.4 us
    reduce_scatter x1, waiting for transfers between devices, local(): lax.psum_scatter(jnp.dot(grad_pre, up_weight.T, preferred_element_type=jn...  61.7 us
    reduce_scatter x1, waiting for transfers between devices, local(): lax.psum_scatter(jnp.dot(hidden, down_weight, preferred_element_type=jnp....  42.6 us
    unnamed x1, blocking collectives  35.2 us
    all_to_all x1, waiting for transfers between devices, local(): lax.all_to_all(to_heads(grad_mixed, 1, classes), 'seq', split_axis=0, con...  34.8 us
  transfers between devices with their start and end apart: 11, of which 8 were waited for; matrix products, arithmetic and copies ran while one was open for 17% of the time, Pallas kernels for 0%

commit v1 on v0

v1 whole, which is shorter than its diff:
```python
import jax
import jax.numpy as jnp
from jax import lax
from jax.sharding import PartitionSpec as P

HEADS = 8
HEAD_DIM = 128
ITEM_LEN = 15
BF = jnp.bfloat16
F32 = jnp.float32


def layer_norm(content_matrix, gain, shift):
    centre = content_matrix - jnp.mean(content_matrix, axis=-1, keepdims=True)
    spread = jnp.mean(centre * centre, axis=-1, keepdims=True)
    return centre * lax.rsqrt(spread + 1e-05) * gain + shift


def tile_allowed(tile_rows):
    position = jnp.arange(tile_rows, dtype=jnp.int32)
    same_item = position[:, None] // ITEM_LEN == position[None, :] // ITEM_LEN
    return same_item & (position[None, :] <= position[:, None])


def dot(a, b):
    return jnp.dot(a, b, preferred_element_type=F32)


def tiles_of(x, tile):
    return x.reshape(-1, tile, HEAD_DIM)


def scores_of(q, k, allowed):
    s = jnp.einsum("tqd,tkd->tqk", q, k, preferred_element_type=F32) * HEAD_DIM ** (-0.5)
    return jnp.where(allowed, s, -1e30)


def attend_forward(packed, tile):
    allowed = tile_allowed(tile)
    width = HEADS * HEAD_DIM
    mixed, saved = [], []
    for h in range(HEADS):
        q, k, v = (tiles_of(packed[:, p * width + h * HEAD_DIM:][:, :HEAD_DIM], tile) for p in range(3))
        probs = jax.nn.softmax(scores_of(q, k, allowed), axis=-1)
        o = jnp.einsum("tqk,tkd->tqd", probs.astype(BF), v, preferred_element_type=F32)
        mixed.append(o.astype(BF).reshape(-1, HEAD_DIM))
        saved.append(probs)
    return jnp.concatenate(mixed, axis=1), saved


def attend_backward(packed, saved, grad_mixed, tile):
    width = HEADS * HEAD_DIM
    scale = HEAD_DIM ** (-0.5)
    parts = ([], [], [])
    for h in range(HEADS):
        q, k, v = (tiles_of(packed[:, p * width + h * HEAD_DIM:][:, :HEAD_DIM], tile) for p in range(3))
        o = tiles_of(grad_mixed[:, h * HEAD_DIM:][:, :HEAD_DIM], tile)
        probs = saved[h]
        dp = jnp.einsum("tqd,tkd->tqk", o, v, preferred_element_type=F32)
        gv = jnp.einsum("tqk,tqd->tkd", probs.astype(BF), o, preferred_element_type=F32)
        gs = (probs * (dp - jnp.sum(probs * dp, axis=-1, keepdims=True))).astype(BF)
        gq = jnp.einsum("tqk,tkd->tqd", gs, k, preferred_element_type=F32) * scale
        gk = jnp.einsum("tqk,tqd->tkd", gs, q, preferred_element_type=F32) * scale
        for part, g in zip(parts, (gq, gk, gv)):
            part.append(g.astype(BF).reshape(-1, HEAD_DIM))
    return jnp.concatenate(parts[0] + parts[1] + parts[2], axis=1)


def general(
    tokens, cotangent, live_items, qkv_weight, out_weight, up_weight, down_weight,
    gain_one, shift_one, gain_two, shift_two,
):
    rows = tokens.shape[0]
    items = rows // ITEM_LEN
    tile = ITEM_LEN * (16 if items % 16 == 0 else 1)
    place = lax.axis_index("ff") * items + jnp.arange(rows, dtype=jnp.int32) // ITEM_LEN
    keep = (place < live_items[0]).astype(F32)[:, None]
    up_all = lax.all_gather(up_weight, "ff", axis=1, tiled=True)
    down_all = lax.all_gather(down_weight, "ff", axis=0, tiled=True)
    inputs = tokens.astype(F32)
    normed, norm_one_pull = jax.vjp(layer_norm, inputs, gain_one, shift_one)
    normed = normed.astype(BF)
    packed = dot(normed, qkv_weight).astype(BF)
    mixed, saved = attend_forward(packed, tile)
    middle = inputs + keep * dot(mixed, out_weight)
    normed_two, norm_two_pull = jax.vjp(layer_norm, middle, gain_two, shift_two)
    normed_two = normed_two.astype(BF)
    grad_out = cotangent.astype(F32)
    grad_branch = (keep * grad_out).astype(BF)
    pre = dot(normed_two, up_all)
    hidden = jax.nn.gelu(pre).astype(BF)
    layer_out = (middle + keep * dot(hidden, down_all)).astype(BF)
    grad_hidden = dot(grad_branch, down_all.T)
    grad_pre = jax.vjp(jax.nn.gelu, pre)[1](grad_hidden)[0].astype(BF)
    grad_down = dot(hidden.T, grad_branch).astype(BF)
    grad_up = dot(normed_two.T, grad_pre).astype(BF)
    grad_middle_norm, grad_gain_two, grad_shift_two = norm_two_pull(dot(grad_pre, up_all.T))
    grad_middle = grad_out + grad_middle_norm
    grad_attended = (keep * grad_middle).astype(BF)
    grad_out_weight = dot(mixed.T, grad_attended).astype(BF)
    grad_mixed = dot(grad_attended, out_weight.T).astype(BF)
    grad_packed = attend_backward(packed, saved, grad_mixed, tile)
    grad_qkv = dot(normed.T, grad_packed).astype(BF)
    grad_inputs, grad_gain_one, grad_shift_one = norm_one_pull(dot(grad_packed, qkv_weight.T))
    grad_tokens = (grad_middle + grad_inputs).astype(BF)

    def scatter(x, axis, dim):
        return lax.psum_scatter(x, axis, scatter_dimension=dim, tiled=True)

    grad_up = scatter(scatter(grad_up, "ff", 1), "seq", 0).astype(F32)
    grad_down = scatter(scatter(grad_down, "ff", 0), "seq", 1).astype(F32)
    shared = [
        lax.psum(scatter(g, "seq", 0), "ff").astype(F32)
        for g in (grad_qkv, grad_out_weight, grad_gain_one, grad_shift_one, grad_gain_two, grad_shift_two)
    ]
    return (layer_out, grad_tokens, shared[0], shared[1], grad_up, grad_down, *shared[2:])


IN_SPECS = (
    P(("seq", "ff"), None), P(("seq", "ff"), None), P("seq"), P(), P(), P(None, "ff"), P("ff", None),
    P(), P(), P(), P(),
)
OUT_SPECS = (
    P(("seq", "ff"), None), P(("seq", "ff"), None), P("seq", None), P("seq", None), P("seq", "ff"),
    P("ff", "seq"), P("seq"), P("seq"), P("seq"), P("seq"),
)


def solution(mesh):
    return jax.shard_map(general, mesh=mesh, in_specs=IN_SPECS, out_specs=OUT_SPECS, check_vma=False)
```

time: 854 us -> 554 us (0.65)
  waiting for transfers between devices: 449 us -> 316 us
  blocking collectives: 155 us -> 41.5 us
  local copies, waits for them, and re-layouts: 76.1 us -> 43.6 us
  matrix products: 88.4 us -> 113 us
  starting transfers between devices: 21.1 us -> 0.94 us
  other arithmetic: 38.2 us -> 19 us
    all_to_all x4 -> x0, waiting for transfers between devices: 195 us -> none  [the longest x2 96.6 us: summed_on_arrival(): lax.all_to_all(pieces, axis, split_axis=0, concat_axis=0, tiled=True)]
    all_to_all x2 -> x0, blocking collectives: 114 us -> none  [the longest x1 86 us: local(): lax.all_to_all(head_packed_grad, 'seq', split_axis=0, concat_axis=0, tile...]
    reshape x12 -> x0, local copies, waits for them, and re-layouts: 47.6 us -> none  [the longest x1 8.61 us: to_heads(): shaped.reshape(HEADS * classes, per_class, ITEM_LEN, parts * HEAD_DIM)]
    psum x1, waiting for transfers between devices: 0.01 us -> 36 us  [general(): lax.psum(scatter(g, 'seq', 0), 'ff').astype(F32)]
    unnamed x43 -> x237, local copies, waits for them, and re-layouts: 5.02 us -> 38.9 us
    reduce_scatter x4 -> x5, waiting for transfers between devices: 229 us -> 258 us  [scatter(): return lax.psum_scatter(x, axis, scatter_dimension=dim, tiled=True)]
    all_gather x2, waiting for transfers between devices: 25.2 us -> 0.04 us  [the longest x1 0.02 us: general(): up_all = lax.all_gather(up_weight, 'ff', axis=1, tiled=True)]
    unnamed x7 -> x10, waiting for transfers between devices: 0.11 us -> 22 us
  transfers between devices with their start and end apart: 11 -> 9, of which waited for: 8 -> 6; matrix products, arithmetic and copies ran while one was open for 17% -> 30% of each run, Pallas kernels for 0% -> 0%
where the time goes in v1:
time: 554 us; the launch traced here: 550 us
  waiting for transfers between devices  316 us (57%)
  matrix products  113 us (20%)
  local copies, waits for them, and re-layouts  43.6 us (8%)
  blocking collectives  41.5 us (7%)
  other arithmetic  19 us (3%)
  between operations  16.5 us (3%)
    reduce_scatter x5, waiting for transfers between devices, scatter(): return lax.psum_scatter(x, axis, scatter_dimension=dim, tiled=True)  258 us
    dot_general x12, matrix products, dot(): return jnp.dot(a, b, preferred_element_type=F32)  56.5 us
    unnamed x237, local copies, waits for them, and re-layouts  38.9 us
    psum x1, waiting for transfers between devices, general(): lax.psum(scatter(g, 'seq', 0), 'ff').astype(F32)  36 us
    unnamed x1, blocking collectives  35.3 us
    unnamed x10, waiting for transfers between devices  22 us
    dot_general x8, matrix products, attend_forward(): jnp.einsum('tqk,tkd->tqd', probs.astype(BF), v, preferred_element_type=F32)  17.6 us
    sub x8, matrix products, attend_forward(): probs = jax.nn.softmax(scores_of(q, k, allowed), axis=-1)  15.7 us
  transfers between devices with their start and end apart: 9, of which 6 were waited for; matrix products, arithmetic and copies ran while one was open for 30% of the time, Pallas kernels for 0%

profile of v1, /device:TPU:0, one launch (start us, length us, event | category | flops | bytes accessed | tf_op | source)
XLA Modules:
  0.0 550.0 jit_solution(14633088662426732493)
XLA Ops:
  10.6 6.6 %convolution_convert_fusion.1 = bf16[480,3072]{1,0:T(8,128)(2,1)S(1)} fusion(bf16[1024,3072]{1,0:T(8,128)(2,1)} %param.14, bf16[480,1024]{1,0:T(8,128)(2,1)S(1)} %copy-done.2, f32[1024]{0:T(1024)S(1)} %copy-done.95, f32[1024]{0:T(1024)S(1)} %copy-done.69, f32[480]{0:T(512)S(1)} %fusion.95, f32[480]{0:T(512)S(1)} %broadcast_multiply_fusion.1), kind=kOutput, calls=%fused_computation.11 | convolution fusion | flops 3024322560 | bytes 10235648 | tf_op jit(solution)/shard_map/dot_general | solution.py:26
  22.4 2.2 convolution_convert_fusion.21
  26.2 2.1 fusion.131
  28.3 2.2 convolution_convert_fusion.20
  34.2 2.2 convolution_convert_fusion.19
  40.1 2.2 convolution_convert_fusion.18
  43.8 2.1 fusion.134
  45.9 2.2 convolution_convert_fusion.17
  51.8 2.2 convolution_convert_fusion.16
  57.6 2.2 convolution_convert_fusion.15
  66.2 2.5 fusion.138
  70.4 5.2 fusion.124
  77.6 5.1 convolution_convert_fusion.2
  83.2 8.1 %fusion.14 = bf16[480,2048]{1,0:T(8,128)(2,1)S(1)} fusion(f32[480,2048]{1,0:T(8,128)} %copy-done.98, bf16[2048,1024]{1,0:T(8,128)(2,1)} %all-gather.5.cloned.1.call-done, bf16[480,1024]{1,0:T(8,128)(2,1)} %param.12, f32[480]{0:T(512)S(1)} %fusion.93), kind=kOutput, calls=%fused_computation.18 | convolution fusion | flops 2034401280 | bytes 11077504 | tf_op jit(solution)/shard_map/dot_general | solution.py:26
  91.3 2.7 multiply_reduce_fusion
  95.9 4.6 convolution_convert_fusion.3
  100.6 2.1 multiply_convert_fusion.1
  120.7 2.7 convolution_convert_fusion.4
  151.4 7.6 %convolution_convert_fusion = bf16[1024,3072]{1,0:T(8,128)(2,1)} fusion(bf16[480,3072]{1,0:T(8,128)(2,1)} %constant_dynamic-update-slice_fusion.8, bf16[480,1024]{1,0:T(8,128)(2,1)S(1)} %copy-done.2, f32[1024]{0:T(1024)S(1)} %copy-done.96, f32[1024]{0:T(1024)S(1)} %copy-done.69, f32[480]{0:T(512)S(1)} %fusion.95, f32[480]{0:T(512)S(1)} %broadcast_multiply_fusion.1), kind=kOutput, calls=%fused_computation.8 | convolution fusion | flops 3025993728 | bytes 10235648 | tf_op jit(solution)/shard_map/dot_general | solution.py:26
  159.1 2.3 copy.69
  162.8 14.4 %reduce-scatter.13.cloned.1.call-done = bf16[1024,512]{1,0:T(8,128)(2,1)} async-done(((bf16[1024,2048]{1,0:T(8,128)(2,1)}), bf16[1024,512]{1,0:T(8,128)(2,1)}) %reduce-scatter.13.cloned.1.call-update) | async-done | bytes 1048592 | tf_op jit(solution)/shard_map/reduce_scatter | solution.py:108
  177.2 6.7 %fusion.125 = (f32[1024]{0:T(1024)S(1)}, f32[480]{0:T(512)S(1)}, f32[480,1024]{1,0:T(8,128)S(1)}) fusion(f32[1024]{0:T(1024)S(1)} %copy-done.69, f32[480]{0:T(512)S(1)} %broadcast_multiply_fusion.1, bf16[480,1024]{1,0:T(8,128)(2,1)S(1)} %copy-done.2, bf16[480,3072]{1,0:T(8,128)(2,1)} %constant_dynamic-update-slice_fusion.8, bf16[1024,3072]{1,0:T(8,128)(2,1)} %param.14), kind=kOutput, calls=%fused_computation.255 | convolution fusion | flops 3022846464 | bytes 12201728 | tf_op jit(solution)/shard_map/dot_general | solution.py:26
  186.1 3.5 add_convert_fusion.1
  189.7 58.4 %reduce-scatter.11.cloned.1.call-done = bf16[128,1024]{1,0:T(8,128)(2,1)} async-done(((bf16[1024,1024]{1,0:T(8,128)(2,1)}), bf16[128,1024]{1,0:T(8,128)(2,1)}) %reduce-scatter.11.cloned.1.call-update) | async-done | bytes 262160 | tf_op jit(solution)/shard_map/reduce_scatter | solution.py:108
  248.1 120.5 %reduce-scatter.9.cloned.1.call-done = bf16[128,3072]{1,0:T(8,128)(2,1)} async-done(((bf16[1024,3072]{1,0:T(8,128)(2,1)}), bf16[128,3072]{1,0:T(8,128)(2,1)}) %reduce-scatter.9.cloned.1.call-update) | async-done | bytes 786448 | tf_op jit(solution)/shard_map/reduce_scatter | solution.py:108
  368.6 35.3 %all-reduce.4 = (f32[1024]{0:T(1024)S(1)}, f32[1024]{0:T(1024)S(1)}, f32[1024]{0:T(1024)S(1)}, f32[1024]{0:T(1024)S(1)}) all-reduce(f32[1024]{0:T(1024)S(1)} %get-tuple-element.12, f32[1024]{0:T(1024)S(1)} %get-tuple-element.15, f32[1024]{0:T(1024)S(1)} %get-tuple-element.10, ...), channel_id=8, replica_groups=mesh['seq'=8,'ff'=4] {'seq'}, use_global_device_ids=true, to_apply=%region_41.42.clone | all-reduce | flops 4096 | bytes 32768
  404.2 6.1 %all-reduce.5 = (f32[128]{0:T(128)}, f32[128]{0:T(128)}, f32[128]{0:T(128)}, f32[128]{0:T(128)}) all-reduce(f32[128]{0:T(128)S(1)} %dynamic-slice.1, f32[128]{0:T(128)S(1)} %dynamic-slice.3, f32[128]{0:T(128)S(1)} %dynamic-slice.5, f32[128]{0:T(128)S(1)} %dynamic-slice.7), channel_id=1, replica_groups=mesh['seq'=8,'ff'=4] {'ff'}, use_global_device_ids=true, to_apply=%region_42.43 | all-reduce | flops 512 | bytes 4096 | tf_op jit(solution)/shard_map/psum | solution.py:113
  410.4 4.4 add_convert_fusion
  414.8 20.5 %reduce-scatter.19.cloned.1.call-done = bf16[128,512]{1,0:T(8,128)(2,1)} async-done(((bf16[1024,512]{1,0:T(8,128)(2,1)}), bf16[128,512]{1,0:T(8,128)(2,1)}) %reduce-scatter.19.cloned.1.call-update) | async-done | bytes 131088
  437.0 64.5 %reduce-scatter.15.cloned.1.call-done = bf16[128,512]{1,0:T(8,128)(2,1)} async-done(((bf16[1024,512]{1,0:T(8,128)(2,1)}), bf16[128,512]{1,0:T(8,128)(2,1)}) %reduce-scatter.15.cloned.1.call-update) | async-done | bytes 131088 | tf_op jit(solution)/shard_map/reduce_scatter | solution.py:108
  503.1 36.0 %all-reduce.9.cloned.1.call-done = (bf16[128,3072]{1,0:T(8,128)(2,1)}, bf16[128,1024]{1,0:T(8,128)(2,1)}) async-done(((bf16[128,3072]{1,0:T(8,128)(2,1)}, bf16[128,1024]{1,0:T(8,128)(2,1)}), (bf16[128,3072]{1,0:T(8,128)(2,1)}, bf16[128,1024]{1,0:T(8,128)(2,1)})) %all-reduce.9.cloned.1.call-update) | async-done | bytes 1048592 | tf_op jit(solution)/shard_map/psum | solution.py:113
  540.9 2.4 convert_element_type.281
  (329 shorter events, 91.7 us)
Async XLA Ops:
  7.2 59.0 %copy-start = (bf16[1024,1024]{1,0:T(8,128)(2,1)S(1)}, bf16[1024,1024]{1,0:T(8,128)(2,1)}, u32[]{:S(2)}) copy-start(bf16[1024,1024]{1,0:T(8,128)(2,1)} %param.15) | copy-start | bytes 6291460
  7.2 63.2 %all-gather.3.cloned.1.call-start = ((), (), s32[]{:S(2)}) async-start(), calls=%async_computation.6 | async-start | bytes 5242880 | tf_op jit(solution)/shard_map/all_gather | solution.py:78
  8.0 75.2 %all-gather.5.cloned.1.call-start = ((), (), s32[]{:S(2)}) async-start(), calls=%async_computation.7 | async-start | bytes 5242880 | tf_op jit(solution)/shard_map/all_gather | solution.py:79
  8.7 150.4 %reduce-scatter.17.cloned.1.call-start = ((), (), s32[]{:S(2)}) async-start(), calls=%async_computation.12 | async-start | bytes 5242880 | tf_op jit(solution)/shard_map/reduce_scatter | solution.py:108
  22.4 8.1 %copy-start.74 = (f32[2,240]{1,0:T(2,128)}, f32[2,240]{1,0:T(2,128)S(1)}, u32[]{:S(2)}) copy-start(f32[2,240]{1,0:T(2,128)S(1)} %get-tuple-element.61) | copy-start | bytes 5764
  28.3 8.1 %copy-start.80 = (f32[2,240]{1,0:T(2,128)}, f32[2,240]{1,0:T(2,128)S(1)}, u32[]{:S(2)}) copy-start(f32[2,240]{1,0:T(2,128)S(1)} %get-tuple-element.63) | copy-start | bytes 5764
  34.2 8.1 %copy-start.88 = (f32[2,240]{1,0:T(2,128)}, f32[2,240]{1,0:T(2,128)S(1)}, u32[]{:S(2)}) copy-start(f32[2,240]{1,0:T(2,128)S(1)} %get-tuple-element.65) | copy-start | bytes 5764
  82.7 94.4 %reduce-scatter.13.cloned.1.call-start = ((), (), s32[]{:S(2)}) async-start(), calls=%async_computation.10 | async-start | bytes 5242880 | tf_op jit(solution)/shard_map/reduce_scatter | solution.py:108
  83.2 8.1 %copy-start.4 = (f32[480,1024]{1,0:T(8,128)S(1)}, f32[480,1024]{1,0:T(8,128)}, u32[]{:S(2)}) copy-start(f32[480,1024]{1,0:T(8,128)} %copy-done.3) | copy-start | bytes 5898244
  83.2 8.1 %copy-start.92 = (bf16[1024,2048]{1,0:T(8,128)(2,1)S(1)}, bf16[1024,2048]{1,0:T(8,128)(2,1)}, u32[]{:S(2)}) copy-start(bf16[1024,2048]{1,0:T(8,128)(2,1)} %all-gather.3.cloned.1.call-done) | copy-start | bytes 12582916
  100.5 147.5 %reduce-scatter.11.cloned.1.call-start = ((), (), s32[]{:S(2)}) async-start(), calls=%async_computation.9 | async-start | bytes 2359296 | tf_op jit(solution)/shard_map/reduce_scatter | solution.py:108
  104.3 9.3 %copy-start.59 = (bf16[480,128]{1,0:T(8,128)(2,1)}, bf16[480,128]{1,0:T(8,128)(2,1)S(1)}, u32[]{:S(2)}) copy-start(bf16[480,128]{1,0:T(8,128)(2,1)S(1)} %get-tuple-element.56) | copy-start | bytes 368644
  104.3 11.5 %copy-start.57 = (bf16[480,128]{1,0:T(8,128)(2,1)}, bf16[480,128]{1,0:T(8,128)(2,1)S(1)}, u32[]{:S(2)}) copy-start(bf16[480,128]{1,0:T(8,128)(2,1)S(1)} %get-tuple-element.55) | copy-start | bytes 368644
  104.3 13.8 %copy-start.53 = (bf16[480,128]{1,0:T(8,128)(2,1)}, bf16[480,128]{1,0:T(8,128)(2,1)S(1)}, u32[]{:S(2)}) copy-start(bf16[480,128]{1,0:T(8,128)(2,1)S(1)} %get-tuple-element.53) | copy-start | bytes 368644
  104.3 15.1 %copy-start.55 = (bf16[480,128]{1,0:T(8,128)(2,1)}, bf16[480,128]{1,0:T(8,128)(2,1)S(1)}, u32[]{:S(2)}) copy-start(bf16[480,128]{1,0:T(8,128)(2,1)S(1)} %get-tuple-element.54) | copy-start | bytes 368644
  123.4 8.7 %copy-start.36 = (bf16[2,240,128]{2,1,0:T(8,128)(2,1)S(1)}, bf16[2,240,128]{2,1,0:T(8,128)(2,1)}, u32[]{:S(2)}) copy-start(bf16[2,240,128]{2,1,0:T(8,128)(2,1)} %fusion.60) | copy-start | bytes 368644
  123.4 9.4 %copy-start.37 = (bf16[2,240,128]{2,1,0:T(8,128)(2,1)S(1)}, bf16[2,240,128]{2,1,0:T(8,128)(2,1)}, u32[]{:S(2)}) copy-start(bf16[2,240,128]{2,1,0:T(8,128)(2,1)} %fusion.61) | copy-start | bytes 368644
  123.4 10.0 %copy-start.38 = (bf16[2,240,128]{2,1,0:T(8,128)(2,1)S(1)}, bf16[2,240,128]{2,1,0:T(8,128)(2,1)}, u32[]{:S(2)}) copy-start(bf16[2,240,128]{2,1,0:T(8,128)(2,1)} %fusion.62) | copy-start | bytes 368644
  123.4 10.7 %copy-start.40 = (bf16[2,240,128]{2,1,0:T(8,128)(2,1)S(1)}, bf16[2,240,128]{2,1,0:T(8,128)(2,1)}, u32[]{:S(2)}) copy-start(bf16[2,240,128]{2,1,0:T(8,128)(2,1)} %fusion.63) | copy-start | bytes 368644
  123.4 11.4 %copy-start.42 = (bf16[2,240,128]{2,1,0:T(8,128)(2,1)S(1)}, bf16[2,240,128]{2,1,0:T(8,128)(2,1)}, u32[]{:S(2)}) copy-start(bf16[2,240,128]{2,1,0:T(8,128)(2,1)} %fusion.64) | copy-start | bytes 368644
  123.4 12.1 %copy-start.16 = (bf16[480,128]{1,0:T(8,128)(2,1)S(1)}, bf16[480,128]{1,0:T(8,128)(2,1)}, u32[]{:S(2)}) copy-start(bf16[480,128]{1,0:T(8,128)(2,1)} %get-tuple-element.34) | copy-start | bytes 368644
  123.4 13.9 %copy-start.34 = (bf16[480,128]{1,0:T(8,128)(2,1)S(1)}, bf16[480,128]{1,0:T(8,128)(2,1)}, u32[]{:S(2)}) copy-start(bf16[480,128]{1,0:T(8,128)(2,1)} %get-tuple-element.52) | copy-start | bytes 368644
  123.5 245.1 %reduce-scatter.9.cloned.1.call-start = ((), (), s32[]{:S(2)}) async-start(), calls=%async_computation.8 | async-start | bytes 7077888 | tf_op jit(solution)/shard_map/reduce_scatter | solution.py:108
  125.8 11.6 %copy-start.68 = (bf16[480,128]{1,0:T(8,128)(2,1)S(1)}, bf16[480,128]{1,0:T(8,128)(2,1)}, u32[]{:S(2)}) copy-start(bf16[480,128]{1,0:T(8,128)(2,1)} %copy-done.67) | copy-start | bytes 368644
  129.7 9.8 %copy-start.28 = (bf16[480,128]{1,0:T(8,128)(2,1)S(1)}, bf16[480,128]{1,0:T(8,128)(2,1)}, u32[]{:S(2)}) copy-start(bf16[480,128]{1,0:T(8,128)(2,1)} %get-tuple-element.49) | copy-start | bytes 368644
  129.7 9.8 %copy-start.66 = (bf16[480,128]{1,0:T(8,128)(2,1)S(1)}, bf16[480,128]{1,0:T(8,128)(2,1)}, u32[]{:S(2)}) copy-start(bf16[480,128]{1,0:T(8,128)(2,1)} %copy-done.65) | copy-start | bytes 368644
  159.1 276.2 %reduce-scatter.19.cloned.1.call-start = ((), (), s32[]{:S(2)}) async-start(), calls=%async_computation.13 | async-start | bytes 1179648
  161.5 340.1 %reduce-scatter.15.cloned.1.call-start = ((), (), s32[]{:S(2)}) async-start(), calls=%async_computation.11 | async-start | bytes 1179648 | tf_op jit(solution)/shard_map/reduce_scatter | solution.py:108
  177.1 362.0 %all-reduce.9.cloned.1.call-start = ((), (), s32[]{:S(2)}) async-start(), calls=%async_computation.14 | async-start | bytes 2097152 | tf_op jit(solution)/shard_map/psum | solution.py:113
  177.2 8.9 %copy-start.91 = (bf16[2048,1024]{1,0:T(8,128)(2,1)S(1)}, bf16[2048,1024]{1,0:T(8,128)(2,1)}, u32[]{:S(2)}) copy-start(bf16[2048,1024]{1,0:T(8,128)(2,1)} %all-gather.5.cloned.1.call-done) | copy-start | bytes 12582916
  177.2 8.9 %copy-start.99 = (f32[480,2048]{1,0:T(8,128)S(1)}, f32[480,2048]{1,0:T(8,128)}, u32[]{:S(2)}) copy-start(f32[480,2048]{1,0:T(8,128)} %copy-done.98) | copy-start | bytes 11796484
  410.4 133.0 %copy-start.1 = (bf16[1024,1024]{1,0:T(8,128)(2,1)S(1)}, bf16[1024,1024]{1,0:T(8,128)(2,1)}, u32[]{:S(2)}) copy-start(bf16[1024,1024]{1,0:T(8,128)(2,1)} %param.15) | copy-start | bytes 6291460
  (77 other events, 281.5 us)
Sparse Core Ops, SparseCore 0:
  9.6 37.1 all-gather.2
  48.4 34.4 all-gather.4
  85.5 44.5 reduce-scatter.16
  132.6 44.4 reduce-scatter.12
  180.5 67.5 reduce-scatter.10
  251.5 117.0 reduce-scatter.8
  372.5 62.6 reduce-scatter.18
  439.0 62.4 reduce-scatter.14
  503.9 35.1 all-reduce.8

commit v2 on v1

--- a/solution.py
+++ b/solution.py
@@ -1,6 +1,8 @@
 import jax
 import jax.numpy as jnp
 from jax import lax
+from jax.experimental import pallas as pl
+from jax.experimental.pallas import tpu as pltpu
 from jax.sharding import PartitionSpec as P
 
 HEADS = 8
@@ -116,6 +118,685 @@
     return (layer_out, grad_tokens, shared[0], shared[1], grad_up, grad_down, *shared[2:])
 
 
+MESH = pl.DeviceIdType.MESH
+ROWS, PAD, D, FF, SHARD = 480, 512, 1024, 2048, 512
+TILE = 240
+WIDE = 256
+STEP = 32
+UP0, UP1, DN0, DN1, OUT, QS, KS, VS = range(8)
+ORDER = {
+    UP0: "lyxh", UP1: "ylxh", DN0: "lxyh", DN1: "xylh", OUT: "xylh", QS: "xlyh", KS: "yxlh", VS: "lyxh",
+}
+EYES = "xhly"
+M_UPC, M_DNC = 0, 1
+M_WX, M_WL, M_WCX, M_WCL = 2, 6, 10, 14
+M_GBT, M_N2T, M_MXT, M_N1T, M_GA = 18, 19, 20, 21, 22
+M_HID, M_GPR = 23, 25
+M_PK = 27
+M_RED = 33
+M_AGC, M_AGX, M_AGF = 73, 77, 81
+M_VEC = 85
+N_MSG = 90
+
+
+def dot_nt(a, b):
+    return lax.dot_general(a, b, (((1,), (1,)), ((), ())), preferred_element_type=F32)
+
+
+def layer_kernel(
+    tok_h, cot_h, live, wq_h, wo_h, up_h, dn_h, g1, s1, g2, s2,
+    lo_h, gt_h, gqkv_h, gout_h, gup_o, gdn_o, gg1_o, gs1_o, gg2_o, gs2_o,
+    wq, wo, upa, dna, tok, gb, nb, mx, pk, pks, xgb, xn2, xmx, xn1, probs, mask, mid, gm, facc,
+    hids, gprs, ga, gas, gw, r0, r1, r2, r3, vsum, vbuf, vrecv, ssem, rsem, lsem,
+):
+    s, f = lax.axis_index("seq"), lax.axis_index("ff")
+    bit = {"h": s // 4, "l": (s // 2) % 2, "y": s % 2, "x": f // 2, "c": f % 2}
+    mate = {
+        "h": (s + 4 - 8 * bit["h"], f), "l": (s + 2 - 4 * bit["l"], f), "y": (s + 1 - 2 * bit["y"], f),
+        "x": (s, f + 2 - 4 * bit["x"]), "c": (s, f + 1 - 2 * bit["c"]),
+    }
+    x, c = bit["x"], bit["c"]
+
+    def at(base, size, unit=128):
+        return pl.ds(pl.multiple_of(base, unit), size)
+
+    def local(i, src, dst):
+        return pltpu.make_async_copy(src, dst, lsem.at[i])
+
+    loads = {
+        0: (tok_h, tok), 1: (cot_h, gb.at[0:ROWS]), 2: (wq_h, wq), 3: (wo_h, wo), 4: (up_h, upa.at[:, 0:SHARD]),
+        5: (dn_h, dna.at[0:SHARD]), 6: (cot_h, nb.at[0:ROWS]), 7: (wq_h, wq),
+        8: (nb.at[0:ROWS], lo_h), 9: (tok, gt_h), 10: (gm.at[0:128], gout_h),
+        11: (facc.at[0:128], gqkv_h.at[:, 0:D]), 12: (facc.at[128:256], gqkv_h.at[:, D:2 * D]),
+        13: (facc.at[256:384], gqkv_h.at[:, 2 * D:3 * D]),
+    }
+
+    def load(i):
+        local(i, *loads[i]).start()
+
+    def loaded(i):
+        local(i, *loads[i]).wait()
+
+    def remote(i, to, src, dst):
+        return pltpu.make_async_remote_copy(
+            src_ref=src, dst_ref=dst, send_sem=ssem.at[i], recv_sem=rsem.at[i], device_id=mate[to], device_id_type=MESH
+        )
+
+    def quarter(k, own, slot, whole):
+        half = bit["l"] if own else 1 - bit["l"]
+        if k < 2:
+            rows = at(half * 512 + k * 256, 256)
+            return (up_h.at[rows, :] if whole else upa.at[rows, slot * SHARD:(slot + 1) * SHARD])
+        start = half * 256 + (k - 2) * 128
+        return dn_h.at[at(start, 128), :] if whole else dna.at[at(slot * SHARD + start, 128), :]
+
+    def weight_x(k):
+        half_mate = quarter(k, True, 2, True)
+        return remote(M_WX + k, "x", half_mate, quarter(k, True, 2, False))
+
+    def weight_l(k):
+        ref = quarter(k, True, 2, False)
+        return remote(M_WL + k, "l", ref, ref)
+
+    def weight_cx(k):
+        return remote(M_WCX + k, "c", quarter(k, True, 2, False), quarter(k, True, 3, False))
+
+    def weight_cl(k):
+        return remote(M_WCL + k, "c", quarter(k, False, 2, False), quarter(k, False, 3, False))
+
+    def relay_x(k):
+        weight_x(k).wait()
+        weight_l(k).start()
+        weight_cx(k).start()
+
+    def relay_l(k):
+        weight_l(k).wait()
+        weight_cl(k).start()
+
+    def weight_c(which):
+        if which == 0:
+            return remote(M_UPC, "c", up_h, upa.at[:, SHARD:2 * SHARD])
+        return remote(M_DNC, "c", dn_h, dna.at[SHARD:2 * SHARD])
+
+    def turned(i, ref):
+        return remote(i, "c", ref.at[:, 0:PAD], ref.at[:, PAD:2 * PAD])
+
+    def own_hid(slot):
+        return wq.at[0:PAD, at(slot * SHARD, SHARD)]
+
+    def own_gpr(slot):
+        return wq.at[PAD:2 * PAD, at(slot * SHARD, SHARD)]
+
+    def hid_copy(g):
+        return remote(M_HID + g, "c", own_hid(2 * g + 1), hids.at[:, at(g * SHARD, SHARD)])
+
+    def gpr_copy(g):
+        return remote(M_GPR + g, "c", own_gpr(2 * g + 1), gprs.at[:, at(g * SHARD, SHARD)])
+
+    def ga_copy():
+        return remote(M_GA, "c", ga.at[:, at((1 - c) * 512, 512)], gas)
+
+    def pk_copy(n, xb, part):
+        return remote(
+            M_PK + n * 3 + part, "c", pk.at[:, at(part * D + (1 - c) * 512 + xb * WIDE, WIDE)],
+            pks.at[:, at(part * 512 + xb * WIDE, WIDE)],
+        )
+
+    landing = (r0, r1, r2, r3)
+
+    def bits_of(p):
+        if p < OUT:
+            return {**bit, "x": 0}
+        return bit
+
+    def chosen(p, k, mine, xb=None):
+        own, order, index = bits_of(p), ORDER[p], []
+        for e in EYES:
+            if e in order[:k]:
+                index.append(own[e])
+            elif e == order[k]:
+                index.append(own[e] if mine else 1 - own[e])
+            elif e == "x" and xb is not None:
+                index.append(xb)
+            else:
+                index.append(slice(None))
+        return index
+
+    def red(p, k, xb=None, part=0):
+        dst = landing[k].at[p] if xb is None else landing[k].at[p, xb]
+        return remote(
+            M_RED + p * 5 + (k + 1 if k else part), ORDER[p][k], gw.at[(p, *chosen(p, k, False, xb))], dst
+        )
+
+    def add(p, k, xb=None):
+        index = chosen(p, k, True, xb)
+        free = [n for n, e in enumerate(index) if isinstance(e, slice)]
+        count = len(free)
+
+        def body(i, _):
+            place = [(i // (1 << (count - 1 - n))) % 2 for n in range(count)]
+            full = list(index)
+            for n, e in zip(free, place):
+                full[n] = e
+            lead = (p, *place) if xb is None else (p, xb, *place)
+            gw[(p, *full)] = (gw[(p, *full)].astype(F32) + landing[k][lead].astype(F32)).astype(BF)
+            return 0
+
+        lax.fori_loop(0, 1 << count, body, 0)
+
+    def first(p, xb, part):
+        if ORDER[p][0] != "x":
+            red(p, 0, xb, part).start()
+        elif isinstance(xb, int):
+            if xb == 1:
+                red(p, 0).start()
+        elif part == 0:
+            red(p, 0).start()
+
+    def first_done(p, xb, part):
+        red(p, 0, xb, part).wait()
+        add(p, 0, xb)
+
+    def done(p, k):
+        red(p, k).wait()
+        add(p, k)
+
+    def step(p, k):
+        done(p, k)
+        red(p, k + 1).start()
+
+    def result(p):
+        red(p, 3).wait()
+        own = bits_of(p)
+        return gw[(p, *(own[e] for e in EYES))].astype(F32) + r3[p].astype(F32)
+
+    def quarters(q, n):
+        return xgb.at[q * 128:(q + 1) * 128, at(n * WIDE, WIDE)]
+
+    own_quarter = 2 * c + x
+
+    def gather_c(q):
+        return remote(M_AGC + q, "c", quarters(q, own_quarter), quarters(q, own_quarter))
+
+    def gather_x(q):
+        return remote(M_AGX + q, "x", quarters(q, own_quarter), quarters(q, own_quarter))
+
+    def gather_f(q):
+        other = 2 * c + 1 - x
+        return remote(M_AGF + q, "c", quarters(q, other), quarters(q, other))
+
+    limit = (live[0] - f * (ROWS // 15)) * 15
+
+    def keep_of(r):
+        rows = r * STEP + lax.broadcasted_iota(jnp.int32, (STEP, 1), 0)
+        return jnp.where(rows < limit, 1.0, 0.0).astype(F32)
+
+    def block(r):
+        return pl.ds(pl.multiple_of(r * STEP, STEP), STEP)
+
+    def centred(v):
+        centre = v - jnp.mean(v, axis=-1, keepdims=True)
+        rstd = lax.rsqrt(jnp.mean(centre * centre, axis=-1, keepdims=True) + 1e-05)
+        return centre * rstd, rstd
+
+    def turn(src, dst):
+        def body(j, _):
+            cols = at(j * 128, 128)
+            dst[cols, 0:PAD] = src[:, cols].T
+            return 0
+
+        lax.fori_loop(0, D // 128, body, 0)
+
+    for i in range(6):
+        load(i)
+    barrier = pltpu.get_barrier_semaphore()
+    for e in "xylhc":
+        pl.semaphore_signal(barrier, inc=1, device_id=mate[e], device_id_type=MESH)
+    for ref in (gb, nb, mx, ga):
+        ref[ROWS:PAD, :] = jnp.zeros((PAD - ROWS, D), BF)
+    pk[ROWS:PAD, :] = jnp.zeros((PAD - ROWS, 3 * D), BF)
+    vsum[...] = jnp.zeros(vsum.shape, F32)
+    qi = lax.broadcasted_iota(jnp.int32, (TILE, TILE), 0)
+    ki = lax.broadcasted_iota(jnp.int32, (TILE, TILE), 1)
+    mask[...] = jnp.where((ki <= qi) & (ki >= qi - lax.rem(qi, 15)), 0.0, -1e30).astype(F32)
+
+    loaded(0)
+
+    def norm_one(r, _):
+        xhat, _r = centred(tok[block(r), :].astype(F32))
+        nb[block(r), :] = (xhat * g1[...] + s1[...]).astype(BF)
+        return 0
+
+    lax.fori_loop(0, ROWS // STEP, norm_one, 0)
+    pl.semaphore_wait(barrier, 5)
+    for k in range(4):
+        weight_x(k).start()
+    weight_c(0).start()
+    weight_c(1).start()
+
+    loaded(2)
+
+    def qkv(n, _):
+        cols = at(n * 512, 512)
+        pk[0:ROWS, cols] = jnp.dot(nb[0:ROWS, :], wq[:, cols], preferred_element_type=F32).astype(BF)
+        return 0
+
+    lax.fori_loop(0, 6, qkv, 0)
+    turn(nb, xn1)
+    turned(M_N1T, xn1).start()
+
+    loaded(1)
+
+    def mask_cot(r, _):
+        gb[block(r), :] = (keep_of(r) * gb[block(r), :].astype(F32)).astype(BF)
+        return 0
+
+    lax.fori_loop(0, ROWS // STEP, mask_cot, 0)
+    turn(gb, xgb)
+    turned(M_GBT, xgb).start()
+
+    def attend(h, _):
+        cols = [at(part * D + h * 128, 128) for part in range(3)]
+        for t in range(2):
+            rows = slice(t * TILE, (t + 1) * TILE)
+            sc = dot_nt(pk[rows, cols[0]], pk[rows, cols[1]]) * (128 ** -0.5) + mask[...]
+            w = jnp.exp(sc - jnp.max(sc, axis=-1, keepdims=True))
+            p = (w * (1.0 / jnp.sum(w, axis=-1, keepdims=True))).astype(BF)
+            probs[h * 2 + t] = p
+            mx[rows, at(h * 128, 128)] = jnp.dot(p, pk[rows, cols[2]], preferred_element_type=F32).astype(BF)
+        return 0
+
+    lax.fori_loop(0, 8, attend, 0)
+    relay_x(0)
+    turn(mx, xmx)
+    turned(M_MXT, xmx).start()
+
+    loaded(3)
+
+    def project(n, _):
+        cols = at(n * 512, 512)
+        facc[:, cols] = jnp.dot(mx[0:ROWS, :], wo[:, cols], preferred_element_type=F32)
+        return 0
+
+    lax.fori_loop(0, 2, project, 0)
+
+    def norm_two(r, _):
+        m = tok[block(r), :].astype(F32) + keep_of(r) * facc[block(r), :]
+        mid[block(r), :] = m
+        xhat, _r = centred(m)
+        nb[block(r), :] = (xhat * g2[...] + s2[...]).astype(BF)
+        return 0
+
+    lax.fori_loop(0, ROWS // STEP, norm_two, 0)
+    relay_x(1)
+    turn(nb, xn2)
+    turned(M_N2T, xn2).start()
+
+    loaded(4)
+    loaded(5)
+    weight_c(0).wait()
+    weight_c(1).wait()
+    wq[ROWS:PAD, 0:FF] = jnp.zeros((PAD - ROWS, FF), BF)
+    wq[PAD + ROWS:2 * PAD, 0:FF] = jnp.zeros((PAD - ROWS, FF), BF)
+
+    def shard(j):
+        cols = at(j * SHARD, SHARD)
+        pre = jnp.dot(nb[0:ROWS, :], upa[:, cols], preferred_element_type=F32)
+        sq = pre * pre
+        t = jnp.tanh(0.7978845608028654 * pre * (1.0 + 0.044715 * sq))
+        half = 0.5 * (1.0 + t)
+        wq[0:ROWS, cols] = (pre * half).astype(BF)
+        slope = half + 0.5 * pre * (1.0 - t * t) * (0.7978845608028654 * (1.0 + 0.134145 * sq))
+        gh = dot_nt(gb[0:ROWS, :], dna[cols, :])
+        wq[PAD:PAD + ROWS, cols] = (gh * slope).astype(BF)
+
+    def group(g, _):
+        @pl.when(g == 1)
+        def _():
+            for k in range(4):
+                weight_cx(k).wait()
+                weight_cl(k).wait()
+
+        def one(n, _):
+            shard(2 * g + 1 - n)
+
+            @pl.when(n == 0)
+            def _():
+                hid_copy(g).start()
+                gpr_copy(g).start()
+
+                @pl.when(g == 0)
+                def _():
+                    relay_x(2)
+                    relay_l(0)
+                    relay_l(1)
+
+            return 0
+
+        lax.fori_loop(0, 2, one, 0)
+
+        @pl.when(g == 0)
+        def _():
+            relay_x(3)
+            relay_l(2)
+            turned(M_N2T, xn2).wait()
+            turned(M_GBT, xgb).wait()
+
+        hid_copy(g).wait()
+        gpr_copy(g).wait()
+        mine, theirs = at(2 * g * SHARD, SHARD), at(g * SHARD, SHARD)
+
+        def sums(n, _):
+            rows = at(n * 512, 512)
+            for lhs, top, low, p in ((xn2, PAD, gprs, UP0), (xgb, 0, hids, DN0)):
+                rhs = jnp.concatenate([wq[top:top + PAD, mine], low[:, theirs]], axis=0)
+                total = jnp.dot(lhs[rows, :], rhs, preferred_element_type=F32).astype(BF)
+                for half in range(2):
+                    gw[p + half, g, n] = total[:, half * WIDE:(half + 1) * WIDE].reshape(2, 2, 128, WIDE)
+            return 0
+
+        lax.fori_loop(0, 2, sums, 0)
+
+        @pl.when(g == 0)
+        def _():
+            for p in (UP0, UP1, DN0, DN1):
+                first(p, 0, 0)
+            relay_l(3)
+
+        @pl.when(g == 1)
+        def _():
+            for p in (DN1, UP0, UP1, DN0):
+                first(p, 1, 1)
+
+        return 0
+
+    lax.fori_loop(0, 2, group, 0)
+    load(6)
+
+    def back_up(n, _):
+        cols = at(n * 512, 512)
+        facc[:, cols] = dot_nt(wq[PAD:PAD + ROWS, 0:FF], upa[cols, :])
+        return 0
+
+    lax.fori_loop(0, 2, back_up, 0)
+    for p in (UP0, UP1, DN0):
+        first_done(p, 0, 0)
+    loaded(6)
+
+    def row_sum(v):
+        total = v[0:8]
+        for n in range(1, STEP // 8):
+            total = total + v[n * 8:(n + 1) * 8]
+        return total
+
+    def norm_back(v, gn, gain, n):
+        xhat, rstd = centred(v)
+        vsum[n] += row_sum(gn * xhat)
+        vsum[n + 1] += row_sum(gn)
+        e = gn * gain
+        return rstd * (e - jnp.mean(e, axis=-1, keepdims=True) - xhat * jnp.mean(e * xhat, axis=-1, keepdims=True))
+
+    def norm_two_back(r, _):
+        total = nb[block(r), :].astype(F32) + norm_back(mid[block(r), :], facc[block(r), :], g2[...], 2)
+        gm[block(r), :] = total
+        ga[block(r), :] = (keep_of(r) * total).astype(BF)
+        return 0
+
+    lax.fori_loop(0, ROWS // STEP, norm_two_back, 0)
+    ga_copy().start()
+
+    def back_out(n, _):
+        cols = at(n * 512, 512)
+        mx[0:ROWS, cols] = dot_nt(ga[0:ROWS, :], wo[cols, :]).astype(BF)
+        return 0
+
+    turned(M_MXT, xmx).wait()
+    lax.fori_loop(0, 2, back_out, 0)
+    ga_copy().wait()
+
+    def out_sums(n, _):
+        rows = at(n * 512, 512)
+        rhs = jnp.concatenate([ga[:, at(c * 512, 512)], gas[...]], axis=0)
+        total = jnp.dot(xmx[rows, :], rhs, preferred_element_type=F32).astype(BF)
+        for half in range(2):
+            gw[OUT, half, n] = total[:, half * WIDE:(half + 1) * WIDE].reshape(2, 2, 128, WIDE)
+        return 0
+
+    lax.fori_loop(0, 2, out_sums, 0)
+    red(OUT, 0).start()
+    for p in (UP0, UP1, DN0):
+        first_done(p, 1, 1)
+        red(p, 1).start()
+    turned(M_N1T, xn1).wait()
+
+    def head_back(h):
+        cols = [at(part * D + h * 128, 128) for part in range(3)]
+        for t in range(2):
+            rows = slice(t * TILE, (t + 1) * TILE)
+            q, k, v = (pk[rows, col] for col in cols)
+            o = mx[rows, at(h * 128, 128)]
+            pb = probs[h * 2 + t]
+            p = pb.astype(F32)
+            dp = dot_nt(o, v)
+            gs = (p * (dp - jnp.sum(p * dp, axis=-1, keepdims=True))).astype(BF)
+            gv = lax.dot_general(pb, o, (((0,), (0,)), ((), ())), preferred_element_type=F32)
+            gq = jnp.dot(gs, k, preferred_element_type=F32) * (128 ** -0.5)
+            gk = lax.dot_general(gs, q, (((0,), (0,)), ((), ())), preferred_element_type=F32) * (128 ** -0.5)
+            for col, g in zip(cols, (gq, gk, gv)):
+                pk[rows, col] = g.astype(BF)
+
+    def pair(i, _):
+        cb = lax.rem(i + 1 + c, 2)
+        later = i // 2
+        xb = lax.rem(later + 1 + x, 2)
+
+        def one(n, _):
+            head_back(cb * 4 + xb * 2 + n)
+            return 0
+
+        lax.fori_loop(0, 2, one, 0)
+
+        for n in range(2):
+            xn = 1 - x if n == 0 else x
+
+            @pl.when(i == 2 * n)
+            def _():
+                for part in range(3):
+                    pk_copy(n, xn, part).start()
+
+        def qkv_sums():
+            def body(n, _):
+                rows = at(n * 512, 512)
+                rhs = jnp.concatenate(
+                    [
+                        jnp.concatenate([pk[:, at(part * D + c * 512 + xb * WIDE, WIDE)] for part in range(3)], axis=1),
+                        jnp.concatenate([pks[:, at(part * 512 + xb * WIDE, WIDE)] for part in range(3)], axis=1),
+                    ],
+                    axis=0,
+                )
+                total = jnp.dot(xn1[rows, :], rhs, preferred_element_type=F32).astype(BF)
+                for part in range(3):
+                    gw[QS + part, xb, n] = total[:, part * WIDE:(part + 1) * WIDE].reshape(2, 2, 128, WIDE)
+                return 0
+
+            lax.fori_loop(0, 2, body, 0)
+
+        @pl.when(i % 2 == 1)
+        def _():
+            for n in range(2):
+                xn = 1 - x if n == 0 else x
+
+                @pl.when(later == n)
+                def _():
+                    for part in range(3):
+                        pk_copy(n, xn, part).wait()
+
+            qkv_sums()
+
+        @pl.when(i == 1)
+        def _():
+            for p in (QS, KS, VS):
+                first(p, 1 - x, 0)
+            step(DN1, 0)
+
+        @pl.when(i == 3)
+        def _():
+            for p in (QS, KS, VS):
+                first(p, x, 1)
+
+        return 0
+
+    lax.fori_loop(0, 4, pair, 0)
+    for p in (UP0, UP1, DN0):
+        step(p, 1)
+    step(OUT, 0)
+
+    def down(n, _):
+        cols = at(n * 512, 512)
+        facc[:, cols] = jnp.dot(wq[0:ROWS, 0:FF], dna[:, cols], preferred_element_type=F32)
+        return 0
+
+    lax.fori_loop(0, 2, down, 0)
+    load(7)
+
+    def finish_out(r, _):
+        nb[block(r), :] = (mid[block(r), :] + keep_of(r) * facc[block(r), :]).astype(BF)
+        return 0
+
+    lax.fori_loop(0, ROWS // STEP, finish_out, 0)
+    load(8)
+    step(DN1, 1)
+    for p in (KS, VS):
+        first_done(p, 1 - x, 0)
+    step(QS, 0)
+    loaded(7)
+
+    def back_qkv(n, _):
+        cols = at(n * 512, 512)
+        facc[:, cols] = dot_nt(pk[0:ROWS, :], wq[cols, :])
+        return 0
+
+    lax.fori_loop(0, 2, back_qkv, 0)
+
+    def norm_one_back(r, _):
+        total = gm[block(r), :] + norm_back(tok[block(r), :].astype(F32), facc[block(r), :], g1[...], 0)
+        tok[block(r), :] = total.astype(BF)
+        return 0
+
+    lax.fori_loop(0, ROWS // STEP, norm_one_back, 0)
+    load(9)
+
+    vbuf[0] = jnp.concatenate(
+        [jnp.sum(vsum[n], axis=0, keepdims=True) for n in range(4)] + [jnp.zeros((4, D), F32)], axis=0
+    )
+
+    def vec(n):
+        return remote(M_VEC + n, "cxylh"[n], vbuf.at[n], vrecv.at[n])
+
+    def vec_step(n):
+        vec(n).wait()
+        vbuf[n + 1] = vbuf[n] + vrecv[n]
+        if n < 4:
+            vec(n + 1).start()
+
+    vec(0).start()
+    for p in (KS, VS):
+        first_done(p, x, 1)
+        red(p, 1).start()
+    vec_step(0)
+    for p in (UP0, UP1, DN0, DN1):
+        step(p, 2)
+    step(OUT, 1)
+    step(QS, 1)
+    vec_step(1)
+    step(KS, 1)
+    step(VS, 1)
+    step(OUT, 2)
+    vec_step(2)
+    for half in range(2):
+        gup_o[:, half * WIDE:(half + 1) * WIDE] = result(UP0 + half)
+    for half in range(2):
+        gdn_o[half * WIDE:(half + 1) * WIDE, :] = result(DN0 + half).T
+    vec_step(3)
+
+    def share(p):
+        quarters(p - OUT, own_quarter)[...] = result(p).astype(BF)
+        gather_c(p - OUT).start()
+        gather_x(p - OUT).start()
+
+    def pass_on(p):
+        gather_x(p - OUT).wait()
+        gather_f(p - OUT).start()
+
+    def write(p, dst, base):
+        gather_c(p - OUT).wait()
+        gather_f(p - OUT).wait()
+        q = p - OUT
+        dst[base:base + 128, :] = xgb[q * 128:(q + 1) * 128, :].astype(F32)
+
+    share(OUT)
+    step(QS, 2)
+    step(KS, 2)
+    step(VS, 2)
+    vec_step(4)
+    pass_on(OUT)
+    for n, ref in enumerate((gg1_o, gs1_o, gg2_o, gs2_o)):
+        ref[...] = vbuf[5, n:n + 1, at(s * 128, 128)]
+    share(QS)
+    share(KS)
+    share(VS)
+    write(OUT, gm, 0)
+    load(10)
+    pass_on(QS)
+    pass_on(KS)
+    pass_on(VS)
+    for n, p in enumerate((QS, KS, VS)):
+        write(p, facc, 128 * n)
+        load(11 + n)
+    for i in range(8, 14):
+        loaded(i)
+
+
+def fused(
+    tokens, cotangent, live_items, qkv_weight, out_weight, up_weight, down_weight,
+    gain_one, shift_one, gain_two, shift_two,
+):
+    rows_of = [v.reshape(1, D) for v in (gain_one, shift_one, gain_two, shift_two)]
+    hbm, vmem = pl.BlockSpec(memory_space=pl.ANY), pl.BlockSpec(memory_space=pltpu.VMEM)
+    shape = jax.ShapeDtypeStruct
+    outs = pl.pallas_call(
+        layer_kernel,
+        name="layer",
+        out_shape=(
+            shape((ROWS, D), BF), shape((ROWS, D), BF), shape((128, 3 * D), F32), shape((128, D), F32),
+            shape((128, SHARD), F32), shape((SHARD, 128), F32),
+            shape((1, 128), F32), shape((1, 128), F32), shape((1, 128), F32), shape((1, 128), F32),
+        ),
+        in_specs=[hbm, hbm, pl.BlockSpec(memory_space=pltpu.SMEM), hbm, hbm, hbm, hbm, vmem, vmem, vmem, vmem],
+        out_specs=[hbm] * 4 + [vmem] * 6,
+        scratch_shapes=[
+            pltpu.VMEM((D, 3 * D), BF), pltpu.VMEM((D, D), BF), pltpu.VMEM((D, FF), BF), pltpu.VMEM((FF, D), BF),
+            pltpu.VMEM((ROWS, D), BF), pltpu.VMEM((PAD, D), BF), pltpu.VMEM((PAD, D), BF), pltpu.VMEM((PAD, D), BF),
+            pltpu.VMEM((PAD, 3 * D), BF), pltpu.VMEM((PAD, 3 * 512), BF),
+            pltpu.VMEM((D, 2 * PAD), BF), pltpu.VMEM((D, 2 * PAD), BF), pltpu.VMEM((D, 2 * PAD), BF),
+            pltpu.VMEM((D, 2 * PAD), BF),
+            pltpu.VMEM((16, TILE, TILE), BF), pltpu.VMEM((TILE, TILE), F32),
+            pltpu.VMEM((ROWS, D), F32), pltpu.VMEM((ROWS, D), F32), pltpu.VMEM((ROWS, D), F32),
+            pltpu.VMEM((PAD, 2 * SHARD), BF), pltpu.VMEM((PAD, 2 * SHARD), BF),
+            pltpu.VMEM((PAD, D), BF), pltpu.VMEM((PAD, 512), BF),
+            pltpu.VMEM((8, 2, 2, 2, 2, 128, WIDE), BF),
+            pltpu.VMEM((8, 2, 2, 2, 128, WIDE), BF), pltpu.VMEM((8, 2, 2, 128, WIDE), BF),
+            pltpu.VMEM((8, 2, 128, WIDE), BF), pltpu.VMEM((8, 128, WIDE), BF),
+            pltpu.VMEM((4, 8, D), F32), pltpu.VMEM((6, 8, D), F32), pltpu.VMEM((5, 8, D), F32),
+            pltpu.SemaphoreType.DMA((N_MSG,)), pltpu.SemaphoreType.DMA((N_MSG,)), pltpu.SemaphoreType.DMA((14,)),
+        ],
+        compiler_params=pltpu.CompilerParams(
+            collective_id=0, has_side_effects=True, vmem_limit_bytes=67_043_328
+        ),
+    )(tokens, cotangent, live_items, qkv_weight, out_weight, up_weight, down_weight, *rows_of)
+    return (*outs[:6], *(v.reshape(128) for v in outs[6:]))
+
+
 IN_SPECS = (
     P(("seq", "ff"), None), P(("seq", "ff"), None), P("seq"), P(), P(), P(None, "ff"), P("ff", None),
     P(), P(), P(), P(),
@@ -127,4 +808,5 @@
 
 
 def solution(mesh):
-    return jax.shard_map(general, mesh=mesh, in_specs=IN_SPECS, out_specs=OUT_SPECS, check_vma=False)
+    body = fused if (mesh.shape["seq"], mesh.shape["ff"]) == (8, 4) else general
+    return jax.shard_map(body, mesh=mesh, in_specs=IN_SPECS, out_specs=OUT_SPECS, check_vma=False)

time: 554 us -> 151 us (0.27)
  waiting for transfers between devices: 316 us -> 0 us
  Pallas kernels: 0 us -> 139 us
  matrix products: 113 us -> 0 us
  blocking collectives: 41.5 us -> 0 us
  local copies, waits for them, and re-layouts: 43.6 us -> 10 us
  other arithmetic: 19 us -> 0 us
  between operations: 16.5 us -> 1.35 us
    reduce_scatter x5 -> x0, waiting for transfers between devices: 258 us -> none  [scatter(): return lax.psum_scatter(x, axis, scatter_dimension=dim, tiled=True)]
    pallas_call x0 -> x1, Pallas kernels: none -> 139 us  [fused(): pl.pallas_call(layer_kernel, name='layer', out_shape=(shape((ROWS, D), BF...]
    dot_general x52 -> x0, matrix products: 97.1 us -> none  [the longest x12 56.5 us: dot(): return jnp.dot(a, b, preferred_element_type=F32)]
    psum x1 -> x0, waiting for transfers between devices: 36 us -> none  [general(): lax.psum(scatter(g, 'seq', 0), 'ff').astype(F32)]
    unnamed x1 -> x0, blocking collectives: 35.3 us -> none
    unnamed x237 -> x26, local copies, waits for them, and re-layouts: 38.9 us -> 10 us
    unnamed x10 -> x0, waiting for transfers between devices: 22 us -> none
    sub x8 -> x0, matrix products: 15.7 us -> none  [attend_forward(): probs = jax.nn.softmax(scores_of(q, k, allowed), axis=-1)]
  transfers between devices with their start and end apart: 9 -> 0, of which waited for: 6 -> 0; matrix products, arithmetic and copies ran while one was open for 30% -> 0% of each run, Pallas kernels for 0% -> 0%
where the time goes in v2:
time: 151 us; the launch traced here: 150 us
  Pallas kernels  139 us (92%)
  local copies, waits for them, and re-layouts  10 us (7%)
    pallas_call x1, Pallas kernels, fused(): pl.pallas_call(layer_kernel, name='layer', out_shape=(shape((ROWS, D), BF...  139 us
    unnamed x26, local copies, waits for them, and re-layouts  10 us

profile of v2, /device:TPU:0, one launch (start us, length us, event | category | flops | bytes accessed | tf_op | source)
XLA Modules:
  0.0 150.3 jit_solution(1763934399194425505)
XLA Ops:
  1.3 138.9 %layer.1 = (bf16[480,1024]{1,0:T(8,128)(2,1)}, bf16[480,1024]{1,0:T(8,128)(2,1)}, f32[128,3072]{1,0:T(8,128)}, f32[128,1024]{1,0:T(8,128)}, f32[128,512]{1,0:T(8...) custom-call(bf16[480,1024]{1,0:T(8,128)(2,1)} %tok_h.1, ...), custom_call_target="tpu_custom_call" | custom-call | tf_op jit(solution)/shard_map/layer/pallas_call | solution.py:767
  140.2 0.0 copy-start
  140.2 2.3 %copy.32 = bf16[480,1024]{1,0:T(8,128)(2,1)} copy(bf16[480,1024]{1,0:T(8,128)(2,1)} %get-tuple-element.40) | data formatting | bytes 1966080
  142.6 0.0 copy-start.1
  142.6 2.3 %copy.33 = bf16[480,1024]{1,0:T(8,128)(2,1)} copy(bf16[480,1024]{1,0:T(8,128)(2,1)} %get-tuple-element.41) | data formatting | bytes 1966080
  144.8 0.0 copy-done
  144.8 0.0 copy-start.3
  144.8 0.0 copy-start.2
  144.8 0.0 copy-start.7
  144.8 0.0 copy-start.6
  144.8 0.0 copy-start.5
  144.9 0.0 copy-start.4
  144.9 1.1 copy.34
  146.0 0.0 copy-done.1
  146.0 0.8 copy.35
  146.8 0.0 copy-done.3
  146.8 0.7 copy.36
  147.5 0.0 copy-done.2
  147.5 0.7 copy.37
  148.2 0.0 copy-done.7
  148.2 0.5 copy.38
  148.7 0.0 copy-done.6
  148.7 0.5 copy.39
  149.2 0.0 copy-done.5
  149.2 0.5 copy.40
  149.8 0.0 copy-done.4
  149.8 0.5 copy.41
Async XLA Ops:
  140.2 4.6 %copy-start = (f32[128,3072]{1,0:T(8,128)S(1)}, f32[128,3072]{1,0:T(8,128)}, u32[]{:S(2)}) copy-start(f32[128,3072]{1,0:T(8,128)} %get-tuple-element.42) | copy-start | bytes 4718596
  142.6 3.5 %copy-start.1 = (f32[128,1024]{1,0:T(8,128)S(1)}, f32[128,1024]{1,0:T(8,128)}, u32[]{:S(2)}) copy-start(f32[128,1024]{1,0:T(8,128)} %get-tuple-element.43) | copy-start | bytes 1572868
  144.8 2.0 %copy-start.3 = (f32[128,512]{1,0:T(8,128)S(1)}, f32[128,512]{1,0:T(8,128)}, u32[]{:S(2)}) copy-start(f32[128,512]{1,0:T(8,128)} %get-tuple-element.44) | copy-start | bytes 786436
  144.8 2.7 %copy-start.2 = (f32[512,128]{1,0:T(8,128)S(1)}, f32[512,128]{1,0:T(8,128)}, u32[]{:S(2)}) copy-start(f32[512,128]{1,0:T(8,128)} %get-tuple-element.45) | copy-start | bytes 786436
  144.8 3.4 %copy-start.7 = (f32[1,128]{1,0:T(1,128)S(1)}, f32[1,128]{1,0:T(1,128)}, u32[]{:S(2)}) copy-start(f32[1,128]{1,0:T(1,128)} %get-tuple-element.26) | copy-start | bytes 1540
  144.8 3.9 %copy-start.6 = (f32[1,128]{1,0:T(1,128)S(1)}, f32[1,128]{1,0:T(1,128)}, u32[]{:S(2)}) copy-start(f32[1,128]{1,0:T(1,128)} %get-tuple-element.27) | copy-start | bytes 1540
  144.8 4.4 %copy-start.5 = (f32[1,128]{1,0:T(1,128)S(1)}, f32[1,128]{1,0:T(1,128)}, u32[]{:S(2)}) copy-start(f32[1,128]{1,0:T(1,128)} %get-tuple-element.28) | copy-start | bytes 1540
  144.9 4.9 %copy-start.4 = (f32[1,128]{1,0:T(1,128)S(1)}, f32[1,128]{1,0:T(1,128)}, u32[]{:S(2)}) copy-start(f32[1,128]{1,0:T(1,128)} %get-tuple-element.29) | copy-start | bytes 1540

commit v3 on v2

--- a/solution.py
+++ b/solution.py
@@ -122,21 +122,97 @@
 ROWS, PAD, D, FF, SHARD = 480, 512, 1024, 2048, 512
 TILE = 240
 WIDE = 256
-STEP = 32
+STEP = 96
 UP0, UP1, DN0, DN1, OUT, QS, KS, VS = range(8)
 ORDER = {
     UP0: "lyxh", UP1: "ylxh", DN0: "lxyh", DN1: "xylh", OUT: "xylh", QS: "xlyh", KS: "yxlh", VS: "lyxh",
 }
 EYES = "xhly"
 M_UPC, M_DNC = 0, 1
-M_WX, M_WL, M_WCX, M_WCL = 2, 6, 10, 14
-M_GBT, M_N2T, M_MXT, M_N1T, M_GA = 18, 19, 20, 21, 22
-M_HID, M_GPR = 23, 25
-M_PK = 27
-M_RED = 33
-M_AGC, M_AGX, M_AGF = 73, 77, 81
-M_VEC = 85
-N_MSG = 90
+M_W = 2
+M_GBT, M_N2T, M_MXT, M_N1T, M_GA = 42, 43, 44, 45, 46
+M_HID, M_GPR = 47, 49
+M_PK = 51
+M_RED = 57
+M_AGC, M_AGX, M_AGF = 97, 101, 105
+M_VEC = 109
+N_MSG = 114
+WAYS = ("X", "Y", "L", "P", "Q")
+SCHED = {
+    ("qkv", 5): (
+        ("X", 0),
+    ),
+    ("att", 0): (
+        ("X", 1),
+    ),
+    ("att", 2): (
+        ("Y", 0), ("L", 0), ("X", 2),
+    ),
+    "mxt": (
+        ("Y", 1), ("L", 1),
+    ),
+    "proj": (
+        ("X", 3), ("P", 0), ("Q", 0),
+    ),
+    "n2t": (
+        ("Y", 2), ("L", 2),
+    ),
+    ("sh", 0): (
+        ("P", 1), ("Q", 1),
+    ),
+    ("sum", 0): (
+        ("Y", 3), ("L", 3),
+    ),
+    ("sum", 2): (
+        ("P", 2), ("Q", 2),
+    ),
+    "weights": (
+        ("P", 3), ("Q", 3),
+    ),
+    ("sum", 5): (
+        ("R", UP0, 0, 0), ("R", UP1, 0, 0),
+    ),
+    "ln2b": (
+        ("R", DN0, 0, 0),
+    ),
+    "osum": (
+        ("R", UP1, 0, 1),
+    ),
+    ("pr", 0): (
+        ("R", UP0, 0, 1),
+    ),
+    ("qs", 0): (
+        ("R", DN1, 0, 0),
+    ),
+    ("pr", 2): (
+        ("R", DN0, 0, 1),
+    ),
+    ("pr", 3): (
+        ("R", UP0, 1, 0),
+    ),
+    ("dwn", 0): (
+        ("R", UP1, 1, 0),
+    ),
+    ("dwn", 1): (
+        ("R", KS, 0, 0),
+    ),
+    "fin": (
+        ("R", OUT, 0, 0),
+    ),
+    ("gn1", 0): (
+        ("R", VS, 0, 0),
+    ),
+    ("gn1", 1): (
+        ("R", DN1, 1, 0),
+    ),
+    "tail": (
+        ("V", 0), ("R", VS, 0, 1), ("R", KS, 0, 1), ("R", DN1, 2, 0), ("R", QS, 0, 0), ("R", OUT, 1, 0),
+        ("R", DN1, 3, 0), ("R", DN0, 1, 0), ("R", UP0, 2, 0), ("R", QS, 1, 0), ("R", VS, 1, 0), ("R", UP1, 2, 0),
+        ("R", OUT, 2, 0), ("V", 1), ("R", DN0, 2, 0), ("R", UP0, 3, 0), ("R", QS, 2, 0), ("V", 2), ("R", UP1, 3, 0),
+        ("R", KS, 1, 0), ("R", OUT, 3, 0), ("R", VS, 2, 0), ("R", DN0, 3, 0), ("G", 0), ("V", 3), ("R", QS, 3, 0),
+        ("R", KS, 2, 0), ("G", 1), ("R", VS, 3, 0), ("V", 4), ("G", 3), ("R", KS, 3, 0), ("G", 2),
+    ),
+}
 
 
 def dot_nt(a, b):
@@ -145,7 +221,7 @@
 
 def layer_kernel(
     tok_h, cot_h, live, wq_h, wo_h, up_h, dn_h, g1, s1, g2, s2,
-    lo_h, gt_h, gqkv_h, gout_h, gup_o, gdn_o, gg1_o, gs1_o, gg2_o, gs2_o,
+    lo_h, gt_h, gq_h, gup_o, gdn_o, gg1_o, gs1_o, gg2_o, gs2_o,
     wq, wo, upa, dna, tok, gb, nb, mx, pk, pks, xgb, xn2, xmx, xn1, probs, mask, mid, gm, facc,
     hids, gprs, ga, gas, gw, r0, r1, r2, r3, vsum, vbuf, vrecv, ssem, rsem, lsem,
 ):
@@ -166,9 +242,7 @@
     loads = {
         0: (tok_h, tok), 1: (cot_h, gb.at[0:ROWS]), 2: (wq_h, wq), 3: (wo_h, wo), 4: (up_h, upa.at[:, 0:SHARD]),
         5: (dn_h, dna.at[0:SHARD]), 6: (cot_h, nb.at[0:ROWS]), 7: (wq_h, wq),
-        8: (nb.at[0:ROWS], lo_h), 9: (tok, gt_h), 10: (gm.at[0:128], gout_h),
-        11: (facc.at[0:128], gqkv_h.at[:, 0:D]), 12: (facc.at[128:256], gqkv_h.at[:, D:2 * D]),
-        13: (facc.at[256:384], gqkv_h.at[:, 2 * D:3 * D]),
+        8: (nb.at[0:ROWS], lo_h), 9: (tok, gt_h), 10: (xgb.at[0:512], gq_h),
     }
 
     def load(i):
@@ -182,36 +256,51 @@
             src_ref=src, dst_ref=dst, send_sem=ssem.at[i], recv_sem=rsem.at[i], device_id=mate[to], device_id_type=MESH
         )
 
-    def quarter(k, own, slot, whole):
-        half = bit["l"] if own else 1 - bit["l"]
+    def region(k, way, slot):
+        yb = bit["y"] if way in ("X", "L") else 1 - bit["y"]
+        lb = bit["l"] if way in ("X", "Y") else 1 - bit["l"]
+        size = 128 if k < 2 else 64
+        start = (2 * yb + lb) * (2 * size) + (k % 2) * size
+        if way in ("P", "Q"):
+            size //= 2
+            start = start + (size if way == "Q" else 0)
+        rows = at(start, size, 32)
+        if slot is None:
+            return up_h.at[rows, :] if k < 2 else dn_h.at[rows, :]
         if k < 2:
-            rows = at(half * 512 + k * 256, 256)
-            return (up_h.at[rows, :] if whole else upa.at[rows, slot * SHARD:(slot + 1) * SHARD])
-        start = half * 256 + (k - 2) * 128
-        return dn_h.at[at(start, 128), :] if whole else dna.at[at(slot * SHARD + start, 128), :]
-
-    def weight_x(k):
-        half_mate = quarter(k, True, 2, True)
-        return remote(M_WX + k, "x", half_mate, quarter(k, True, 2, False))
-
-    def weight_l(k):
-        ref = quarter(k, True, 2, False)
-        return remote(M_WL + k, "l", ref, ref)
-
-    def weight_cx(k):
-        return remote(M_WCX + k, "c", quarter(k, True, 2, False), quarter(k, True, 3, False))
-
-    def weight_cl(k):
-        return remote(M_WCL + k, "c", quarter(k, False, 2, False), quarter(k, False, 3, False))
-
-    def relay_x(k):
-        weight_x(k).wait()
-        weight_l(k).start()
-        weight_cx(k).start()
-
-    def relay_l(k):
-        weight_l(k).wait()
-        weight_cl(k).start()
+            return upa.at[rows, slot * SHARD:(slot + 1) * SHARD]
+        return dna.at[at(slot * SHARD + start, size, 32), :]
+
+    def onward(k, way):
+        yb = bit["y"] if way == "Q" else 1 - bit["y"]
+        lb = bit["l"] if way == "P" else 1 - bit["l"]
+        size = 64 if k < 2 else 32
+        start = (2 * yb + lb) * (4 * size) + (k % 2) * (2 * size) + (size if way == "Q" else 0)
+        if k < 2:
+            return upa.at[at(start, size, 32), 2 * SHARD:3 * SHARD]
+        return dna.at[at(2 * SHARD + start, size, 32), :]
+
+    def weight(k, way):
+        i = M_W + k * 10 + WAYS.index(way)
+        if way == "X":
+            return remote(i, "x", region(k, "X", None), region(k, "X", 2))
+        if way in ("Y", "L"):
+            return remote(i, way.lower(), region(k, "X", 2), region(k, "X", 2))
+        return remote(i, "l" if way == "P" else "y", onward(k, way), onward(k, way))
+
+    def weight_mate(k, way):
+        return remote(M_W + k * 10 + 5 + WAYS.index(way), "c", region(k, way, 2), region(k, way, 3))
+
+    def relay(way, k):
+        weight(k, way).wait()
+        if way == "X":
+            weight(k, "Y").start()
+            weight(k, "L").start()
+        elif way == "Y":
+            weight(k, "P").start()
+        elif way == "L":
+            weight(k, "Q").start()
+        weight_mate(k, way).start()
 
     def weight_c(which):
         if which == 0:
@@ -284,31 +373,40 @@
 
         lax.fori_loop(0, 1 << count, body, 0)
 
+    parts_done = {}
+
     def first(p, xb, part):
         if ORDER[p][0] != "x":
             red(p, 0, xb, part).start()
-        elif isinstance(xb, int):
-            if xb == 1:
-                red(p, 0).start()
-        elif part == 0:
+        elif (part == 1) == (p < OUT):
             red(p, 0).start()
 
-    def first_done(p, xb, part):
-        red(p, 0, xb, part).wait()
-        add(p, 0, xb)
-
-    def done(p, k):
-        red(p, k).wait()
-        add(p, k)
-
-    def step(p, k):
-        done(p, k)
-        red(p, k + 1).start()
-
-    def result(p):
-        red(p, 3).wait()
-        own = bits_of(p)
-        return gw[(p, *(own[e] for e in EYES))].astype(F32) + r3[p].astype(F32)
+    def reduced(p, k, part):
+        if k == 0 and ORDER[p][0] != "x" and p != OUT:
+            xb = part if p < OUT else (1 - x if part == 0 else x)
+            red(p, 0, xb, part).wait()
+            add(p, 0, xb)
+            parts_done[p] = parts_done.get(p, 0) + 1
+            if parts_done[p] == 2:
+                red(p, 1).start()
+        elif k < 3:
+            red(p, k).wait()
+            add(p, k)
+            red(p, k + 1).start()
+        else:
+            red(p, 3).wait()
+            own = bits_of(p)
+            total = gw[(p, *(own[e] for e in EYES))].astype(F32) + r3[p].astype(F32)
+            if p in (UP0, UP1):
+                half = p - UP0
+                gup_o[:, half * WIDE:(half + 1) * WIDE] = total
+            elif p in (DN0, DN1):
+                half = p - DN0
+                gdn_o[half * WIDE:(half + 1) * WIDE, :] = total.T
+            else:
+                quarters(p - OUT, own_quarter)[...] = total.astype(BF)
+                gather_c(p - OUT).start()
+                gather_x(p - OUT).start()
 
     def quarters(q, n):
         return xgb.at[q * 128:(q + 1) * 128, at(n * WIDE, WIDE)]
@@ -324,6 +422,39 @@
     def gather_f(q):
         other = 2 * c + 1 - x
         return remote(M_AGF + q, "c", quarters(q, other), quarters(q, other))
+
+    def vec(n):
+        return remote(M_VEC + n, "cxylh"[n], vbuf.at[n], vrecv.at[n])
+
+    def vec_step(n):
+        vec(n).wait()
+        vbuf[n + 1] = vbuf[n] + vrecv[n]
+        if n < 4:
+            vec(n + 1).start()
+
+    def handle(event):
+        kind = event[0]
+        if kind == "R":
+            reduced(*event[1:])
+        elif kind == "G":
+            gather_x(event[1]).wait()
+            gather_f(event[1]).start()
+        elif kind == "V":
+            vec_step(event[1])
+        else:
+            relay(kind, event[1])
+
+    def poll(name):
+        for event in SCHED.get(name, ()):
+            handle(event)
+
+    def poll_at(name, i, count):
+        for n in range(count):
+            if (name, n) in SCHED:
+                @pl.when(i == n)
+                def _():
+                    for event in SCHED[(name, n)]:
+                        handle(event)
 
     limit = (live[0] - f * (ROWS // 15)) * 15
 
@@ -347,19 +478,26 @@
 
         lax.fori_loop(0, D // 128, body, 0)
 
-    for i in range(6):
-        load(i)
+    load(0)
+    load(2)
     barrier = pltpu.get_barrier_semaphore()
     for e in "xylhc":
         pl.semaphore_signal(barrier, inc=1, device_id=mate[e], device_id_type=MESH)
-    for ref in (gb, nb, mx, ga):
+    for i in (1, 3, 4, 5):
+        load(i)
+    qi = lax.broadcasted_iota(jnp.int32, (TILE, TILE), 0)
+    ki = lax.broadcasted_iota(jnp.int32, (TILE, TILE), 1)
+    mask[...] = jnp.where((ki <= qi) & (ki >= qi - lax.rem(qi, 15)), 0.0, -1e30).astype(F32)
+    nb[ROWS:PAD, :] = jnp.zeros((PAD - ROWS, D), BF)
+    pl.semaphore_wait(barrier, 5)
+    for k in range(4):
+        weight(k, "X").start()
+    weight_c(0).start()
+    weight_c(1).start()
+    for ref in (gb, mx, ga):
         ref[ROWS:PAD, :] = jnp.zeros((PAD - ROWS, D), BF)
     pk[ROWS:PAD, :] = jnp.zeros((PAD - ROWS, 3 * D), BF)
     vsum[...] = jnp.zeros(vsum.shape, F32)
-    qi = lax.broadcasted_iota(jnp.int32, (TILE, TILE), 0)
-    ki = lax.broadcasted_iota(jnp.int32, (TILE, TILE), 1)
-    mask[...] = jnp.where((ki <= qi) & (ki >= qi - lax.rem(qi, 15)), 0.0, -1e30).astype(F32)
-
     loaded(0)
 
     def norm_one(r, _):
@@ -368,23 +506,19 @@
         return 0
 
     lax.fori_loop(0, ROWS // STEP, norm_one, 0)
-    pl.semaphore_wait(barrier, 5)
-    for k in range(4):
-        weight_x(k).start()
-    weight_c(0).start()
-    weight_c(1).start()
-
+    poll("ln1")
     loaded(2)
 
     def qkv(n, _):
         cols = at(n * 512, 512)
         pk[0:ROWS, cols] = jnp.dot(nb[0:ROWS, :], wq[:, cols], preferred_element_type=F32).astype(BF)
+        poll_at("qkv", n, 6)
         return 0
 
     lax.fori_loop(0, 6, qkv, 0)
     turn(nb, xn1)
     turned(M_N1T, xn1).start()
-
+    poll("n1t")
     loaded(1)
 
     def mask_cot(r, _):
@@ -394,23 +528,24 @@
     lax.fori_loop(0, ROWS // STEP, mask_cot, 0)
     turn(gb, xgb)
     turned(M_GBT, xgb).start()
-
-    def attend(h, _):
-        cols = [at(part * D + h * 128, 128) for part in range(3)]
-        for t in range(2):
+    poll("gbt")
+
+    def attend(i, _):
+        for h, t in ((i * 2 + n, t) for n in range(2) for t in range(2)):
+            cols = [at(part * D + h * 128, 128) for part in range(3)]
             rows = slice(t * TILE, (t + 1) * TILE)
             sc = dot_nt(pk[rows, cols[0]], pk[rows, cols[1]]) * (128 ** -0.5) + mask[...]
             w = jnp.exp(sc - jnp.max(sc, axis=-1, keepdims=True))
             p = (w * (1.0 / jnp.sum(w, axis=-1, keepdims=True))).astype(BF)
             probs[h * 2 + t] = p
             mx[rows, at(h * 128, 128)] = jnp.dot(p, pk[rows, cols[2]], preferred_element_type=F32).astype(BF)
-        return 0
-
-    lax.fori_loop(0, 8, attend, 0)
-    relay_x(0)
+        poll_at("att", i, 4)
+        return 0
+
+    lax.fori_loop(0, 4, attend, 0)
     turn(mx, xmx)
     turned(M_MXT, xmx).start()
-
+    poll("mxt")
     loaded(3)
 
     def project(n, _):
@@ -419,6 +554,7 @@
         return 0
 
     lax.fori_loop(0, 2, project, 0)
+    poll("proj")
 
     def norm_two(r, _):
         m = tok[block(r), :].astype(F32) + keep_of(r) * facc[block(r), :]
@@ -428,14 +564,13 @@
         return 0
 
     lax.fori_loop(0, ROWS // STEP, norm_two, 0)
-    relay_x(1)
+    poll("ln2")
     turn(nb, xn2)
     turned(M_N2T, xn2).start()
+    poll("n2t")
 
     loaded(4)
     loaded(5)
-    weight_c(0).wait()
-    weight_c(1).wait()
     wq[ROWS:PAD, 0:FF] = jnp.zeros((PAD - ROWS, FF), BF)
     wq[PAD + ROWS:2 * PAD, 0:FF] = jnp.zeros((PAD - ROWS, FF), BF)
 
@@ -451,11 +586,17 @@
         wq[PAD:PAD + ROWS, cols] = (gh * slope).astype(BF)
 
     def group(g, _):
+        @pl.when(g == 0)
+        def _():
+            weight_c(0).wait()
+            weight_c(1).wait()
+
         @pl.when(g == 1)
         def _():
+            poll("weights")
             for k in range(4):
-                weight_cx(k).wait()
-                weight_cl(k).wait()
+                for way in WAYS:
+                    weight_mate(k, way).wait()
 
         def one(n, _):
             shard(2 * g + 1 - n)
@@ -465,20 +606,13 @@
                 hid_copy(g).start()
                 gpr_copy(g).start()
 
-                @pl.when(g == 0)
-                def _():
-                    relay_x(2)
-                    relay_l(0)
-                    relay_l(1)
-
+            poll_at("sh", 2 * g + n, 4)
             return 0
 
         lax.fori_loop(0, 2, one, 0)
 
         @pl.when(g == 0)
         def _():
-            relay_x(3)
-            relay_l(2)
             turned(M_N2T, xn2).wait()
             turned(M_GBT, xgb).wait()
 
@@ -486,28 +620,27 @@
         gpr_copy(g).wait()
         mine, theirs = at(2 * g * SHARD, SHARD), at(g * SHARD, SHARD)
 
-        def sums(n, _):
+        def sums(i, _):
+            n = lax.rem(i, 2)
             rows = at(n * 512, 512)
-            for lhs, top, low, p in ((xn2, PAD, gprs, UP0), (xgb, 0, hids, DN0)):
-                rhs = jnp.concatenate([wq[top:top + PAD, mine], low[:, theirs]], axis=0)
-                total = jnp.dot(lhs[rows, :], rhs, preferred_element_type=F32).astype(BF)
-                for half in range(2):
-                    gw[p + half, g, n] = total[:, half * WIDE:(half + 1) * WIDE].reshape(2, 2, 128, WIDE)
+            for m, lhs, top, low, p in ((0, xn2, PAD, gprs, UP0), (1, xgb, 0, hids, DN0)):
+                @pl.when(i // 2 == m)
+                def _():
+                    rhs = jnp.concatenate([wq[top:top + PAD, mine], low[:, theirs]], axis=0)
+                    total = jnp.dot(lhs[rows, :], rhs, preferred_element_type=F32).astype(BF)
+                    for half in range(2):
+                        gw[p + half, g, n] = total[:, half * WIDE:(half + 1) * WIDE].reshape(2, 2, 128, WIDE)
+
+                    for part in range(2):
+                        @pl.when((n == 1) & (g == part))
+                        def _():
+                            for half in range(2):
+                                first(p + half, part, part)
+
+            poll_at("sum", 4 * g + i, 8)
             return 0
 
-        lax.fori_loop(0, 2, sums, 0)
-
-        @pl.when(g == 0)
-        def _():
-            for p in (UP0, UP1, DN0, DN1):
-                first(p, 0, 0)
-            relay_l(3)
-
-        @pl.when(g == 1)
-        def _():
-            for p in (DN1, UP0, UP1, DN0):
-                first(p, 1, 1)
-
+        lax.fori_loop(0, 4, sums, 0)
         return 0
 
     lax.fori_loop(0, 2, group, 0)
@@ -516,11 +649,10 @@
     def back_up(n, _):
         cols = at(n * 512, 512)
         facc[:, cols] = dot_nt(wq[PAD:PAD + ROWS, 0:FF], upa[cols, :])
+        poll_at("bup", n, 2)
         return 0
 
     lax.fori_loop(0, 2, back_up, 0)
-    for p in (UP0, UP1, DN0):
-        first_done(p, 0, 0)
     loaded(6)
 
     def row_sum(v):
@@ -544,6 +676,7 @@
 
     lax.fori_loop(0, ROWS // STEP, norm_two_back, 0)
     ga_copy().start()
+    poll("ln2b")
 
     def back_out(n, _):
         cols = at(n * 512, 512)
@@ -552,6 +685,7 @@
 
     turned(M_MXT, xmx).wait()
     lax.fori_loop(0, 2, back_out, 0)
+    poll("bout")
     ga_copy().wait()
 
     def out_sums(n, _):
@@ -564,14 +698,12 @@
 
     lax.fori_loop(0, 2, out_sums, 0)
     red(OUT, 0).start()
-    for p in (UP0, UP1, DN0):
-        first_done(p, 1, 1)
-        red(p, 1).start()
+    poll("osum")
     turned(M_N1T, xn1).wait()
 
-    def head_back(h):
-        cols = [at(part * D + h * 128, 128) for part in range(3)]
-        for t in range(2):
+    def heads_back(h0):
+        for h, t in ((h0 + n, t) for n in range(2) for t in range(2)):
+            cols = [at(part * D + h * 128, 128) for part in range(3)]
             rows = slice(t * TILE, (t + 1) * TILE)
             q, k, v = (pk[rows, col] for col in cols)
             o = mx[rows, at(h * 128, 128)]
@@ -589,22 +721,23 @@
         cb = lax.rem(i + 1 + c, 2)
         later = i // 2
         xb = lax.rem(later + 1 + x, 2)
-
-        def one(n, _):
-            head_back(cb * 4 + xb * 2 + n)
-            return 0
-
-        lax.fori_loop(0, 2, one, 0)
-
+        heads_back(cb * 4 + xb * 2)
         for n in range(2):
-            xn = 1 - x if n == 0 else x
-
             @pl.when(i == 2 * n)
             def _():
                 for part in range(3):
-                    pk_copy(n, xn, part).start()
-
-        def qkv_sums():
+                    pk_copy(n, 1 - x if n == 0 else x, part).start()
+
+        poll_at("pr", i, 4)
+
+        @pl.when(i % 2 == 1)
+        def _():
+            for n in range(2):
+                @pl.when(later == n)
+                def _():
+                    for part in range(3):
+                        pk_copy(n, 1 - x if n == 0 else x, part).wait()
+
             def body(n, _):
                 rows = at(n * 512, 512)
                 rhs = jnp.concatenate(
@@ -620,40 +753,21 @@
                 return 0
 
             lax.fori_loop(0, 2, body, 0)
-
-        @pl.when(i % 2 == 1)
-        def _():
             for n in range(2):
-                xn = 1 - x if n == 0 else x
-
                 @pl.when(later == n)
                 def _():
-                    for part in range(3):
-                        pk_copy(n, xn, part).wait()
-
-            qkv_sums()
-
-        @pl.when(i == 1)
-        def _():
-            for p in (QS, KS, VS):
-                first(p, 1 - x, 0)
-            step(DN1, 0)
-
-        @pl.when(i == 3)
-        def _():
-            for p in (QS, KS, VS):
-                first(p, x, 1)
+                    for p in (QS, KS, VS):
+                        first(p, 1 - x if n == 0 else x, n)
+                    poll(("qs", n))
 
         return 0
 
     lax.fori_loop(0, 4, pair, 0)
-    for p in (UP0, UP1, DN0):
-        step(p, 1)
-    step(OUT, 0)
 
     def down(n, _):
         cols = at(n * 512, 512)
         facc[:, cols] = jnp.dot(wq[0:ROWS, 0:FF], dna[:, cols], preferred_element_type=F32)
+        poll_at("dwn", n, 2)
         return 0
 
     lax.fori_loop(0, 2, down, 0)
@@ -665,15 +779,13 @@
 
     lax.fori_loop(0, ROWS // STEP, finish_out, 0)
     load(8)
-    step(DN1, 1)
-    for p in (KS, VS):
-        first_done(p, 1 - x, 0)
-    step(QS, 0)
+    poll("fin")
     loaded(7)
 
     def back_qkv(n, _):
         cols = at(n * 512, 512)
         facc[:, cols] = dot_nt(pk[0:ROWS, :], wq[cols, :])
+        poll_at("gn1", n, 2)
         return 0
 
     lax.fori_loop(0, 2, back_qkv, 0)
@@ -685,76 +797,42 @@
 
     lax.fori_loop(0, ROWS // STEP, norm_one_back, 0)
     load(9)
-
     vbuf[0] = jnp.concatenate(
         [jnp.sum(vsum[n], axis=0, keepdims=True) for n in range(4)] + [jnp.zeros((4, D), F32)], axis=0
     )
-
-    def vec(n):
-        return remote(M_VEC + n, "cxylh"[n], vbuf.at[n], vrecv.at[n])
-
-    def vec_step(n):
-        vec(n).wait()
-        vbuf[n + 1] = vbuf[n] + vrecv[n]
-        if n < 4:
-            vec(n + 1).start()
-
     vec(0).start()
-    for p in (KS, VS):
-        first_done(p, x, 1)
-        red(p, 1).start()
-    vec_step(0)
-    for p in (UP0, UP1, DN0, DN1):
-        step(p, 2)
-    step(OUT, 1)
-    step(QS, 1)
-    vec_step(1)
-    step(KS, 1)
-    step(VS, 1)
-    step(OUT, 2)
-    vec_step(2)
-    for half in range(2):
-        gup_o[:, half * WIDE:(half + 1) * WIDE] = result(UP0 + half)
-    for half in range(2):
-        gdn_o[half * WIDE:(half + 1) * WIDE, :] = result(DN0 + half).T
-    vec_step(3)
-
-    def share(p):
-        quarters(p - OUT, own_quarter)[...] = result(p).astype(BF)
-        gather_c(p - OUT).start()
-        gather_x(p - OUT).start()
-
-    def pass_on(p):
-        gather_x(p - OUT).wait()
-        gather_f(p - OUT).start()
-
-    def write(p, dst, base):
+    poll("ln1b")
+    poll("tail")
+    for n, ref in enumerate((gg1_o, gs1_o, gg2_o, gs2_o)):
+        ref[...] = vbuf[5, n:n + 1, at(s * 128, 128)]
+    for p in (OUT, QS, KS, VS):
         gather_c(p - OUT).wait()
         gather_f(p - OUT).wait()
-        q = p - OUT
-        dst[base:base + 128, :] = xgb[q * 128:(q + 1) * 128, :].astype(F32)
-
-    share(OUT)
-    step(QS, 2)
-    step(KS, 2)
-    step(VS, 2)
-    vec_step(4)
-    pass_on(OUT)
-    for n, ref in enumerate((gg1_o, gs1_o, gg2_o, gs2_o)):
-        ref[...] = vbuf[5, n:n + 1, at(s * 128, 128)]
-    share(QS)
-    share(KS)
-    share(VS)
-    write(OUT, gm, 0)
     load(10)
-    pass_on(QS)
-    pass_on(KS)
-    pass_on(VS)
-    for n, p in enumerate((QS, KS, VS)):
-        write(p, facc, 128 * n)
-        load(11 + n)
-    for i in range(8, 14):
+    for i in (8, 9, 10):
         loaded(i)
+
+
+def result_kernel(lo, gt, gq, gup, gdn, gg1, gs1, gg2, gs2, lo_o, gt_o, gqkv_o, gout_o, gup_o, gdn_o, gg1_o, gs1_o, gg2_o, gs2_o, lov, gtv, gqv, gqkv, gout, sem):
+    ins = [pltpu.make_async_copy(a, b, sem.at[n]) for n, (a, b) in enumerate(((lo, lov), (gt, gtv), (gq, gqv)))]
+    for copy in ins:
+        copy.start()
+    gup_o[...] = gup[...]
+    gdn_o[...] = gdn[...]
+    for a, b in ((gg1, gg1_o), (gs1, gs1_o), (gg2, gg2_o), (gs2, gs2_o)):
+        b[...] = a[...].reshape(128)
+    outs = [pltpu.make_async_copy(a, b, sem.at[3 + n]) for n, (a, b) in enumerate(((lov, lo_o), (gtv, gt_o), (gout, gout_o), (gqkv, gqkv_o)))]
+    for n in range(2):
+        ins[n].wait()
+        outs[n].start()
+    ins[2].wait()
+    gout[...] = gqv[0:128, :].astype(F32)
+    outs[2].start()
+    for n in range(3):
+        gqkv[:, n * D:(n + 1) * D] = gqv[(n + 1) * 128:(n + 2) * 128, :].astype(F32)
+    outs[3].start()
+    for copy in outs:
+        copy.wait()
 
 
 def fused(
@@ -768,12 +846,12 @@
         layer_kernel,
         name="layer",
         out_shape=(
-            shape((ROWS, D), BF), shape((ROWS, D), BF), shape((128, 3 * D), F32), shape((128, D), F32),
+            shape((ROWS, D), BF), shape((ROWS, D), BF), shape((512, D), BF),
             shape((128, SHARD), F32), shape((SHARD, 128), F32),
             shape((1, 128), F32), shape((1, 128), F32), shape((1, 128), F32), shape((1, 128), F32),
         ),
         in_specs=[hbm, hbm, pl.BlockSpec(memory_space=pltpu.SMEM), hbm, hbm, hbm, hbm, vmem, vmem, vmem, vmem],
-        out_specs=[hbm] * 4 + [vmem] * 6,
+        out_specs=[hbm] * 3 + [vmem] * 6,
         scratch_shapes=[
             pltpu.VMEM((D, 3 * D), BF), pltpu.VMEM((D, D), BF), pltpu.VMEM((D, FF), BF), pltpu.VMEM((FF, D), BF),
             pltpu.VMEM((ROWS, D), BF), pltpu.VMEM((PAD, D), BF), pltpu.VMEM((PAD, D), BF), pltpu.VMEM((PAD, D), BF),
@@ -794,7 +872,21 @@
             collective_id=0, has_side_effects=True, vmem_limit_bytes=67_043_328
         ),
     )(tokens, cotangent, live_items, qkv_weight, out_weight, up_weight, down_weight, *rows_of)
-    return (*outs[:6], *(v.reshape(128) for v in outs[6:]))
+    return pl.pallas_call(
+        result_kernel,
+        name="results",
+        out_shape=(
+            shape((ROWS, D), BF), shape((ROWS, D), BF), shape((128, 3 * D), F32), shape((128, D), F32),
+            shape((128, SHARD), F32), shape((SHARD, 128), F32),
+            shape((128,), F32), shape((128,), F32), shape((128,), F32), shape((128,), F32),
+        ),
+        in_specs=[hbm] * 3 + [vmem] * 6,
+        out_specs=[hbm] * 4 + [vmem] * 6,
+        scratch_shapes=[
+            pltpu.VMEM((ROWS, D), BF), pltpu.VMEM((ROWS, D), BF), pltpu.VMEM((512, D), BF),
+            pltpu.VMEM((128, 3 * D), F32), pltpu.VMEM((128, D), F32), pltpu.SemaphoreType.DMA((7,)),
+        ],
+    )(*outs)
 
 
 IN_SPECS = (

time: 151 us -> 123 us (0.81)
  Pallas kernels: 139 us -> 122 us
  local copies, waits for them, and re-layouts: 10 us -> 0 us
    pallas_call x1, Pallas kernels: 139 us -> 117 us  [fused(): pl.pallas_call(layer_kernel, name='layer', out_shape=(shape((ROWS, D), BF...]
    unnamed x26 -> x0, local copies, waits for them, and re-layouts: 10 us -> none
    pallas_call x0 -> x1, Pallas kernels: none -> 5.08 us  [fused(): pl.pallas_call(result_kernel, name='results', out_shape=(shape((ROWS, D),...]
where the time goes in v3:
time: 123 us
  Pallas kernels  122 us (99%)
  between operations  1.3 us (1%)
    pallas_call x1, Pallas kernels, fused(): pl.pallas_call(layer_kernel, name='layer', out_shape=(shape((ROWS, D), BF...  117 us
    pallas_call x1, Pallas kernels, fused(): pl.pallas_call(result_kernel, name='results', out_shape=(shape((ROWS, D),...  5.08 us

profile of v3, /device:TPU:0, one launch (start us, length us, event | category | flops | bytes accessed | tf_op | source)
XLA Modules:
  0.0 123.1 jit_solution(1986361100941862661)
XLA Ops:
  1.3 116.7 %layer.1 = (bf16[480,1024]{1,0:T(8,128)(2,1)}, bf16[480,1024]{1,0:T(8,128)(2,1)}, bf16[512,1024]{1,0:T(8,128)(2,1)}, f32[128,512]{1,0:T(8,128)}, f32[512,128]{1,...) custom-call(bf16[480,1024]{1,0:T(8,128)(2,1)} %tok_h.1, ...), custom_call_target="tpu_custom_call" | custom-call | tf_op jit(solution)/shard_map/layer/pallas_call | solution.py:845
  118.0 5.1 %results.1 = (bf16[480,1024]{1,0:T(8,128)(2,1)}, bf16[480,1024]{1,0:T(8,128)(2,1)}, f32[128,3072]{1,0:T(8,128)}, f32[128,1024]{1,0:T(8,128)}, f32[128,512]{1,0:T...) custom-call(bf16[480,1024]{1,0:T(8,128)(2,1)} %get-tuple-element.19.lo, ...), custom_call_target="tpu_custom_call" | custom-call | tf_op jit(solution)/shard_map/results/pallas_call | solution.py:875

commit v4 on v3

--- a/solution.py
+++ b/solution.py
@@ -124,93 +124,105 @@
 WIDE = 256
 STEP = 96
 UP0, UP1, DN0, DN1, OUT, QS, KS, VS = range(8)
-ORDER = {
-    UP0: "lyxh", UP1: "ylxh", DN0: "lxyh", DN1: "xylh", OUT: "xylh", QS: "xlyh", KS: "yxlh", VS: "lyxh",
-}
+SUB = 2
+OUT_AT = 1
+LANES = WIDE // SUB
+ORDER = (
+    "lyhx", "yxlh", "xylh", "ylhx", "hyxl", "xylh", "yhlx", "lxyh",
+    "hxly", "yxlh", "xyhl", "xylh", "xyhl", "xyhl", "ylhx", "lyxh",
+)
 EYES = "xhly"
 M_UPC, M_DNC = 0, 1
 M_W = 2
 M_GBT, M_N2T, M_MXT, M_N1T, M_GA = 42, 43, 44, 45, 46
 M_HID, M_GPR = 47, 49
 M_PK = 51
-M_RED = 57
-M_AGC, M_AGX, M_AGF = 97, 101, 105
-M_VEC = 109
-N_MSG = 114
-WAYS = ("X", "Y", "L", "P", "Q")
+M_VEC = 57
+M_RED = 62
+M_AGC = M_RED + 40 * SUB
+M_AGX = M_AGC + 4 * SUB
+M_AGF = M_AGX + 4 * SUB
+N_MSG = M_AGF + 4 * SUB
+WAYS = ("XYLPQ", "XYLPQ", "XYLD", "XYLD")
 SCHED = {
-    ("qkv", 5): (
+    ("qkv", 3): (
         ("X", 0),
     ),
-    ("att", 0): (
+    ("att", 1): (
         ("X", 1),
     ),
-    ("att", 2): (
+    ("att", 3): (
         ("Y", 0), ("L", 0), ("X", 2),
     ),
-    "mxt": (
-        ("Y", 1), ("L", 1),
-    ),
-    "proj": (
-        ("X", 3), ("P", 0), ("Q", 0),
-    ),
-    "n2t": (
-        ("Y", 2), ("L", 2),
+    "ln2": (
+        ("Y", 1), ("L", 1), ("X", 3),
     ),
     ("sh", 0): (
-        ("P", 1), ("Q", 1),
-    ),
-    ("sum", 0): (
+        ("P", 0), ("Q", 0),
+    ),
+    ("sh", 1): (
+        ("D", 2), ("Y", 2), ("L", 2),
+    ),
+    ("sum", 1): (
+        ("P", 1), ("Q", 1), ("D", 3),
+    ),
+    "weights": (
         ("Y", 3), ("L", 3),
     ),
-    ("sum", 2): (
-        ("P", 2), ("Q", 2),
-    ),
-    "weights": (
-        ("P", 3), ("Q", 3),
+    ("sh", 2): (
+        ("R", 6, 0, 0),
     ),
     ("sum", 5): (
-        ("R", UP0, 0, 0), ("R", UP1, 0, 0),
+        ("R", 7, 0, 0), ("R", 1, 0, 0),
+    ),
+    ("sum", 6): (
+        ("R", 4, 0, 0),
+    ),
+    ("bup", 0): (
+        ("R", 0, 0, 0), ("R", 3, 0, 0),
     ),
     "ln2b": (
-        ("R", DN0, 0, 0),
-    ),
-    "osum": (
-        ("R", UP1, 0, 1),
+        ("R", 6, 0, 1),
     ),
     ("pr", 0): (
-        ("R", UP0, 0, 1),
+        ("R", 5, 0, 0), ("R", 7, 0, 1), ("R", 1, 0, 1), ("R", 4, 0, 1),
+    ),
+    ("pr", 1): (
+        ("R", 0, 0, 1), ("R", 3, 0, 1),
+    ),
+    ("pr", 2): (
+        ("R", 2, 0, 0), ("R", 5, 1, 0), ("R", 6, 1, 0),
     ),
     ("qs", 0): (
-        ("R", DN1, 0, 0),
-    ),
-    ("pr", 2): (
-        ("R", DN0, 0, 1),
-    ),
-    ("pr", 3): (
-        ("R", UP0, 1, 0),
-    ),
-    ("dwn", 0): (
-        ("R", UP1, 1, 0),
+        ("R", 7, 1, 0), ("R", 3, 1, 0), ("R", 4, 1, 0),
+    ),
+    ("qs", 1): (
+        ("R", 1, 1, 0), ("R", 0, 1, 0),
     ),
     ("dwn", 1): (
-        ("R", KS, 0, 0),
+        ("R", 5, 2, 0),
     ),
     "fin": (
-        ("R", OUT, 0, 0),
+        ("R", 10, 0, 0), ("R", 6, 2, 0), ("R", 9, 0, 0),
     ),
     ("gn1", 0): (
-        ("R", VS, 0, 0),
+        ("R", 8, 0, 0),
     ),
     ("gn1", 1): (
-        ("R", DN1, 1, 0),
+        ("R", 15, 0, 0), ("R", 2, 1, 0),
+    ),
+    "ln1b": (
+        ("R", 3, 2, 0), ("R", 11, 0, 0), ("R", 14, 0, 0),
     ),
     "tail": (
-        ("V", 0), ("R", VS, 0, 1), ("R", KS, 0, 1), ("R", DN1, 2, 0), ("R", QS, 0, 0), ("R", OUT, 1, 0),
-        ("R", DN1, 3, 0), ("R", DN0, 1, 0), ("R", UP0, 2, 0), ("R", QS, 1, 0), ("R", VS, 1, 0), ("R", UP1, 2, 0),
-        ("R", OUT, 2, 0), ("V", 1), ("R", DN0, 2, 0), ("R", UP0, 3, 0), ("R", QS, 2, 0), ("V", 2), ("R", UP1, 3, 0),
-        ("R", KS, 1, 0), ("R", OUT, 3, 0), ("R", VS, 2, 0), ("R", DN0, 3, 0), ("G", 0), ("V", 3), ("R", QS, 3, 0),
-        ("R", KS, 2, 0), ("G", 1), ("R", VS, 3, 0), ("V", 4), ("G", 3), ("R", KS, 3, 0), ("G", 2),
+        ("R", 15, 0, 1), ("R", 7, 2, 0), ("V", 0), ("R", 1, 2, 0), ("R", 14, 0, 1), ("R", 0, 2, 0), ("R", 12, 0, 0),
+        ("R", 2, 2, 0), ("R", 5, 3, 0), ("R", 10, 1, 0), ("R", 7, 3, 0), ("R", 1, 3, 0), ("R", 11, 1, 0),
+        ("R", 14, 1, 0), ("R", 13, 0, 0), ("R", 2, 3, 0), ("R", 4, 2, 0), ("R", 15, 1, 0), ("R", 6, 3, 0),
+        ("R", 11, 2, 0), ("R", 10, 2, 0), ("R", 12, 1, 0), ("R", 9, 1, 0), ("R", 4, 3, 0), ("R", 14, 2, 0),
+        ("R", 10, 3, 0), ("R", 13, 1, 0), ("R", 8, 1, 0), ("R", 11, 3, 0), ("R", 3, 3, 0), ("V", 1), ("R", 0, 3, 0),
+        ("R", 9, 2, 0), ("R", 12, 2, 0), ("R", 15, 2, 0), ("R", 14, 3, 0), ("V", 2), ("G", 2), ("R", 8, 2, 0),
+        ("G", 3), ("R", 13, 2, 0), ("R", 12, 3, 0), ("G", 6), ("R", 9, 3, 0), ("V", 3), ("R", 8, 3, 0),
+        ("R", 15, 3, 0), ("R", 13, 3, 0), ("G", 4), ("G", 1), ("G", 0), ("G", 7), ("V", 4), ("G", 5),
     ),
 }
 
@@ -220,8 +232,9 @@
 
 
 def layer_kernel(
-    tok_h, cot_h, live, wq_h, wo_h, up_h, dn_h, g1, s1, g2, s2,
-    lo_h, gt_h, gq_h, gup_o, gdn_o, gg1_o, gs1_o, gg2_o, gs2_o,
+    tok_h, cot_h, live, wq_h, wo_h, up_h, dn_h, g1_h, s1_h, g2_h, s2_h,
+    lo_h, gt_h, gq_h, gup_h, gdn_h, vec_h,
+    g1, s1, g2, s2, gup_o, gdn_o, vec_o,
     wq, wo, upa, dna, tok, gb, nb, mx, pk, pks, xgb, xn2, xmx, xn1, probs, mask, mid, gm, facc,
     hids, gprs, ga, gas, gw, r0, r1, r2, r3, vsum, vbuf, vrecv, ssem, rsem, lsem,
 ):
@@ -240,9 +253,11 @@
         return pltpu.make_async_copy(src, dst, lsem.at[i])
 
     loads = {
-        0: (tok_h, tok), 1: (cot_h, gb.at[0:ROWS]), 2: (wq_h, wq), 3: (wo_h, wo), 4: (up_h, upa.at[:, 0:SHARD]),
+        0: (tok_h, tok), 1: (cot_h, gb.at[0:ROWS]), 3: (wo_h, wo), 4: (up_h, upa.at[:, 0:SHARD]),
         5: (dn_h, dna.at[0:SHARD]), 6: (cot_h, nb.at[0:ROWS]), 7: (wq_h, wq),
-        8: (nb.at[0:ROWS], lo_h), 9: (tok, gt_h), 10: (xgb.at[0:512], gq_h),
+        8: (nb.at[0:ROWS], lo_h), 9: (tok, gt_h), 10: (gup_o, gup_h), 15: (gdn_o, gdn_h), 16: (vec_o, vec_h),
+        17: (g1_h, g1), 18: (s1_h, s1), 19: (g2_h, g2), 20: (s2_h, s2),
+        **{21 + n: (xgb.at[n * 128:(n + 1) * 128], gq_h.at[n * 128:(n + 1) * 128]) for n in range(4)},
     }
 
     def load(i):
@@ -250,6 +265,10 @@
 
     def loaded(i):
         local(i, *loads[i]).wait()
+
+    def wq_chunk(n):
+        cols = at(n * 768, 768)
+        return local(11 + n, wq_h.at[:, cols], wq.at[:, cols])
 
     def remote(i, to, src, dst):
         return pltpu.make_async_remote_copy(
@@ -281,24 +300,24 @@
         return dna.at[at(2 * SHARD + start, size, 32), :]
 
     def weight(k, way):
-        i = M_W + k * 10 + WAYS.index(way)
-        if way == "X":
-            return remote(i, "x", region(k, "X", None), region(k, "X", 2))
+        i = M_W + k * 10 + WAYS[k].index(way)
+        if way in ("X", "D"):
+            return remote(i, "x", region(k, way, None), region(k, way, 2))
         if way in ("Y", "L"):
             return remote(i, way.lower(), region(k, "X", 2), region(k, "X", 2))
         return remote(i, "l" if way == "P" else "y", onward(k, way), onward(k, way))
 
     def weight_mate(k, way):
-        return remote(M_W + k * 10 + 5 + WAYS.index(way), "c", region(k, way, 2), region(k, way, 3))
+        return remote(M_W + k * 10 + 5 + WAYS[k].index(way), "c", region(k, way, 2), region(k, way, 3))
 
     def relay(way, k):
         weight(k, way).wait()
         if way == "X":
             weight(k, "Y").start()
             weight(k, "L").start()
-        elif way == "Y":
+        elif way == "Y" and k < 2:
             weight(k, "P").start()
-        elif way == "L":
+        elif way == "L" and k < 2:
             weight(k, "Q").start()
         weight_mate(k, way).start()
 
@@ -333,10 +352,11 @@
 
     landing = (r0, r1, r2, r3)
 
+    def lanes_of(p):
+        return slice((p % SUB) * LANES, (p % SUB + 1) * LANES)
+
     def bits_of(p):
-        if p < OUT:
-            return {**bit, "x": 0}
-        return bit
+        return {**bit, "x": 0} if p // SUB < OUT else bit
 
     def chosen(p, k, mine, xb=None):
         own, order, index = bits_of(p), ORDER[p], []
@@ -352,38 +372,48 @@
         return index
 
     def red(p, k, xb=None, part=0):
-        dst = landing[k].at[p] if xb is None else landing[k].at[p, xb]
+        lead = (p // SUB,) if xb is None else (p // SUB, xb)
+        rest = (slice(None), lanes_of(p))
+        free = sum(isinstance(e, slice) for e in chosen(p, k, False, xb))
         return remote(
-            M_RED + p * 5 + (k + 1 if k else part), ORDER[p][k], gw.at[(p, *chosen(p, k, False, xb))], dst
+            M_RED + p * 5 + (k + 1 if k else part), ORDER[p][k],
+            gw.at[(p // SUB, *chosen(p, k, False, xb), *rest)],
+            landing[k].at[(*lead, *[slice(None)] * free, *rest)],
         )
 
     def add(p, k, xb=None):
         index = chosen(p, k, True, xb)
         free = [n for n, e in enumerate(index) if isinstance(e, slice)]
         count = len(free)
+        rest = (slice(None), lanes_of(p))
 
         def body(i, _):
             place = [(i // (1 << (count - 1 - n))) % 2 for n in range(count)]
             full = list(index)
             for n, e in zip(free, place):
                 full[n] = e
-            lead = (p, *place) if xb is None else (p, xb, *place)
-            gw[(p, *full)] = (gw[(p, *full)].astype(F32) + landing[k][lead].astype(F32)).astype(BF)
+            own = (p // SUB, *full, *rest)
+            lead = (p // SUB, *place) if xb is None else (p // SUB, xb, *place)
+            gw[own] = (gw[own].astype(F32) + landing[k][(*lead, *rest)].astype(F32)).astype(BF)
             return 0
 
         lax.fori_loop(0, 1 << count, body, 0)
 
     parts_done = {}
 
-    def first(p, xb, part):
-        if ORDER[p][0] != "x":
-            red(p, 0, xb, part).start()
-        elif (part == 1) == (p < OUT):
-            red(p, 0).start()
+    def first(n, xb, part):
+        for p in range(n * SUB, (n + 1) * SUB):
+            if n == OUT:
+                red(p, 0).start()
+            elif ORDER[p][0] != "x":
+                red(p, 0, xb, part).start()
+            elif (part == 1) == (n < OUT):
+                red(p, 0).start()
 
     def reduced(p, k, part):
-        if k == 0 and ORDER[p][0] != "x" and p != OUT:
-            xb = part if p < OUT else (1 - x if part == 0 else x)
+        n = p // SUB
+        if k == 0 and ORDER[p][0] != "x" and n != OUT:
+            xb = part if n < OUT else (1 - x if part == 0 else x)
             red(p, 0, xb, part).wait()
             add(p, 0, xb)
             parts_done[p] = parts_done.get(p, 0) + 1
@@ -395,21 +425,23 @@
             red(p, k + 1).start()
         else:
             red(p, 3).wait()
-            own = bits_of(p)
-            total = gw[(p, *(own[e] for e in EYES))].astype(F32) + r3[p].astype(F32)
-            if p in (UP0, UP1):
-                half = p - UP0
-                gup_o[:, half * WIDE:(half + 1) * WIDE] = total
-            elif p in (DN0, DN1):
-                half = p - DN0
-                gdn_o[half * WIDE:(half + 1) * WIDE, :] = total.T
+            own, rest = bits_of(p), (slice(None), lanes_of(p))
+            total = gw[(n, *(own[e] for e in EYES), *rest)].astype(F32) + r3[(n, *rest)].astype(F32)
+            if n < OUT:
+                cols = slice((n % 2) * WIDE + (p % SUB) * LANES, (n % 2) * WIDE + (p % SUB + 1) * LANES)
+            if n in (UP0, UP1):
+                gup_o[:, cols] = total
+            elif n in (DN0, DN1):
+                gdn_o[cols, :] = total.T
             else:
-                quarters(p - OUT, own_quarter)[...] = total.astype(BF)
-                gather_c(p - OUT).start()
-                gather_x(p - OUT).start()
+                q = p - OUT * SUB
+                quarters(q, own_quarter)[...] = total.astype(BF)
+                gather_c(q).start()
+                gather_x(q).start()
 
     def quarters(q, n):
-        return xgb.at[q * 128:(q + 1) * 128, at(n * WIDE, WIDE)]
+        row = (q // SUB) * 128
+        return xgb.at[row:row + 128, at(n * WIDE + (q % SUB) * LANES, LANES)]
 
     own_quarter = 2 * c + x
 
@@ -470,21 +502,17 @@
         rstd = lax.rsqrt(jnp.mean(centre * centre, axis=-1, keepdims=True) + 1e-05)
         return centre * rstd, rstd
 
-    def turn(src, dst):
-        def body(j, _):
-            cols = at(j * 128, 128)
-            dst[cols, 0:PAD] = src[:, cols].T
-            return 0
-
-        lax.fori_loop(0, D // 128, body, 0)
-
-    load(0)
-    load(2)
+    def turn(src, dst, j):
+        cols = at(j * 128, 128)
+        dst[cols, 0:PAD] = src[:, cols].T
+
+    for i in (0, 17, 18):
+        load(i)
+    for n in range(4):
+        wq_chunk(n).start()
     barrier = pltpu.get_barrier_semaphore()
     for e in "xylhc":
         pl.semaphore_signal(barrier, inc=1, device_id=mate[e], device_id_type=MESH)
-    for i in (1, 3, 4, 5):
-        load(i)
     qi = lax.broadcasted_iota(jnp.int32, (TILE, TILE), 0)
     ki = lax.broadcasted_iota(jnp.int32, (TILE, TILE), 1)
     mask[...] = jnp.where((ki <= qi) & (ki >= qi - lax.rem(qi, 15)), 0.0, -1e30).astype(F32)
@@ -492,13 +520,16 @@
     pl.semaphore_wait(barrier, 5)
     for k in range(4):
         weight(k, "X").start()
+    for k in (2, 3):
+        weight(k, "D").start()
     weight_c(0).start()
     weight_c(1).start()
     for ref in (gb, mx, ga):
         ref[ROWS:PAD, :] = jnp.zeros((PAD - ROWS, D), BF)
     pk[ROWS:PAD, :] = jnp.zeros((PAD - ROWS, 3 * D), BF)
     vsum[...] = jnp.zeros(vsum.shape, F32)
-    loaded(0)
+    for i in (0, 17, 18):
+        loaded(i)
 
     def norm_one(r, _):
         xhat, _r = centred(tok[block(r), :].astype(F32))
@@ -507,18 +538,20 @@
 
     lax.fori_loop(0, ROWS // STEP, norm_one, 0)
     poll("ln1")
-    loaded(2)
+    for i in (1, 3, 4, 5, 19, 20):
+        load(i)
 
     def qkv(n, _):
-        cols = at(n * 512, 512)
+        wq_chunk(n).wait()
+        cols = at(n * 768, 768)
         pk[0:ROWS, cols] = jnp.dot(nb[0:ROWS, :], wq[:, cols], preferred_element_type=F32).astype(BF)
-        poll_at("qkv", n, 6)
-        return 0
-
-    lax.fori_loop(0, 6, qkv, 0)
-    turn(nb, xn1)
+        for m in range(2):
+            turn(nb, xn1, n * 2 + m)
+        poll_at("qkv", n, 4)
+        return 0
+
+    lax.fori_loop(0, 4, qkv, 0)
     turned(M_N1T, xn1).start()
-    poll("n1t")
     loaded(1)
 
     def mask_cot(r, _):
@@ -526,9 +559,7 @@
         return 0
 
     lax.fori_loop(0, ROWS // STEP, mask_cot, 0)
-    turn(gb, xgb)
-    turned(M_GBT, xgb).start()
-    poll("gbt")
+    poll("msk")
 
     def attend(i, _):
         for h, t in ((i * 2 + n, t) for n in range(2) for t in range(2)):
@@ -543,18 +574,22 @@
         return 0
 
     lax.fori_loop(0, 4, attend, 0)
-    turn(mx, xmx)
-    turned(M_MXT, xmx).start()
-    poll("mxt")
     loaded(3)
 
     def project(n, _):
         cols = at(n * 512, 512)
         facc[:, cols] = jnp.dot(mx[0:ROWS, :], wo[:, cols], preferred_element_type=F32)
+        for m in range(4):
+            turn(gb, xgb, n * 4 + m)
+            turn(mx, xmx, n * 4 + m)
+        poll_at("prj", n, 2)
         return 0
 
     lax.fori_loop(0, 2, project, 0)
-    poll("proj")
+    turned(M_GBT, xgb).start()
+
+    loaded(19)
+    loaded(20)
 
     def norm_two(r, _):
         m = tok[block(r), :].astype(F32) + keep_of(r) * facc[block(r), :]
@@ -565,7 +600,12 @@
 
     lax.fori_loop(0, ROWS // STEP, norm_two, 0)
     poll("ln2")
-    turn(nb, xn2)
+
+    def turn_two(j, _):
+        turn(nb, xn2, j)
+        return 0
+
+    lax.fori_loop(0, D // 128, turn_two, 0)
     turned(M_N2T, xn2).start()
     poll("n2t")
 
@@ -595,7 +635,7 @@
         def _():
             poll("weights")
             for k in range(4):
-                for way in WAYS:
+                for way in WAYS[k]:
                     weight_mate(k, way).wait()
 
         def one(n, _):
@@ -611,19 +651,20 @@
 
         lax.fori_loop(0, 2, one, 0)
 
-        @pl.when(g == 0)
-        def _():
-            turned(M_N2T, xn2).wait()
-            turned(M_GBT, xgb).wait()
-
-        hid_copy(g).wait()
-        gpr_copy(g).wait()
         mine, theirs = at(2 * g * SHARD, SHARD), at(g * SHARD, SHARD)
 
         def sums(i, _):
             n = lax.rem(i, 2)
             rows = at(n * 512, 512)
-            for m, lhs, top, low, p in ((0, xn2, PAD, gprs, UP0), (1, xgb, 0, hids, DN0)):
+            for m, lhs, top, low, p in ((0, xgb, 0, hids, DN0), (1, xn2, PAD, gprs, UP0)):
+                @pl.when(i == 2 * m)
+                def _():
+                    (gpr_copy if m else hid_copy)(g).wait()
+
+                    @pl.when(g == 0)
+                    def _():
+                        turned((M_GBT, M_N2T)[m], lhs).wait()
+
                 @pl.when(i // 2 == m)
                 def _():
                     rhs = jnp.concatenate([wq[top:top + PAD, mine], low[:, theirs]], axis=0)
@@ -644,6 +685,7 @@
         return 0
 
     lax.fori_loop(0, 2, group, 0)
+    turned(M_MXT, xmx).start()
     load(6)
 
     def back_up(n, _):
@@ -683,10 +725,8 @@
         mx[0:ROWS, cols] = dot_nt(ga[0:ROWS, :], wo[cols, :]).astype(BF)
         return 0
 
-    turned(M_MXT, xmx).wait()
     lax.fori_loop(0, 2, back_out, 0)
     poll("bout")
-    ga_copy().wait()
 
     def out_sums(n, _):
         rows = at(n * 512, 512)
@@ -695,11 +735,6 @@
         for half in range(2):
             gw[OUT, half, n] = total[:, half * WIDE:(half + 1) * WIDE].reshape(2, 2, 128, WIDE)
         return 0
-
-    lax.fori_loop(0, 2, out_sums, 0)
-    red(OUT, 0).start()
-    poll("osum")
-    turned(M_N1T, xn1).wait()
 
     def heads_back(h0):
         for h, t in ((h0 + n, t) for n in range(2) for t in range(2)):
@@ -718,20 +753,32 @@
                 pk[rows, col] = g.astype(BF)
 
     def pair(i, _):
-        cb = lax.rem(i + 1 + c, 2)
-        later = i // 2
-        xb = lax.rem(later + 1 + x, 2)
+        later = lax.rem(i, 2)
+        cb = c + (1 - i // 2) * (1 - 2 * c)
+        xb = x + (1 - later) * (1 - 2 * x)
         heads_back(cb * 4 + xb * 2)
         for n in range(2):
-            @pl.when(i == 2 * n)
+            @pl.when(i == n)
             def _():
                 for part in range(3):
                     pk_copy(n, 1 - x if n == 0 else x, part).start()
 
         poll_at("pr", i, 4)
 
-        @pl.when(i % 2 == 1)
+        @pl.when(i == OUT_AT)
         def _():
+            turned(M_MXT, xmx).wait()
+            ga_copy().wait()
+            lax.fori_loop(0, 2, out_sums, 0)
+            first(OUT, None, 0)
+            poll("osum")
+
+        @pl.when(i >= 2)
+        def _():
+            @pl.when(i == 2)
+            def _():
+                turned(M_N1T, xn1).wait()
+
             for n in range(2):
                 @pl.when(later == n)
                 def _():
@@ -803,36 +850,41 @@
     vec(0).start()
     poll("ln1b")
     poll("tail")
-    for n, ref in enumerate((gg1_o, gs1_o, gg2_o, gs2_o)):
-        ref[...] = vbuf[5, n:n + 1, at(s * 128, 128)]
-    for p in (OUT, QS, KS, VS):
-        gather_c(p - OUT).wait()
-        gather_f(p - OUT).wait()
-    load(10)
-    for i in (8, 9, 10):
+    vec_o[...] = vbuf[5, :, at(s * 128, 128)]
+    for i in (10, 15, 16):
+        load(i)
+    for n in range(4):
+        for q in range(n * SUB, (n + 1) * SUB):
+            gather_c(q).wait()
+            gather_f(q).wait()
+        load(21 + n)
+    for i in (8, 9, 10, 15, 16, 21, 22, 23, 24):
         loaded(i)
 
 
-def result_kernel(lo, gt, gq, gup, gdn, gg1, gs1, gg2, gs2, lo_o, gt_o, gqkv_o, gout_o, gup_o, gdn_o, gg1_o, gs1_o, gg2_o, gs2_o, lov, gtv, gqv, gqkv, gout, sem):
-    ins = [pltpu.make_async_copy(a, b, sem.at[n]) for n, (a, b) in enumerate(((lo, lov), (gt, gtv), (gq, gqv)))]
-    for copy in ins:
-        copy.start()
-    gup_o[...] = gup[...]
-    gdn_o[...] = gdn[...]
-    for a, b in ((gg1, gg1_o), (gs1, gs1_o), (gg2, gg2_o), (gs2, gs2_o)):
-        b[...] = a[...].reshape(128)
-    outs = [pltpu.make_async_copy(a, b, sem.at[3 + n]) for n, (a, b) in enumerate(((lov, lo_o), (gtv, gt_o), (gout, gout_o), (gqkv, gqkv_o)))]
-    for n in range(2):
-        ins[n].wait()
-        outs[n].start()
-    ins[2].wait()
-    gout[...] = gqv[0:128, :].astype(F32)
-    outs[2].start()
+def result_kernel(*refs):
+    lo, gt, gq, gup, gdn, vec = refs[:6]
+    lo_o, gt_o, gqkv_o, gout_o, gup_o, gdn_o = refs[6:12]
+    lov, gtv, gqv, gupv, gdnv, vecv, gqkv, gout, sem = refs[16:]
+    pairs = [(gq, gqv), (lo, lov), (gt, gtv), (gup, gupv), (gdn, gdnv), (vec, vecv)]
+    pairs += [(lov, lo_o), (gtv, gt_o), (gupv, gup_o), (gdnv, gdn_o), (gout, gout_o)]
+    pairs += [(vecv.at[n], refs[12 + n]) for n in range(4)]
+    pairs += [(gqkv.at[:, n * D:(n + 1) * D], gqkv_o.at[:, n * D:(n + 1) * D]) for n in range(3)]
+    copies = [pltpu.make_async_copy(a, b, sem.at[n]) for n, (a, b) in enumerate(pairs)]
+    for n in range(6):
+        copies[n].start()
+    copies[0].wait()
     for n in range(3):
         gqkv[:, n * D:(n + 1) * D] = gqv[(n + 1) * 128:(n + 2) * 128, :].astype(F32)
-    outs[3].start()
-    for copy in outs:
-        copy.wait()
+        copies[15 + n].start()
+    gout[...] = gqv[0:128, :].astype(F32)
+    copies[10].start()
+    for n in range(1, 6):
+        copies[n].wait()
+        for m in ((n + 5,) if n < 5 else range(11, 15)):
+            copies[m].start()
+    for n in range(6, 18):
+        copies[n].wait()
 
 
 def fused(
@@ -840,19 +892,20 @@
     gain_one, shift_one, gain_two, shift_two,
 ):
     rows_of = [v.reshape(1, D) for v in (gain_one, shift_one, gain_two, shift_two)]
-    hbm, vmem = pl.BlockSpec(memory_space=pl.ANY), pl.BlockSpec(memory_space=pltpu.VMEM)
+    hbm = pl.BlockSpec(memory_space=pl.ANY)
     shape = jax.ShapeDtypeStruct
     outs = pl.pallas_call(
         layer_kernel,
         name="layer",
         out_shape=(
             shape((ROWS, D), BF), shape((ROWS, D), BF), shape((512, D), BF),
-            shape((128, SHARD), F32), shape((SHARD, 128), F32),
-            shape((1, 128), F32), shape((1, 128), F32), shape((1, 128), F32), shape((1, 128), F32),
+            shape((128, SHARD), F32), shape((SHARD, 128), F32), shape((8, 128), F32),
         ),
-        in_specs=[hbm, hbm, pl.BlockSpec(memory_space=pltpu.SMEM), hbm, hbm, hbm, hbm, vmem, vmem, vmem, vmem],
-        out_specs=[hbm] * 3 + [vmem] * 6,
+        in_specs=[hbm, hbm, pl.BlockSpec(memory_space=pltpu.SMEM)] + [hbm] * 8,
+        out_specs=[hbm] * 6,
         scratch_shapes=[
+            *[pltpu.VMEM((1, D), F32)] * 4,
+            pltpu.VMEM((128, SHARD), F32), pltpu.VMEM((SHARD, 128), F32), pltpu.VMEM((8, 128), F32),
             pltpu.VMEM((D, 3 * D), BF), pltpu.VMEM((D, D), BF), pltpu.VMEM((D, FF), BF), pltpu.VMEM((FF, D), BF),
             pltpu.VMEM((ROWS, D), BF), pltpu.VMEM((PAD, D), BF), pltpu.VMEM((PAD, D), BF), pltpu.VMEM((PAD, D), BF),
             pltpu.VMEM((PAD, 3 * D), BF), pltpu.VMEM((PAD, 3 * 512), BF),
@@ -866,7 +919,7 @@
             pltpu.VMEM((8, 2, 2, 2, 128, WIDE), BF), pltpu.VMEM((8, 2, 2, 128, WIDE), BF),
             pltpu.VMEM((8, 2, 128, WIDE), BF), pltpu.VMEM((8, 128, WIDE), BF),
             pltpu.VMEM((4, 8, D), F32), pltpu.VMEM((6, 8, D), F32), pltpu.VMEM((5, 8, D), F32),
-            pltpu.SemaphoreType.DMA((N_MSG,)), pltpu.SemaphoreType.DMA((N_MSG,)), pltpu.SemaphoreType.DMA((14,)),
+            pltpu.SemaphoreType.DMA((N_MSG,)), pltpu.SemaphoreType.DMA((N_MSG,)), pltpu.SemaphoreType.DMA((25,)),
         ],
         compiler_params=pltpu.CompilerParams(
             collective_id=0, has_side_effects=True, vmem_limit_bytes=67_043_328
@@ -880,11 +933,12 @@
             shape((128, SHARD), F32), shape((SHARD, 128), F32),
             shape((128,), F32), shape((128,), F32), shape((128,), F32), shape((128,), F32),
         ),
-        in_specs=[hbm] * 3 + [vmem] * 6,
-        out_specs=[hbm] * 4 + [vmem] * 6,
+        in_specs=[hbm] * 6,
+        out_specs=[hbm] * 10,
         scratch_shapes=[
             pltpu.VMEM((ROWS, D), BF), pltpu.VMEM((ROWS, D), BF), pltpu.VMEM((512, D), BF),
-            pltpu.VMEM((128, 3 * D), F32), pltpu.VMEM((128, D), F32), pltpu.SemaphoreType.DMA((7,)),
+            pltpu.VMEM((128, SHARD), F32), pltpu.VMEM((SHARD, 128), F32), pltpu.VMEM((8, 128), F32),
+            pltpu.VMEM((128, 3 * D), F32), pltpu.VMEM((128, D), F32), pltpu.SemaphoreType.DMA((18,)),
         ],
     )(*outs)
 

time: 123 us -> 108 us (0.88)
  Pallas kernels: 122 us -> 106 us
    pallas_call x1, Pallas kernels: 117 us -> 103 us  [fused(): pl.pallas_call(layer_kernel, name='layer', out_shape=(shape((ROWS, D), BF...]
    pallas_call x1, Pallas kernels: 5.08 us -> 3.56 us  [fused(): pl.pallas_call(result_kernel, name='results', out_shape=(shape((ROWS, D),...]
where the time goes in v4:
time: 108 us
  Pallas kernels  106 us (98%)
  between operations  1.46 us (1%)
    pallas_call x1, Pallas kernels, fused(): pl.pallas_call(layer_kernel, name='layer', out_shape=(shape((ROWS, D), BF...  103 us
    pallas_call x1, Pallas kernels, fused(): pl.pallas_call(result_kernel, name='results', out_shape=(shape((ROWS, D),...  3.56 us

profile of v4, /device:TPU:0, one launch (start us, length us, event | category | flops | bytes accessed | tf_op | source)
XLA Modules:
  0.0 107.8 jit_solution(2062945115433758869)
XLA Ops:
  1.3 102.8 %layer.1 = (bf16[480,1024]{1,0:T(8,128)(2,1)}, bf16[480,1024]{1,0:T(8,128)(2,1)}, bf16[512,1024]{1,0:T(8,128)(2,1)}, f32[128,512]{1,0:T(8,128)}, f32[512,128]{1,0:T(8,128)}, /*index=5*/f32[8,128]{1,0:T(8,128)}) custom-call(bf16[480,1024]{1,0:T(8,128)(2,1)} %tok_h.1, bf16[480,1024]{1,0:T(8,128)(2,1)} %cot_h.1, s32[1]{0:T(128)S(6)} %copy.21.live, ...), custom_call_target="tpu_custom_call" | custom-call | tf_op jit(solution)/shard_map/layer/pallas_call | solution.py:897
  104.1 3.6 %results.1 = (bf16[480,1024]{1,0:T(8,128)(2,1)}, bf16[480,1024]{1,0:T(8,128)(2,1)}, f32[128,3072]{1,0:T(8,128)}, f32[128,1024]{1,0:T(8,128)}, f32[128,512]{1,0:T...) custom-call(bf16[480,1024]{1,0:T(8,128)(2,1)} %get-tuple-element.16.refs_0_, ...), custom_call_target="tpu_custom_call" | custom-call | tf_op jit(solution)/shard_map/results/pallas_call | solution.py:928

commit v5 on v4

--- a/solution.py
+++ b/solution.py
@@ -122,113 +122,115 @@
 ROWS, PAD, D, FF, SHARD = 480, 512, 1024, 2048, 512
 TILE = 240
 WIDE = 256
-STEP = 96
+STEP = 240
 UP0, UP1, DN0, DN1, OUT, QS, KS, VS = range(8)
 SUB = 2
-OUT_AT = 1
+OUT_AT = 0
 LANES = WIDE // SUB
 ORDER = (
-    "lyhx", "yxlh", "xylh", "ylhx", "hyxl", "xylh", "yhlx", "lxyh",
-    "hxly", "yxlh", "xyhl", "xylh", "xyhl", "xyhl", "ylhx", "lyxh",
+    "xylh", "lyhx", "lxhy", "lxhy", "ylxh", "xlhy", "yxhl", "ylxh",
+    "xlyh", "yxlh", "yxlh", "lyxh", "xlhy", "yxlh", "yxlh", "yxlh",
 )
 EYES = "xhly"
 M_UPC, M_DNC = 0, 1
 M_W = 2
-M_GBT, M_N2T, M_MXT, M_N1T, M_GA = 42, 43, 44, 45, 46
-M_HID, M_GPR = 47, 49
-M_PK = 51
-M_VEC = 57
-M_RED = 62
-M_AGC = M_RED + 40 * SUB
-M_AGX = M_AGC + 4 * SUB
-M_AGF = M_AGX + 4 * SUB
-N_MSG = M_AGF + 4 * SUB
-WAYS = ("XYLPQ", "XYLPQ", "XYLD", "XYLD")
+M_MATE = 22
+M_GBT, M_N2T, M_MXT, M_N1T, M_GA = 24, 25, 26, 27, 28
+M_HID, M_GPR = 29, 31
+M_PK = 33
+M_VEC = 35
+M_RED = 40
+M_AGX = M_RED + 48 * SUB
+M_AG = M_AGX + 4 * SUB
+N_MSG = M_AG + 4
+WAYS = ("XYLPQ", "XYLD", "XYLPQ", "XYLD")
 SCHED = {
-    ("qkv", 3): (
+    ("att", 0): (
         ("X", 0),
     ),
     ("att", 1): (
         ("X", 1),
     ),
-    ("att", 3): (
-        ("Y", 0), ("L", 0), ("X", 2),
-    ),
-    "ln2": (
-        ("Y", 1), ("L", 1), ("X", 3),
+    "n2t": (
+        ("X", 2),
     ),
     ("sh", 0): (
-        ("P", 0), ("Q", 0),
-    ),
-    ("sh", 1): (
-        ("D", 2), ("Y", 2), ("L", 2),
+        ("Y", 0), ("L", 0),
+    ),
+    ("bk", 1): (
+        ("X", 3),
+    ),
+    ("sum", 0): (
+        ("Y", 1), ("L", 1),
     ),
     ("sum", 1): (
-        ("P", 1), ("Q", 1), ("D", 3),
-    ),
-    "weights": (
+        ("Y", 2), ("L", 2),
+    ),
+    "wup": (
+        ("D", 1), ("P", 0), ("Q", 0), ("D", 3),
+    ),
+    ("sh", 3): (
         ("Y", 3), ("L", 3),
     ),
-    ("sh", 2): (
-        ("R", 6, 0, 0),
-    ),
-    ("sum", 5): (
-        ("R", 7, 0, 0), ("R", 1, 0, 0),
-    ),
-    ("sum", 6): (
-        ("R", 4, 0, 0),
-    ),
-    ("bup", 0): (
-        ("R", 0, 0, 0), ("R", 3, 0, 0),
+    "wdn": (
+        ("P", 2), ("Q", 2),
+    ),
+    ("sum", 2): (
+        ("R", 4, 0, 0), ("R", 1, 0, 0),
+    ),
+    "bup": (
+        ("R", 6, 0, 0), ("R", 2, 0, 0),
     ),
     "ln2b": (
-        ("R", 6, 0, 1),
+        ("R", 7, 0, 0), ("R", 3, 0, 0),
     ),
     ("pr", 0): (
-        ("R", 5, 0, 0), ("R", 7, 0, 1), ("R", 1, 0, 1), ("R", 4, 0, 1),
+        ("R", 4, 0, 1), ("R", 1, 0, 1), ("R", 5, 0, 0),
+    ),
+    "osum": (
+        ("R", 6, 0, 1), ("R", 2, 0, 1),
     ),
     ("pr", 1): (
-        ("R", 0, 0, 1), ("R", 3, 0, 1),
-    ),
-    ("pr", 2): (
-        ("R", 2, 0, 0), ("R", 5, 1, 0), ("R", 6, 1, 0),
+        ("R", 7, 0, 1), ("R", 3, 0, 1), ("R", 0, 0, 0),
     ),
     ("qs", 0): (
-        ("R", 7, 1, 0), ("R", 3, 1, 0), ("R", 4, 1, 0),
+        ("R", 4, 1, 0), ("R", 1, 1, 0),
     ),
     ("qs", 1): (
-        ("R", 1, 1, 0), ("R", 0, 1, 0),
-    ),
-    ("dwn", 1): (
-        ("R", 5, 2, 0),
+        ("R", 5, 1, 0),
+    ),
+    "dwn": (
+        ("R", 8, 0, 0),
     ),
     "fin": (
-        ("R", 10, 0, 0), ("R", 6, 2, 0), ("R", 9, 0, 0),
-    ),
-    ("gn1", 0): (
-        ("R", 8, 0, 0),
-    ),
-    ("gn1", 1): (
-        ("R", 15, 0, 0), ("R", 2, 1, 0),
+        ("R", 9, 0, 0), ("R", 7, 1, 0), ("R", 6, 1, 0),
+    ),
+    "gn1": (
+        ("R", 0, 1, 0), ("R", 11, 0, 0), ("R", 2, 1, 0),
     ),
     "ln1b": (
-        ("R", 3, 2, 0), ("R", 11, 0, 0), ("R", 14, 0, 0),
+        ("R", 1, 2, 0), ("R", 10, 0, 0), ("R", 3, 1, 0), ("R", 11, 0, 1),
     ),
     "tail": (
-        ("R", 15, 0, 1), ("R", 7, 2, 0), ("V", 0), ("R", 1, 2, 0), ("R", 14, 0, 1), ("R", 0, 2, 0), ("R", 12, 0, 0),
-        ("R", 2, 2, 0), ("R", 5, 3, 0), ("R", 10, 1, 0), ("R", 7, 3, 0), ("R", 1, 3, 0), ("R", 11, 1, 0),
-        ("R", 14, 1, 0), ("R", 13, 0, 0), ("R", 2, 3, 0), ("R", 4, 2, 0), ("R", 15, 1, 0), ("R", 6, 3, 0),
-        ("R", 11, 2, 0), ("R", 10, 2, 0), ("R", 12, 1, 0), ("R", 9, 1, 0), ("R", 4, 3, 0), ("R", 14, 2, 0),
-        ("R", 10, 3, 0), ("R", 13, 1, 0), ("R", 8, 1, 0), ("R", 11, 3, 0), ("R", 3, 3, 0), ("V", 1), ("R", 0, 3, 0),
-        ("R", 9, 2, 0), ("R", 12, 2, 0), ("R", 15, 2, 0), ("R", 14, 3, 0), ("V", 2), ("G", 2), ("R", 8, 2, 0),
-        ("G", 3), ("R", 13, 2, 0), ("R", 12, 3, 0), ("G", 6), ("R", 9, 3, 0), ("V", 3), ("R", 8, 3, 0),
-        ("R", 15, 3, 0), ("R", 13, 3, 0), ("G", 4), ("G", 1), ("G", 0), ("G", 7), ("V", 4), ("G", 5),
+        ("R", 13, 0, 0), ("V", 0), ("R", 5, 2, 0), ("R", 14, 0, 0), ("R", 8, 1, 0), ("R", 12, 0, 0), ("R", 4, 2, 0),
+        ("R", 6, 2, 0), ("R", 15, 0, 0), ("R", 0, 2, 0), ("R", 9, 1, 0), ("R", 2, 2, 0), ("R", 10, 0, 1),
+        ("R", 7, 2, 0), ("R", 1, 3, 0), ("V", 1), ("R", 3, 2, 0), ("R", 13, 0, 1), ("R", 12, 1, 0), ("R", 6, 3, 0),
+        ("R", 4, 3, 0), ("R", 10, 1, 0), ("R", 14, 0, 1), ("R", 0, 3, 0), ("R", 9, 2, 0), ("R", 7, 3, 0),
+        ("R", 13, 1, 0), ("R", 15, 0, 1), ("R", 10, 2, 0), ("R", 12, 2, 0), ("R", 14, 1, 0), ("R", 11, 1, 0),
+        ("R", 5, 3, 0), ("R", 13, 2, 0), ("R", 9, 3, 0), ("R", 8, 2, 0), ("R", 15, 1, 0), ("R", 2, 3, 0),
+        ("R", 10, 3, 0), ("R", 14, 2, 0), ("V", 2), ("R", 11, 2, 0), ("R", 3, 3, 0), ("G", 1), ("R", 12, 3, 0),
+        ("R", 13, 3, 0), ("G", 2), ("R", 15, 2, 0), ("R", 8, 3, 0), ("G", 4), ("V", 3), ("R", 14, 3, 0), ("G", 5),
+        ("R", 11, 3, 0), ("G", 0), ("R", 15, 3, 0), ("G", 6), ("V", 4), ("G", 3), ("G", 7),
     ),
 }
 
 
 def dot_nt(a, b):
     return lax.dot_general(a, b, (((1,), (1,)), ((), ())), preferred_element_type=F32)
+
+
+def dot_tn(a, b):
+    return lax.dot_general(a, b, (((0,), (0,)), ((), ())), preferred_element_type=F32)
 
 
 def layer_kernel(
@@ -236,18 +238,21 @@
     lo_h, gt_h, gq_h, gup_h, gdn_h, vec_h,
     g1, s1, g2, s2, gup_o, gdn_o, vec_o,
     wq, wo, upa, dna, tok, gb, nb, mx, pk, pks, xgb, xn2, xmx, xn1, probs, mask, mid, gm, facc,
-    hids, gprs, ga, gas, gw, r0, r1, r2, r3, vsum, vbuf, vrecv, ssem, rsem, lsem,
+    hids, gprs, gas, gw, r0, r1, r2, r3, vsum, vbuf, vrecv, ssem, rsem, lsem,
 ):
     s, f = lax.axis_index("seq"), lax.axis_index("ff")
     bit = {"h": s // 4, "l": (s // 2) % 2, "y": s % 2, "x": f // 2, "c": f % 2}
     mate = {
         "h": (s + 4 - 8 * bit["h"], f), "l": (s + 2 - 4 * bit["l"], f), "y": (s + 1 - 2 * bit["y"], f),
         "x": (s, f + 2 - 4 * bit["x"]), "c": (s, f + 1 - 2 * bit["c"]),
+        "lh": (s + 6 - 4 * bit["l"] - 8 * bit["h"], f),
     }
     x, c = bit["x"], bit["c"]
 
     def at(base, size, unit=128):
         return pl.ds(pl.multiple_of(base, unit), size)
+
+    ga = xn2.at[0:PAD]
 
     def local(i, src, dst):
         return pltpu.make_async_copy(src, dst, lsem.at[i])
@@ -300,7 +305,7 @@
         return dna.at[at(2 * SHARD + start, size, 32), :]
 
     def weight(k, way):
-        i = M_W + k * 10 + WAYS[k].index(way)
+        i = M_W + k * 5 + WAYS[k].index(way)
         if way in ("X", "D"):
             return remote(i, "x", region(k, way, None), region(k, way, 2))
         if way in ("Y", "L"):
@@ -308,16 +313,21 @@
         return remote(i, "l" if way == "P" else "y", onward(k, way), onward(k, way))
 
     def weight_mate(k, way):
-        return remote(M_W + k * 10 + 5 + WAYS[k].index(way), "c", region(k, way, 2), region(k, way, 3))
+        return remote(M_MATE + k // 2, "c", region(k, way, 2), region(k, way, 3))
+
+    def weight_mates(m):
+        if m == 0:
+            return remote(M_MATE, "c", upa.at[:, 2 * SHARD:3 * SHARD], upa.at[:, 3 * SHARD:4 * SHARD])
+        return remote(M_MATE + 1, "c", dna.at[2 * SHARD:3 * SHARD], dna.at[3 * SHARD:4 * SHARD])
 
     def relay(way, k):
         weight(k, way).wait()
         if way == "X":
             weight(k, "Y").start()
             weight(k, "L").start()
-        elif way == "Y" and k < 2:
+        elif way == "Y" and k % 2 == 0:
             weight(k, "P").start()
-        elif way == "L" and k < 2:
+        elif way == "L" and k % 2 == 0:
             weight(k, "Q").start()
         weight_mate(k, way).start()
 
@@ -336,19 +346,22 @@
         return wq.at[PAD:2 * PAD, at(slot * SHARD, SHARD)]
 
     def hid_copy(g):
-        return remote(M_HID + g, "c", own_hid(2 * g + 1), hids.at[:, at(g * SHARD, SHARD)])
+        return remote(M_HID + g, "c", own_hid(2 * g + 1), hids)
 
     def gpr_copy(g):
-        return remote(M_GPR + g, "c", own_gpr(2 * g + 1), gprs.at[:, at(g * SHARD, SHARD)])
+        return remote(M_GPR + g, "c", own_gpr(2 * g + 1), gprs)
 
     def ga_copy():
         return remote(M_GA, "c", ga.at[:, at((1 - c) * 512, 512)], gas)
 
     def pk_copy(n, xb, part):
         return remote(
-            M_PK + n * 3 + part, "c", pk.at[:, at(part * D + (1 - c) * 512 + xb * WIDE, WIDE)],
+            M_PK + n, "c", pk.at[:, at(part * D + (1 - c) * 512 + xb * WIDE, WIDE)],
             pks.at[:, at(part * 512 + xb * WIDE, WIDE)],
         )
+
+    def pk_copies(n):
+        return remote(M_PK + n, "c", pks.at[:, 0:3 * WIDE], pks.at[:, 0:3 * WIDE])
 
     landing = (r0, r1, r2, r3)
 
@@ -376,7 +389,7 @@
         rest = (slice(None), lanes_of(p))
         free = sum(isinstance(e, slice) for e in chosen(p, k, False, xb))
         return remote(
-            M_RED + p * 5 + (k + 1 if k else part), ORDER[p][k],
+            M_RED + p * 6 + (k + 1 if k else part), ORDER[p][k],
             gw.at[(p // SUB, *chosen(p, k, False, xb), *rest)],
             landing[k].at[(*lead, *[slice(None)] * free, *rest)],
         )
@@ -399,6 +412,23 @@
 
         lax.fori_loop(0, 1 << count, body, 0)
 
+    def line(p):
+        own, rest, copies = bits_of(p), (slice(None), lanes_of(p)), []
+        for n, to in enumerate(("l", "h", "lh")):
+            block = {e: 1 - own[e] if e in to else own[e] for e in EYES}
+            copies.append(remote(
+                M_RED + p * 6 + 3 + n, to, gw.at[(p // SUB, *(block[e] for e in EYES), *rest)], lands(p)[n].at[rest]
+            ))
+        return copies
+
+    def lands(p):
+        n = p // SUB
+        return (r2.at[n, 0], r2.at[n, 1], r3.at[n])
+
+    def go(p, k):
+        for copy in line(p) if ORDER[p][k] == "z" else (red(p, k),):
+            copy.start()
+
     parts_done = {}
 
     def first(n, xb, part):
@@ -418,15 +448,21 @@
             add(p, 0, xb)
             parts_done[p] = parts_done.get(p, 0) + 1
             if parts_done[p] == 2:
-                red(p, 1).start()
-        elif k < 3:
+                go(p, 1)
+        elif k < len(ORDER[p]) - 1:
             red(p, k).wait()
             add(p, k)
-            red(p, k + 1).start()
+            go(p, k + 1)
         else:
-            red(p, 3).wait()
             own, rest = bits_of(p), (slice(None), lanes_of(p))
-            total = gw[(n, *(own[e] for e in EYES), *rest)].astype(F32) + r3[(n, *rest)].astype(F32)
+            total = gw[(n, *(own[e] for e in EYES), *rest)].astype(F32)
+            if k == 2:
+                for copy, land in zip(line(p), lands(p)):
+                    copy.wait()
+                    total = total + land[rest].astype(F32)
+            else:
+                red(p, 3).wait()
+                total = total + r3[(n, *rest)].astype(F32)
             if n < OUT:
                 cols = slice((n % 2) * WIDE + (p % SUB) * LANES, (n % 2) * WIDE + (p % SUB + 1) * LANES)
             if n in (UP0, UP1):
@@ -446,14 +482,18 @@
     own_quarter = 2 * c + x
 
     def gather_c(q):
-        return remote(M_AGC + q, "c", quarters(q, own_quarter), quarters(q, own_quarter))
+        return remote(M_AG + q // SUB, "c", quarters(q, own_quarter), quarters(q, own_quarter))
 
     def gather_x(q):
         return remote(M_AGX + q, "x", quarters(q, own_quarter), quarters(q, own_quarter))
 
     def gather_f(q):
         other = 2 * c + 1 - x
-        return remote(M_AGF + q, "c", quarters(q, other), quarters(q, other))
+        return remote(M_AG + q // SUB, "c", quarters(q, other), quarters(q, other))
+
+    def gathered(n):
+        half = xgb.at[n * 128:(n + 1) * 128, 0:2 * WIDE]
+        return remote(M_AG + n, "c", half, half)
 
     def vec(n):
         return remote(M_VEC + n, "cxylh"[n], vbuf.at[n], vrecv.at[n])
@@ -480,8 +520,8 @@
         for event in SCHED.get(name, ()):
             handle(event)
 
-    def poll_at(name, i, count):
-        for n in range(count):
+    def poll_at(name, i, places):
+        for n in places:
             if (name, n) in SCHED:
                 @pl.when(i == n)
                 def _():
@@ -513,18 +553,18 @@
     barrier = pltpu.get_barrier_semaphore()
     for e in "xylhc":
         pl.semaphore_signal(barrier, inc=1, device_id=mate[e], device_id_type=MESH)
-    qi = lax.broadcasted_iota(jnp.int32, (TILE, TILE), 0)
-    ki = lax.broadcasted_iota(jnp.int32, (TILE, TILE), 1)
+    ki = lax.broadcasted_iota(jnp.int32, (TILE, TILE), 0)
+    qi = lax.broadcasted_iota(jnp.int32, (TILE, TILE), 1)
     mask[...] = jnp.where((ki <= qi) & (ki >= qi - lax.rem(qi, 15)), 0.0, -1e30).astype(F32)
     nb[ROWS:PAD, :] = jnp.zeros((PAD - ROWS, D), BF)
     pl.semaphore_wait(barrier, 5)
     for k in range(4):
         weight(k, "X").start()
-    for k in (2, 3):
+    for k in (1, 3):
         weight(k, "D").start()
     weight_c(0).start()
     weight_c(1).start()
-    for ref in (gb, mx, ga):
+    for ref in (gb, mx):
         ref[ROWS:PAD, :] = jnp.zeros((PAD - ROWS, D), BF)
     pk[ROWS:PAD, :] = jnp.zeros((PAD - ROWS, 3 * D), BF)
     vsum[...] = jnp.zeros(vsum.shape, F32)
@@ -547,7 +587,7 @@
         pk[0:ROWS, cols] = jnp.dot(nb[0:ROWS, :], wq[:, cols], preferred_element_type=F32).astype(BF)
         for m in range(2):
             turn(nb, xn1, n * 2 + m)
-        poll_at("qkv", n, 4)
+        poll_at("qkv", n, range(4))
         return 0
 
     lax.fori_loop(0, 4, qkv, 0)
@@ -562,30 +602,25 @@
     poll("msk")
 
     def attend(i, _):
-        for h, t in ((i * 2 + n, t) for n in range(2) for t in range(2)):
+        for h, t in ((i * 4 + n, t) for n in range(4) for t in range(2)):
             cols = [at(part * D + h * 128, 128) for part in range(3)]
             rows = slice(t * TILE, (t + 1) * TILE)
-            sc = dot_nt(pk[rows, cols[0]], pk[rows, cols[1]]) * (128 ** -0.5) + mask[...]
-            w = jnp.exp(sc - jnp.max(sc, axis=-1, keepdims=True))
-            p = (w * (1.0 / jnp.sum(w, axis=-1, keepdims=True))).astype(BF)
+            sc = dot_nt(pk[rows, cols[1]], pk[rows, cols[0]]) * (128 ** -0.5) + mask[...]
+            w = jnp.exp(sc - jnp.max(sc, axis=0, keepdims=True))
+            p = (w * (1.0 / jnp.sum(w, axis=0, keepdims=True))).astype(BF)
             probs[h * 2 + t] = p
-            mx[rows, at(h * 128, 128)] = jnp.dot(p, pk[rows, cols[2]], preferred_element_type=F32).astype(BF)
-        poll_at("att", i, 4)
-        return 0
-
-    lax.fori_loop(0, 4, attend, 0)
+            mx[rows, at(h * 128, 128)] = dot_tn(p, pk[rows, cols[2]]).astype(BF)
+        poll_at("att", i, range(2))
+        return 0
+
+    lax.fori_loop(0, 2, attend, 0)
     loaded(3)
 
-    def project(n, _):
-        cols = at(n * 512, 512)
-        facc[:, cols] = jnp.dot(mx[0:ROWS, :], wo[:, cols], preferred_element_type=F32)
-        for m in range(4):
-            turn(gb, xgb, n * 4 + m)
-            turn(mx, xmx, n * 4 + m)
-        poll_at("prj", n, 2)
-        return 0
-
-    lax.fori_loop(0, 2, project, 0)
+    facc[...] = jnp.dot(mx[0:ROWS, :], wo[...], preferred_element_type=F32)
+    for m in range(8):
+        turn(gb, xgb, m)
+        turn(mx, xmx, m)
+    poll("prj")
     turned(M_GBT, xgb).start()
 
     loaded(19)
@@ -606,7 +641,6 @@
         return 0
 
     lax.fori_loop(0, D // 128, turn_two, 0)
-    turned(M_N2T, xn2).start()
     poll("n2t")
 
     loaded(4)
@@ -614,7 +648,7 @@
     wq[ROWS:PAD, 0:FF] = jnp.zeros((PAD - ROWS, FF), BF)
     wq[PAD + ROWS:2 * PAD, 0:FF] = jnp.zeros((PAD - ROWS, FF), BF)
 
-    def shard(j):
+    def widen(j):
         cols = at(j * SHARD, SHARD)
         pre = jnp.dot(nb[0:ROWS, :], upa[:, cols], preferred_element_type=F32)
         sq = pre * pre
@@ -622,79 +656,71 @@
         half = 0.5 * (1.0 + t)
         wq[0:ROWS, cols] = (pre * half).astype(BF)
         slope = half + 0.5 * pre * (1.0 - t * t) * (0.7978845608028654 * (1.0 + 0.134145 * sq))
+        facc[:, at(lax.rem(j, 2) * SHARD, SHARD)] = slope
+
+    def narrow_back(j):
+        cols = at(j * SHARD, SHARD)
         gh = dot_nt(gb[0:ROWS, :], dna[cols, :])
-        wq[PAD:PAD + ROWS, cols] = (gh * slope).astype(BF)
+        wq[PAD:PAD + ROWS, cols] = (gh * facc[:, at(lax.rem(j, 2) * SHARD, SHARD)]).astype(BF)
 
     def group(g, _):
-        @pl.when(g == 0)
-        def _():
-            weight_c(0).wait()
-            weight_c(1).wait()
-
-        @pl.when(g == 1)
-        def _():
-            poll("weights")
-            for k in range(4):
-                for way in WAYS[k]:
-                    weight_mate(k, way).wait()
-
-        def one(n, _):
-            shard(2 * g + 1 - n)
-
-            @pl.when(n == 0)
+        mine = at(2 * g * SHARD, SHARD)
+        for m, work, copy in ((0, widen, hid_copy), (1, narrow_back, gpr_copy)):
+            @pl.when(g == 0)
             def _():
-                hid_copy(g).start()
-                gpr_copy(g).start()
-
-            poll_at("sh", 2 * g + n, 4)
-            return 0
-
-        lax.fori_loop(0, 2, one, 0)
-
-        mine, theirs = at(2 * g * SHARD, SHARD), at(g * SHARD, SHARD)
-
-        def sums(i, _):
-            n = lax.rem(i, 2)
-            rows = at(n * 512, 512)
-            for m, lhs, top, low, p in ((0, xgb, 0, hids, DN0), (1, xn2, PAD, gprs, UP0)):
-                @pl.when(i == 2 * m)
+                weight_c(m).wait()
+
+            @pl.when(g == 1)
+            def _():
+                poll("wdn" if m else "wup")
+                weight_mates(m).wait()
+                if m == 0:
+                    for p in (DN0, DN1, UP0, UP1):
+                        first(p, 0, 0)
+
+            def one(n, _):
+                work(2 * g + 1 - n)
+
+                @pl.when(n == 0)
                 def _():
-                    (gpr_copy if m else hid_copy)(g).wait()
-
-                    @pl.when(g == 0)
-                    def _():
-                        turned((M_GBT, M_N2T)[m], lhs).wait()
-
-                @pl.when(i // 2 == m)
+                    copy(g).start()
+
+                poll_at("bk" if m else "sh", 2 * g + n, range(4))
+                return 0
+
+            lax.fori_loop(0, 2, one, 0)
+            if m == 0:
+                @pl.when(g == 0)
                 def _():
-                    rhs = jnp.concatenate([wq[top:top + PAD, mine], low[:, theirs]], axis=0)
-                    total = jnp.dot(lhs[rows, :], rhs, preferred_element_type=F32).astype(BF)
-                    for half in range(2):
-                        gw[p + half, g, n] = total[:, half * WIDE:(half + 1) * WIDE].reshape(2, 2, 128, WIDE)
-
-                    for part in range(2):
-                        @pl.when((n == 1) & (g == part))
-                        def _():
-                            for half in range(2):
-                                first(p + half, part, part)
-
-            poll_at("sum", 4 * g + i, 8)
-            return 0
-
-        lax.fori_loop(0, 4, sums, 0)
+                    turned(M_N2T, xn2).start()
+
+        for m, copy, lhs, top, low, p in ((0, hid_copy, xgb, 0, hids, DN0), (1, gpr_copy, xn2, PAD, gprs, UP0)):
+            copy(g).wait()
+
+            @pl.when(g == 0)
+            def _():
+                turned((M_GBT, M_N2T)[m], lhs).wait()
+
+            rhs = jnp.concatenate([wq[top:top + PAD, mine], low[...]], axis=0)
+            total = jnp.dot(lhs[...], rhs, preferred_element_type=F32).astype(BF)
+            for half in range(2):
+                gw[p + half, g] = total[:, half * WIDE:(half + 1) * WIDE].reshape(2, 2, 2, 128, WIDE)
+
+            @pl.when(g == 1)
+            def _():
+                for half in range(2):
+                    first(p + half, 1, 1)
+
+            poll_at("sum", 2 * g + m, (m, 2 + m))
+
         return 0
 
     lax.fori_loop(0, 2, group, 0)
     turned(M_MXT, xmx).start()
     load(6)
 
-    def back_up(n, _):
-        cols = at(n * 512, 512)
-        facc[:, cols] = dot_nt(wq[PAD:PAD + ROWS, 0:FF], upa[cols, :])
-        poll_at("bup", n, 2)
-        return 0
-
-    lax.fori_loop(0, 2, back_up, 0)
+    facc[...] = dot_nt(wq[PAD:PAD + ROWS, 0:FF], upa[...])
+    poll("bup")
     loaded(6)
 
     def row_sum(v):
@@ -716,108 +742,89 @@
         ga[block(r), :] = (keep_of(r) * total).astype(BF)
         return 0
 
+    ga[ROWS:PAD, :] = jnp.zeros((PAD - ROWS, D), BF)
     lax.fori_loop(0, ROWS // STEP, norm_two_back, 0)
     ga_copy().start()
     poll("ln2b")
 
-    def back_out(n, _):
-        cols = at(n * 512, 512)
-        mx[0:ROWS, cols] = dot_nt(ga[0:ROWS, :], wo[cols, :]).astype(BF)
-        return 0
-
-    lax.fori_loop(0, 2, back_out, 0)
+    mx[0:ROWS, :] = dot_nt(ga[0:ROWS, :], wo[...]).astype(BF)
     poll("bout")
 
-    def out_sums(n, _):
-        rows = at(n * 512, 512)
+    def out_sums():
         rhs = jnp.concatenate([ga[:, at(c * 512, 512)], gas[...]], axis=0)
-        total = jnp.dot(xmx[rows, :], rhs, preferred_element_type=F32).astype(BF)
+        total = jnp.dot(xmx[...], rhs, preferred_element_type=F32).astype(BF)
         for half in range(2):
-            gw[OUT, half, n] = total[:, half * WIDE:(half + 1) * WIDE].reshape(2, 2, 128, WIDE)
-        return 0
-
-    def heads_back(h0):
-        for h, t in ((h0 + n, t) for n in range(2) for t in range(2)):
+            gw[OUT, half] = total[:, half * WIDE:(half + 1) * WIDE].reshape(2, 2, 2, 128, WIDE)
+
+    def heads_back(i, _):
+        h0 = 4 * (c + (1 - i) * (1 - 2 * c))
+        for h, t in ((h0 + n, t) for n in range(4) for t in range(2)):
             cols = [at(part * D + h * 128, 128) for part in range(3)]
             rows = slice(t * TILE, (t + 1) * TILE)
             q, k, v = (pk[rows, col] for col in cols)
             o = mx[rows, at(h * 128, 128)]
             pb = probs[h * 2 + t]
             p = pb.astype(F32)
-            dp = dot_nt(o, v)
-            gs = (p * (dp - jnp.sum(p * dp, axis=-1, keepdims=True))).astype(BF)
-            gv = lax.dot_general(pb, o, (((0,), (0,)), ((), ())), preferred_element_type=F32)
-            gq = jnp.dot(gs, k, preferred_element_type=F32) * (128 ** -0.5)
-            gk = lax.dot_general(gs, q, (((0,), (0,)), ((), ())), preferred_element_type=F32) * (128 ** -0.5)
+            dp = dot_nt(v, o)
+            gs = (p * (dp - jnp.sum(p * dp, axis=0, keepdims=True))).astype(BF)
+            gv = jnp.dot(pb, o, preferred_element_type=F32)
+            gq = dot_tn(gs, k) * (128 ** -0.5)
+            gk = jnp.dot(gs, q, preferred_element_type=F32) * (128 ** -0.5)
             for col, g in zip(cols, (gq, gk, gv)):
                 pk[rows, col] = g.astype(BF)
 
-    def pair(i, _):
-        later = lax.rem(i, 2)
-        cb = c + (1 - i // 2) * (1 - 2 * c)
-        xb = x + (1 - later) * (1 - 2 * x)
-        heads_back(cb * 4 + xb * 2)
-        for n in range(2):
-            @pl.when(i == n)
-            def _():
+        @pl.when(i == 0)
+        def _():
+            for n in range(2):
                 for part in range(3):
                     pk_copy(n, 1 - x if n == 0 else x, part).start()
 
-        poll_at("pr", i, 4)
+        poll_at("pr", i, range(2))
 
         @pl.when(i == OUT_AT)
         def _():
             turned(M_MXT, xmx).wait()
             ga_copy().wait()
-            lax.fori_loop(0, 2, out_sums, 0)
+            out_sums()
             first(OUT, None, 0)
             poll("osum")
 
-        @pl.when(i >= 2)
-        def _():
-            @pl.when(i == 2)
+        return 0
+
+    lax.fori_loop(0, 2, heads_back, 0)
+    turned(M_N1T, xn1).wait()
+
+    def qkv_sums(later, _):
+        xb = x + (1 - later) * (1 - 2 * x)
+        for n in range(2):
+            @pl.when(later == n)
             def _():
-                turned(M_N1T, xn1).wait()
-
-            for n in range(2):
-                @pl.when(later == n)
-                def _():
-                    for part in range(3):
-                        pk_copy(n, 1 - x if n == 0 else x, part).wait()
-
-            def body(n, _):
-                rows = at(n * 512, 512)
-                rhs = jnp.concatenate(
-                    [
-                        jnp.concatenate([pk[:, at(part * D + c * 512 + xb * WIDE, WIDE)] for part in range(3)], axis=1),
-                        jnp.concatenate([pks[:, at(part * 512 + xb * WIDE, WIDE)] for part in range(3)], axis=1),
-                    ],
-                    axis=0,
-                )
-                total = jnp.dot(xn1[rows, :], rhs, preferred_element_type=F32).astype(BF)
-                for part in range(3):
-                    gw[QS + part, xb, n] = total[:, part * WIDE:(part + 1) * WIDE].reshape(2, 2, 128, WIDE)
-                return 0
-
-            lax.fori_loop(0, 2, body, 0)
-            for n in range(2):
-                @pl.when(later == n)
-                def _():
-                    for p in (QS, KS, VS):
-                        first(p, 1 - x if n == 0 else x, n)
-                    poll(("qs", n))
-
-        return 0
-
-    lax.fori_loop(0, 4, pair, 0)
-
-    def down(n, _):
-        cols = at(n * 512, 512)
-        facc[:, cols] = jnp.dot(wq[0:ROWS, 0:FF], dna[:, cols], preferred_element_type=F32)
-        poll_at("dwn", n, 2)
-        return 0
-
-    lax.fori_loop(0, 2, down, 0)
+                pk_copies(n).wait()
+
+        rhs = jnp.concatenate(
+            [
+                jnp.concatenate([pk[:, at(part * D + c * 512 + xb * WIDE, WIDE)] for part in range(3)], axis=1),
+                jnp.concatenate([pks[:, at(part * 512 + xb * WIDE, WIDE)] for part in range(3)], axis=1),
+            ],
+            axis=0,
+        )
+        for m in range(2):
+            total = jnp.dot(xn1[m * 512:(m + 1) * 512, :], rhs, preferred_element_type=F32).astype(BF)
+            for part in range(3):
+                gw[QS + part, xb, m] = total[:, part * WIDE:(part + 1) * WIDE].reshape(2, 2, 128, WIDE)
+        for n in range(2):
+            @pl.when(later == n)
+            def _():
+                for p in (QS, KS, VS):
+                    first(p, 1 - x if n == 0 else x, n)
+                poll(("qs", n))
+
+        return 0
+
+    lax.fori_loop(0, 2, qkv_sums, 0)
+
+    facc[...] = jnp.dot(wq[0:ROWS, 0:FF], dna[...], preferred_element_type=F32)
+    poll("dwn")
     load(7)
 
     def finish_out(r, _):
@@ -829,13 +836,8 @@
     poll("fin")
     loaded(7)
 
-    def back_qkv(n, _):
-        cols = at(n * 512, 512)
-        facc[:, cols] = dot_nt(pk[0:ROWS, :], wq[cols, :])
-        poll_at("gn1", n, 2)
-        return 0
-
-    lax.fori_loop(0, 2, back_qkv, 0)
+    facc[...] = dot_nt(pk[0:ROWS, :], wq[...])
+    poll("gn1")
 
     def norm_one_back(r, _):
         total = gm[block(r), :] + norm_back(tok[block(r), :].astype(F32), facc[block(r), :], g1[...], 0)
@@ -854,9 +856,7 @@
     for i in (10, 15, 16):
         load(i)
     for n in range(4):
-        for q in range(n * SUB, (n + 1) * SUB):
-            gather_c(q).wait()
-            gather_f(q).wait()
+        gathered(n).wait()
         load(21 + n)
     for i in (8, 9, 10, 15, 16, 21, 22, 23, 24):
         loaded(i)
@@ -913,8 +913,7 @@
             pltpu.VMEM((D, 2 * PAD), BF),
             pltpu.VMEM((16, TILE, TILE), BF), pltpu.VMEM((TILE, TILE), F32),
             pltpu.VMEM((ROWS, D), F32), pltpu.VMEM((ROWS, D), F32), pltpu.VMEM((ROWS, D), F32),
-            pltpu.VMEM((PAD, 2 * SHARD), BF), pltpu.VMEM((PAD, 2 * SHARD), BF),
-            pltpu.VMEM((PAD, D), BF), pltpu.VMEM((PAD, 512), BF),
+            pltpu.VMEM((PAD, SHARD), BF), pltpu.VMEM((PAD, SHARD), BF), pltpu.VMEM((PAD, 512), BF),
             pltpu.VMEM((8, 2, 2, 2, 2, 128, WIDE), BF),
             pltpu.VMEM((8, 2, 2, 2, 128, WIDE), BF), pltpu.VMEM((8, 2, 2, 128, WIDE), BF),
             pltpu.VMEM((8, 2, 128, WIDE), BF), pltpu.VMEM((8, 128, WIDE), BF),

time: 108 us -> 105 us (0.972)
  Pallas kernels: 106 us -> 103 us
    pallas_call x1, Pallas kernels: 103 us -> 99.9 us  [fused(): pl.pallas_call(layer_kernel, name='layer', out_shape=(shape((ROWS, D), BF...]
where the time goes in v5:
time: 105 us
  Pallas kernels  103 us (98%)
  between operations  1.46 us (1%)
    pallas_call x1, Pallas kernels, fused(): pl.pallas_call(layer_kernel, name='layer', out_shape=(shape((ROWS, D), BF...  99.9 us
    pallas_call x1, Pallas kernels, fused(): pl.pallas_call(result_kernel, name='results', out_shape=(shape((ROWS, D),...  3.56 us

profile of v5, /device:TPU:0, one launch (start us, length us, event | category | flops | bytes accessed | tf_op | source)
XLA Modules:
  0.0 104.9 jit_solution(6207502125032689201)
XLA Ops:
  1.3 99.9 %layer.1 = (bf16[480,1024]{1,0:T(8,128)(2,1)}, bf16[480,1024]{1,0:T(8,128)(2,1)}, bf16[512,1024]{1,0:T(8,128)(2,1)}, f32[128,512]{1,0:T(8,128)}, f32[512,128]{1,0:T(8,128)}, /*index=5*/f32[8,128]{1,0:T(8,128)}) custom-call(bf16[480,1024]{1,0:T(8,128)(2,1)} %tok_h.1, bf16[480,1024]{1,0:T(8,128)(2,1)} %cot_h.1, s32[1]{0:T(128)S(6)} %copy.21.live, ...), custom_call_target="tpu_custom_call" | custom-call | tf_op jit(solution)/shard_map/layer/pallas_call | solution.py:897
  101.2 3.6 %results.1 = (bf16[480,1024]{1,0:T(8,128)(2,1)}, bf16[480,1024]{1,0:T(8,128)(2,1)}, f32[128,3072]{1,0:T(8,128)}, f32[128,1024]{1,0:T(8,128)}, f32[128,512]{1,0:T...) custom-call(bf16[480,1024]{1,0:T(8,128)(2,1)} %get-tuple-element.16.refs_0_, ...), custom_call_target="tpu_custom_call" | custom-call | tf_op jit(solution)/shard_map/results/pallas_call | solution.py:927

commit v6 on v5

--- a/solution.py
+++ b/solution.py
@@ -140,9 +140,10 @@
 M_PK = 33
 M_VEC = 35
 M_RED = 40
-M_AGX = M_RED + 48 * SUB
+M_AGX = M_RED + 40 * SUB
 M_AG = M_AGX + 4 * SUB
 N_MSG = M_AG + 4
+N_SENT = M_RED + 16 * SUB
 WAYS = ("XYLPQ", "XYLD", "XYLPQ", "XYLD")
 SCHED = {
     ("att", 0): (
@@ -275,9 +276,10 @@
         cols = at(n * 768, 768)
         return local(11 + n, wq_h.at[:, cols], wq.at[:, cols])
 
-    def remote(i, to, src, dst):
+    def remote(i, to, src, dst, sent=None):
         return pltpu.make_async_remote_copy(
-            src_ref=src, dst_ref=dst, send_sem=ssem.at[i], recv_sem=rsem.at[i], device_id=mate[to], device_id_type=MESH
+            src_ref=src, dst_ref=dst, send_sem=ssem.at[i if sent is None else sent], recv_sem=rsem.at[i],
+            device_id=mate[to], device_id_type=MESH,
         )
 
     def region(k, way, slot):
@@ -389,9 +391,9 @@
         rest = (slice(None), lanes_of(p))
         free = sum(isinstance(e, slice) for e in chosen(p, k, False, xb))
         return remote(
-            M_RED + p * 6 + (k + 1 if k else part), ORDER[p][k],
+            M_RED + p * 5 + (k + 1 if k else part), ORDER[p][k],
             gw.at[(p // SUB, *chosen(p, k, False, xb), *rest)],
-            landing[k].at[(*lead, *[slice(None)] * free, *rest)],
+            landing[k].at[(*lead, *[slice(None)] * free, *rest)], M_RED + p * 2 + part,
         )
 
     def add(p, k, xb=None):
@@ -412,23 +414,6 @@
 
         lax.fori_loop(0, 1 << count, body, 0)
 
-    def line(p):
-        own, rest, copies = bits_of(p), (slice(None), lanes_of(p)), []
-        for n, to in enumerate(("l", "h", "lh")):
-            block = {e: 1 - own[e] if e in to else own[e] for e in EYES}
-            copies.append(remote(
-                M_RED + p * 6 + 3 + n, to, gw.at[(p // SUB, *(block[e] for e in EYES), *rest)], lands(p)[n].at[rest]
-            ))
-        return copies
-
-    def lands(p):
-        n = p // SUB
-        return (r2.at[n, 0], r2.at[n, 1], r3.at[n])
-
-    def go(p, k):
-        for copy in line(p) if ORDER[p][k] == "z" else (red(p, k),):
-            copy.start()
-
     parts_done = {}
 
     def first(n, xb, part):
@@ -448,21 +433,16 @@
             add(p, 0, xb)
             parts_done[p] = parts_done.get(p, 0) + 1
             if parts_done[p] == 2:
-                go(p, 1)
-        elif k < len(ORDER[p]) - 1:
+                red(p, 1).start()
+        elif k < 3:
             red(p, k).wait()
             add(p, k)
-            go(p, k + 1)
+            red(p, k + 1).start()
         else:
             own, rest = bits_of(p), (slice(None), lanes_of(p))
             total = gw[(n, *(own[e] for e in EYES), *rest)].astype(F32)
-            if k == 2:
-                for copy, land in zip(line(p), lands(p)):
-                    copy.wait()
-                    total = total + land[rest].astype(F32)
-            else:
-                red(p, 3).wait()
-                total = total + r3[(n, *rest)].astype(F32)
+            red(p, 3).wait()
+            total = total + r3[(n, *rest)].astype(F32)
             if n < OUT:
                 cols = slice((n % 2) * WIDE + (p % SUB) * LANES, (n % 2) * WIDE + (p % SUB + 1) * LANES)
             if n in (UP0, UP1):
@@ -482,18 +462,21 @@
     own_quarter = 2 * c + x
 
     def gather_c(q):
-        return remote(M_AG + q // SUB, "c", quarters(q, own_quarter), quarters(q, own_quarter))
+        sent = M_W + q // SUB
+        return remote(M_AG + q // SUB, "c", quarters(q, own_quarter), quarters(q, own_quarter), sent)
 
     def gather_x(q):
-        return remote(M_AGX + q, "x", quarters(q, own_quarter), quarters(q, own_quarter))
+        sent = M_RED + (OUT * SUB + q) * 2
+        return remote(M_AGX + q, "x", quarters(q, own_quarter), quarters(q, own_quarter), sent)
 
     def gather_f(q):
         other = 2 * c + 1 - x
-        return remote(M_AG + q // SUB, "c", quarters(q, other), quarters(q, other))
+        sent = M_W + q // SUB
+        return remote(M_AG + q // SUB, "c", quarters(q, other), quarters(q, other), sent)
 
     def gathered(n):
         half = xgb.at[n * 128:(n + 1) * 128, 0:2 * WIDE]
-        return remote(M_AG + n, "c", half, half)
+        return remote(M_AG + n, "c", half, half, M_W + n)
 
     def vec(n):
         return remote(M_VEC + n, "cxylh"[n], vbuf.at[n], vrecv.at[n])
@@ -918,7 +901,7 @@
             pltpu.VMEM((8, 2, 2, 2, 128, WIDE), BF), pltpu.VMEM((8, 2, 2, 128, WIDE), BF),
             pltpu.VMEM((8, 2, 128, WIDE), BF), pltpu.VMEM((8, 128, WIDE), BF),
             pltpu.VMEM((4, 8, D), F32), pltpu.VMEM((6, 8, D), F32), pltpu.VMEM((5, 8, D), F32),
-            pltpu.SemaphoreType.DMA((N_MSG,)), pltpu.SemaphoreType.DMA((N_MSG,)), pltpu.SemaphoreType.DMA((25,)),
+            pltpu.SemaphoreType.DMA((N_SENT,)), pltpu.SemaphoreType.DMA((N_MSG,)), pltpu.SemaphoreType.DMA((25,)),
         ],
         compiler_params=pltpu.CompilerParams(
             collective_id=0, has_side_effects=True, vmem_limit_bytes=67_043_328

time: 105 us -> 104 us (level)
  no operation moved by 1% of the time
where the time goes in v6:
time: 104 us
  Pallas kernels  103 us (99%)
  between operations  1.46 us (1%)
    pallas_call x1, Pallas kernels, fused(): pl.pallas_call(layer_kernel, name='layer', out_shape=(shape((ROWS, D), BF...  99.1 us
    pallas_call x1, Pallas kernels, fused(): pl.pallas_call(result_kernel, name='results', out_shape=(shape((ROWS, D),...  3.56 us

profile of v6, /device:TPU:0, one launch (start us, length us, event | category | flops | bytes accessed | tf_op | source)
XLA Modules:
  0.0 104.1 jit_solution(682202113785459221)
XLA Ops:
  1.3 99.1 %layer.1 = (bf16[480,1024]{1,0:T(8,128)(2,1)}, bf16[480,1024]{1,0:T(8,128)(2,1)}, bf16[512,1024]{1,0:T(8,128)(2,1)}, f32[128,512]{1,0:T(8,128)}, f32[512,128]{1,0:T(8,128)}, /*index=5*/f32[8,128]{1,0:T(8,128)}) custom-call(bf16[480,1024]{1,0:T(8,128)(2,1)} %tok_h.1, bf16[480,1024]{1,0:T(8,128)(2,1)} %cot_h.1, s32[1]{0:T(128)S(6)} %copy.21.live, ...), custom_call_target="tpu_custom_call" | custom-call | tf_op jit(solution)/shard_map/layer/pallas_call | solution.py:880
  100.4 3.6 %results.1 = (bf16[480,1024]{1,0:T(8,128)(2,1)}, bf16[480,1024]{1,0:T(8,128)(2,1)}, f32[128,3072]{1,0:T(8,128)}, f32[128,1024]{1,0:T(8,128)}, f32[128,512]{1,0:T...) custom-call(bf16[480,1024]{1,0:T(8,128)(2,1)} %get-tuple-element.16.refs_0_, ...), custom_call_target="tpu_custom_call" | custom-call | tf_op jit(solution)/shard_map/results/pallas_call | solution.py:910

commit v7 on v6

--- a/solution.py
+++ b/solution.py
@@ -849,24 +849,30 @@
     lo, gt, gq, gup, gdn, vec = refs[:6]
     lo_o, gt_o, gqkv_o, gout_o, gup_o, gdn_o = refs[6:12]
     lov, gtv, gqv, gupv, gdnv, vecv, gqkv, gout, sem = refs[16:]
-    pairs = [(gq, gqv), (lo, lov), (gt, gtv), (gup, gupv), (gdn, gdnv), (vec, vecv)]
-    pairs += [(lov, lo_o), (gtv, gt_o), (gupv, gup_o), (gdnv, gdn_o), (gout, gout_o)]
+    halves = [slice(0, ROWS // 2), slice(ROWS // 2, ROWS)]
+    moved = [(lo, lov, lo_o), (gt, gtv, gt_o)]
+    pairs = [(gq, gqv)]
+    pairs += [(src.at[h], mid.at[h]) for src, mid, _ in moved for h in halves]
+    pairs += [(gup, gupv), (gdn, gdnv), (vec, vecv)]
+    pairs += [(mid.at[h], dst.at[h]) for _, mid, dst in moved for h in halves]
+    pairs += [(gupv, gup_o), (gdnv, gdn_o)]
     pairs += [(vecv.at[n], refs[12 + n]) for n in range(4)]
     pairs += [(gqkv.at[:, n * D:(n + 1) * D], gqkv_o.at[:, n * D:(n + 1) * D]) for n in range(3)]
+    pairs += [(gout, gout_o)]
     copies = [pltpu.make_async_copy(a, b, sem.at[n]) for n, (a, b) in enumerate(pairs)]
-    for n in range(6):
+    for n in range(8):
         copies[n].start()
     copies[0].wait()
     for n in range(3):
         gqkv[:, n * D:(n + 1) * D] = gqv[(n + 1) * 128:(n + 2) * 128, :].astype(F32)
-        copies[15 + n].start()
+        copies[18 + n].start()
     gout[...] = gqv[0:128, :].astype(F32)
-    copies[10].start()
-    for n in range(1, 6):
+    copies[21].start()
+    for n in range(1, 8):
         copies[n].wait()
-        for m in ((n + 5,) if n < 5 else range(11, 15)):
+        for m in ((n + 7,) if n < 7 else range(14, 18)):
             copies[m].start()
-    for n in range(6, 18):
+    for n in range(8, 22):
         copies[n].wait()
 
 
@@ -920,7 +926,7 @@
         scratch_shapes=[
             pltpu.VMEM((ROWS, D), BF), pltpu.VMEM((ROWS, D), BF), pltpu.VMEM((512, D), BF),
             pltpu.VMEM((128, SHARD), F32), pltpu.VMEM((SHARD, 128), F32), pltpu.VMEM((8, 128), F32),
-            pltpu.VMEM((128, 3 * D), F32), pltpu.VMEM((128, D), F32), pltpu.SemaphoreType.DMA((18,)),
+            pltpu.VMEM((128, 3 * D), F32), pltpu.VMEM((128, D), F32), pltpu.SemaphoreType.DMA((22,)),
         ],
     )(*outs)
 

time: 104 us -> 104 us (level)
  no operation moved by 1% of the time
where the time goes in v7:
time: 104 us
  Pallas kernels  103 us (99%)
  between operations  1.46 us (1%)
    pallas_call x1, Pallas kernels, fused(): pl.pallas_call(layer_kernel, name='layer', out_shape=(shape((ROWS, D), BF...  99.1 us
    pallas_call x1, Pallas kernels, fused(): pl.pallas_call(result_kernel, name='results', out_shape=(shape((ROWS, D),...  3.59 us

profile of v7, /device:TPU:0, one launch (start us, length us, event | category | flops | bytes accessed | tf_op | source)
XLA Modules:
  0.0 104.1 jit_solution(1769936125758219538)
XLA Ops:
  1.3 99.1 %layer.1 = (bf16[480,1024]{1,0:T(8,128)(2,1)}, bf16[480,1024]{1,0:T(8,128)(2,1)}, bf16[512,1024]{1,0:T(8,128)(2,1)}, f32[128,512]{1,0:T(8,128)}, f32[512,128]{1,0:T(8,128)}, /*index=5*/f32[8,128]{1,0:T(8,128)}) custom-call(bf16[480,1024]{1,0:T(8,128)(2,1)} %tok_h.1, bf16[480,1024]{1,0:T(8,128)(2,1)} %cot_h.1, s32[1]{0:T(128)S(6)} %copy.21.live, ...), custom_call_target="tpu_custom_call" | custom-call | tf_op jit(solution)/shard_map/layer/pallas_call | solution.py:886
  100.4 3.6 %results.1 = (bf16[480,1024]{1,0:T(8,128)(2,1)}, bf16[480,1024]{1,0:T(8,128)(2,1)}, f32[128,3072]{1,0:T(8,128)}, f32[128,1024]{1,0:T(8,128)}, f32[128,512]{1,0:T...) custom-call(bf16[480,1024]{1,0:T(8,128)(2,1)} %get-tuple-element.16.refs_0_, ...), custom_call_target="tpu_custom_call" | custom-call | tf_op jit(solution)/shard_map/results/pallas_call | solution.py:916
